TPU v7x, 32 devices: a whole 2x2x4 slice. The times are simulated.
32 devices in a mesh: dp: 8 (over z, x), expert: 4 (over y, core).
Axes of the slice: x: 2, y: 2, z: 4, core: 2. Of those that a mesh axis runs over, the one named last changes fastest.
Arguments:
- tokens: bfloat16 [24576, 768], P(('dp', 'expert')), may hold values from -6 to 6
- prev_logits: bfloat16 [24576, 8], P(('dp', 'expert')), may hold values from -3 to 3
- segment_ids: int32 [32, 768], P(('dp', 'expert')), may hold values from 0 to 7, never falling along the last dimension, each value on 1 to 384 neighbouring positions
- pad_mask: int32 [32, 768], P(('dp', 'expert')), may hold values 0 or 1
- routes: int32 [32, 768, 2], P(('dp', 'expert')), may hold values from 0 to 7, all different within a row
- slot_order: int32 [32, 1536], P(('dp', 'expert')), may hold values from 0 to 1535, each once within a row
- cotangent: bfloat16 [24576, 768], P(('dp', 'expert')), may hold values from -6 to 6
- attn_gain: bfloat16 [768], P('dp'), may hold values from 0.5 to 1.5
- qkv_weight: bfloat16 [768, 2304], P('dp'), may hold values from -0.21875 to 0.21875
- out_weight: bfloat16 [768, 768], P('dp'), may hold values from -0.875 to 0.875
- ffn_gain: bfloat16 [768], P('dp'), may hold values from 0.5 to 1.5
- router_weight: bfloat16 [768, 8], P('dp'), may hold values from -0.109375 to 0.109375
- mix_weight: bfloat16 [768, 4], P('dp'), may hold values from -0.21875 to 0.21875
- const_weight: bfloat16 [768, 2], P('dp'), may hold values from -5 to 5
- gate_up_weight: bfloat16 [4, 768, 4096], P('expert', 'dp'), may hold values from -0.21875 to 0.21875
- down_weight: bfloat16 [4, 2048, 768], P('expert', 'dp'), may hold values from -0.25 to 0.25
Outputs:
- layer_out: bfloat16 [24576, 768], P(('dp', 'expert'))
- tokens_grad: float32 [24576, 768], P(('dp', 'expert'))
- prev_grad: float32 [24576, 8], P(('dp', 'expert'))
- attn_gain_grad: float32 [768], P('dp')
- qkv_weight_grad: float32 [768, 2304], P('dp')
- out_weight_grad: float32 [768, 768], P('dp')
- ffn_gain_grad: float32 [768], P('dp')
- router_weight_grad: float32 [768, 8], P('dp')
- mix_weight_grad: float32 [768, 4], P('dp')
- const_weight_grad: float32 [768, 2], P('dp')
- gate_up_grad: float32 [4, 768, 4096], P('expert', 'dp')
- down_grad: float32 [4, 2048, 768], P('expert', 'dp')
Inputs may be any that keep to these rules, and one draw needn't show every extreme that they name: Each token names two different routes; below 4 the SwiGLU experts, 4 the zero expert, 5 the copy expert, 6 and 7 the constant experts. `slot_order`: each row is a permutation; entry 2 t + k ranks route k of token t. `segment_ids`: never falling along a row. `pad_mask`: 1 marks a real token, 0 padding.
All inputs are finite; a program needn't handle non-finite values. No bound on the sum of `pad_mask` on one device may be relied on, other than what follows from the above.
Results may differ from a plain program's by a relative error of at most 0.02.
Values may be sent and summed in bfloat16 or wider, within the bound.
A program may use at most 192 MiB of HBM per device.

v0:
```python
import jax
import jax.numpy as jnp
from jax import lax
from jax.sharding import PartitionSpec as P

HEAD_DIM = 64


epsilon = 1e-06
highest = lax.Precision.HIGHEST


def rope_tables(length, half):
    positions = jnp.arange(length).astype(jnp.float32)[:, None]
    inverse = 10000.0 ** (-(jnp.arange(half).astype(jnp.float32) / half))
    angles = positions * inverse[None, :]
    return (jnp.cos(angles)[:, None, :], jnp.sin(angles)[:, None, :])


def rotate(values, cosine, sine):
    half = values.shape[-1] // 2
    first = values[..., :half]
    second = values[..., half:]
    return jnp.concatenate(
        [first * cosine - second * sine, second * cosine + first * sine], axis=-1
    )


def rotate_back(grads, cosine, sine):
    half = grads.shape[-1] // 2
    first = grads[..., :half]
    second = grads[..., half:]
    return jnp.concatenate(
        [first * cosine + second * sine, second * cosine - first * sine], axis=-1
    )


def masked_scores(query_block, key_rows, block_start, segments, padding):
    block_rows = query_block.shape[0]
    scores = jnp.einsum("qhd,khd->hqk", query_block, key_rows, preferred_element_type=jnp.float32)
    row_index = block_start + jnp.arange(block_rows)
    col_index = jnp.arange(key_rows.shape[0])
    allowed = (
        (col_index[None, :] <= row_index[:, None])
        & (segments[:, None] == segments[None, :])
        & ((padding[None, :] == 1) | (col_index[None, :] == row_index[:, None]))
    )
    return jnp.where(allowed[None], scores, -1e30)


def norm_backward(values, inverse, gain, grad_normed):
    scaled = gain * grad_normed
    correction = jnp.sum(scaled * values, axis=-1, keepdims=True) / values.shape[-1]
    return (
        inverse * scaled - values * inverse * inverse * inverse * correction,
        jnp.sum(grad_normed * values * inverse, axis=0),
    )


def per_device(
    tokens,
    prev_logits,
    segment_ids,
    pad_mask,
    routes,
    slot_order,
    cotangent,
    attn_gain,
    qkv_weight,
    out_weight,
    ffn_gain,
    router_weight,
    mix_weight,
    const_weight,
    gate_up_weight,
    down_weight,
):
    length, width = tokens.shape
    owners = lax.axis_size("expert")
    real_count = owners * gate_up_weight.shape[0]
    capacity = 2 * length // (real_count + 4)
    hidden_units = gate_up_weight.shape[2] // 2
    heads = width // HEAD_DIM
    block_rows = min(length, 768)
    starts = jnp.arange(length // block_rows) * block_rows
    query_scale = HEAD_DIM ** (-0.5)
    dense_parts = (
        attn_gain,
        qkv_weight,
        out_weight,
        ffn_gain,
        router_weight,
        mix_weight,
        const_weight,
    )
    dense_full = (
        lax.all_gather(dense_parts[0], "dp", axis=0, tiled=True),
        lax.all_gather(dense_parts[1], "dp", axis=0, tiled=True),
        lax.all_gather(dense_parts[2], "dp", axis=0, tiled=True),
        lax.all_gather(dense_parts[3], "dp", axis=0, tiled=True),
        lax.all_gather(dense_parts[4], "dp", axis=0, tiled=True),
        lax.all_gather(dense_parts[5], "dp", axis=0, tiled=True),
        lax.all_gather(dense_parts[6], "dp", axis=0, tiled=True),
    )
    expert_full = (
        lax.all_gather(gate_up_weight, "dp", axis=1, tiled=True),
        lax.all_gather(down_weight, "dp", axis=1, tiled=True),
    )
    gain_one, qkv_full, out_full, gain_two, router_full, mix_full, const_full = dense_full
    gate_up_local = expert_full[0][0]
    down_local = expert_full[1][0]
    inputs = tokens.astype(jnp.float32)
    inverse_one = lax.rsqrt(jnp.mean(inputs * inputs, axis=-1, keepdims=True) + epsilon)
    normed = (inputs * inverse_one * gain_one.astype(jnp.float32)).astype(jnp.bfloat16)
    qkv = jnp.dot(normed, qkv_full, preferred_element_type=jnp.float32).reshape(
        length, 3, heads, HEAD_DIM
    )
    cosine, sine = rope_tables(length, HEAD_DIM // 2)
    queries = (rotate(qkv[:, 0], cosine, sine) * query_scale).astype(jnp.bfloat16)
    key_rows = rotate(qkv[:, 1], cosine, sine).astype(jnp.bfloat16)
    value_rows = qkv[:, 2].astype(jnp.bfloat16)
    segments = segment_ids[0]
    padding = pad_mask[0]

    def forward_block(block_start):
        scores = masked_scores(queries, key_rows, block_start, segments, padding)
        highest_score = jnp.max(scores, axis=-1, keepdims=True)
        exponent = jnp.exp(scores - highest_score)
        denominator = jnp.sum(exponent, axis=-1, keepdims=True)
        probabilities = (exponent / denominator).astype(jnp.bfloat16)
        attended_block = jnp.einsum(
            "hqk,khd->qhd", probabilities, value_rows, preferred_element_type=jnp.float32
        )
        return (attended_block.astype(jnp.bfloat16), (highest_score + jnp.log(denominator))[..., 0])

    attended_blocks, log_totals = lax.map(forward_block, starts)
    attended = attended_blocks.reshape(length, width)
    hidden_state = inputs + jnp.dot(attended, out_full, preferred_element_type=jnp.float32)
    inverse_two = lax.rsqrt(jnp.mean(hidden_state * hidden_state, axis=-1, keepdims=True) + epsilon)
    gain_float = gain_two.astype(jnp.float32)
    ffn_normed = (hidden_state * inverse_two * gain_float).astype(jnp.bfloat16)
    ffn_float = ffn_normed.astype(jnp.float32)
    logits = jnp.dot(
        ffn_normed, router_full, preferred_element_type=jnp.float32
    ) + prev_logits.astype(jnp.float32)
    route_rows = routes[0]
    route_ids = jnp.arange(real_count + 4)
    chosen = (route_rows[:, :, None] == route_ids[None, None, :]).astype(jnp.float32)
    picked = jnp.sum(chosen * logits[:, None, :], axis=-1)
    gate_weights = jax.nn.softmax(picked, axis=-1)
    mix = jax.nn.softmax(
        jnp.dot(ffn_normed, mix_full, preferred_element_type=jnp.float32).reshape(length, 2, 2),
        axis=-1,
    )
    is_copy = (route_rows == real_count + 1).astype(jnp.float32)
    const_ids = real_count + 2 + jnp.arange(2)
    is_const = (route_rows[:, :, None] == const_ids[None, None, :]).astype(jnp.float32)
    route_copy = is_copy + jnp.sum(is_const * mix[:, None, :, 0], axis=-1)
    copy_coef = jnp.sum(gate_weights * route_copy, axis=-1)
    const_select = jnp.sum(gate_weights[:, :, None] * is_const, axis=1)
    const_coef = const_select * mix[:, :, 1]
    pair_expert = route_rows.reshape(2 * length)
    order = slot_order[0]
    expert_range = jnp.arange(real_count)
    onehot = (pair_expert[:, None] == expert_range[None, :]).astype(jnp.int32)
    placed = jnp.zeros_like(onehot).at[order].set(onehot)
    before = jnp.cumsum(placed, axis=0) - placed
    slot_rank = jnp.sum(before[order] * onehot, axis=1)
    is_kept = (pair_expert < real_count) & (slot_rank < capacity)
    flat_slot = jnp.where(is_kept, pair_expert * capacity + slot_rank, real_count * capacity)
    pair_token = jnp.arange(2 * length) // 2
    slot_token = jnp.zeros(real_count * capacity + 1, jnp.int32).at[flat_slot].set(pair_token)[:-1]
    slot_valid = jnp.zeros(real_count * capacity + 1, jnp.int32).at[flat_slot].set(1)[:-1]
    send_rows = jnp.where(
        slot_valid[:, None] > 0, ffn_normed[slot_token], jnp.zeros((), jnp.bfloat16)
    ).reshape(real_count, capacity, width)
    received = lax.all_to_all(send_rows, "expert", split_axis=0, concat_axis=0, tiled=True)
    expert_input = received.reshape(-1, width)
    projected = jnp.dot(expert_input, gate_up_local, preferred_element_type=jnp.float32)
    gate_part = projected[:, :hidden_units]
    up_part = projected[:, hidden_units:]
    activated = (jax.nn.silu(gate_part) * up_part).astype(jnp.bfloat16)
    expert_out = (
        jnp.dot(activated, down_local, preferred_element_type=jnp.float32)
        .astype(jnp.bfloat16)
        .reshape(received.shape)
    )
    returned = lax.all_to_all(expert_out, "expert", split_axis=0, concat_axis=0, tiled=True)
    returned_rows = jnp.concatenate(
        [returned.reshape(-1, width), jnp.zeros((1, width), jnp.bfloat16)], axis=0
    )
    pair_rows = returned_rows[flat_slot].astype(jnp.float32).reshape(length, 2, width)
    const_float = const_full.astype(jnp.float32)
    branch_out = (
        jnp.sum(gate_weights[:, :, None] * pair_rows, axis=1)
        + copy_coef[:, None] * ffn_float
        + jnp.dot(const_coef, const_float.T, precision=highest)
    )
    layer_out = (hidden_state + branch_out).astype(jnp.bfloat16)
    dense_back = (
        lax.all_gather(dense_parts[0], "dp", axis=0, tiled=True),
        lax.all_gather(dense_parts[1], "dp", axis=0, tiled=True),
        lax.all_gather(dense_parts[2], "dp", axis=0, tiled=True),
        lax.all_gather(dense_parts[3], "dp", axis=0, tiled=True),
        lax.all_gather(dense_parts[4], "dp", axis=0, tiled=True),
        lax.all_gather(dense_parts[5], "dp", axis=0, tiled=True),
        lax.all_gather(dense_parts[6], "dp", axis=0, tiled=True),
    )
    expert_back = (
        lax.all_gather(gate_up_weight, "dp", axis=1, tiled=True),
        lax.all_gather(down_weight, "dp", axis=1, tiled=True),
    )
    qkv_back = dense_back[1]
    out_back = dense_back[2]
    router_back = dense_back[4]
    mix_back = dense_back[5]
    gate_up_back = expert_back[0][0]
    down_back = expert_back[1][0]
    out_grad = cotangent.astype(jnp.float32)
    pair_grad = (
        (gate_weights[:, :, None] * out_grad[:, None, :])
        .astype(jnp.bfloat16)
        .reshape(2 * length, width)
    )
    slot_grad = (
        jnp.zeros((real_count * capacity + 1, width), jnp.bfloat16)
        .at[flat_slot]
        .set(pair_grad)[:-1]
    )
    slot_grad = slot_grad.reshape(real_count, capacity, width)
    expert_out_grad = lax.all_to_all(
        slot_grad, "expert", split_axis=0, concat_axis=0, tiled=True
    ).reshape(-1, width)
    activated_grad = jnp.einsum(
        "rd,fd->rf", expert_out_grad, down_back, preferred_element_type=jnp.float32
    )
    sigmoid_gate = jax.nn.sigmoid(gate_part)
    gate_grad = activated_grad * up_part * sigmoid_gate * (1.0 + gate_part * (1.0 - sigmoid_gate))
    up_grad = activated_grad * gate_part * sigmoid_gate
    projected_grad = jnp.concatenate([gate_grad, up_grad], axis=1).astype(jnp.bfloat16)
    down_weight_grad = jnp.einsum(
        "rf,rd->fd", activated, expert_out_grad, preferred_element_type=jnp.float32
    )
    gate_up_weight_grad = jnp.einsum(
        "rd,rf->df", expert_input, projected_grad, preferred_element_type=jnp.float32
    )
    input_grad_rows = jnp.einsum(
        "rf,df->rd", projected_grad, gate_up_back, preferred_element_type=jnp.float32
    ).astype(jnp.bfloat16)
    back_rows = lax.all_to_all(
        input_grad_rows.reshape(received.shape), "expert", split_axis=0, concat_axis=0, tiled=True
    )
    back_padded = jnp.concatenate(
        [back_rows.reshape(-1, width), jnp.zeros((1, width), jnp.bfloat16)], axis=0
    )
    routed_grad = jnp.sum(
        back_padded[flat_slot].astype(jnp.float32).reshape(length, 2, width), axis=1
    )
    expert_shards = (
        lax.psum_scatter(
            gate_up_weight_grad[None].astype(jnp.bfloat16), "dp", scatter_dimension=1, tiled=True
        ).astype(jnp.float32),
        lax.psum_scatter(
            down_weight_grad[None].astype(jnp.bfloat16), "dp", scatter_dimension=1, tiled=True
        ).astype(jnp.float32),
    )
    grad_dot_normed = jnp.sum(out_grad * ffn_float, axis=-1)
    grad_dot_const = jnp.dot(out_grad, const_float, precision=highest)
    grad_dot_pairs = jnp.sum(out_grad[:, None, :] * pair_rows, axis=-1)
    gate_grads = (
        grad_dot_pairs
        + route_copy * grad_dot_normed[:, None]
        + jnp.sum(is_const * (mix[:, None, :, 1] * grad_dot_const[:, None, :]), axis=-1)
    )
    picked_grad = gate_weights * (
        gate_grads - jnp.sum(gate_weights * gate_grads, axis=-1, keepdims=True)
    )
    prev_grad = jnp.sum(chosen * picked_grad[:, :, None], axis=1)
    logits_low = prev_grad.astype(jnp.bfloat16)
    router_weight_grad = jnp.einsum(
        "ld,lr->dr", ffn_normed, logits_low, preferred_element_type=jnp.float32
    )
    mix_grad = jnp.stack(
        [const_select * grad_dot_normed[:, None], const_select * grad_dot_const], axis=-1
    )
    mix_logit_grad = (
        (mix * (mix_grad - jnp.sum(mix * mix_grad, axis=-1, keepdims=True)))
        .reshape(length, 4)
        .astype(jnp.bfloat16)
    )
    mix_weight_grad = jnp.einsum(
        "ld,lm->dm", ffn_normed, mix_logit_grad, preferred_element_type=jnp.float32
    )
    const_weight_grad = jnp.einsum("ld,lj->dj", out_grad, const_coef, precision=highest)
    normed_two_grad = routed_grad + copy_coef[:, None] * out_grad
    normed_two_grad = normed_two_grad + jnp.einsum(
        "lr,dr->ld", logits_low, router_back, preferred_element_type=jnp.float32
    )
    normed_two_grad = normed_two_grad + jnp.einsum(
        "lm,dm->ld", mix_logit_grad, mix_back, preferred_element_type=jnp.float32
    )
    hidden_part, gain_two_grad = norm_backward(
        hidden_state, inverse_two, gain_float, normed_two_grad
    )
    hidden_grad = out_grad + hidden_part
    attn_grad = hidden_grad.astype(jnp.bfloat16)
    out_weight_grad = jnp.einsum(
        "ld,le->de", attended, attn_grad, preferred_element_type=jnp.float32
    )
    attended_grad = (
        jnp.einsum("le,de->ld", attn_grad, out_back, preferred_element_type=jnp.float32)
        .astype(jnp.bfloat16)
        .reshape(length, heads, HEAD_DIM)
    )

    def backward_block(carry, block_input):
        key_grad, value_grad = carry
        block_start, log_block = block_input
        scores = masked_scores(queries, key_rows, block_start, segments, padding)
        probs_full = jnp.exp(scores - log_block[..., None])
        probs_low = probs_full.astype(jnp.bfloat16)
        prob_grad = jnp.einsum(
            "qhd,khd->hqk", attended_grad, value_rows, preferred_element_type=jnp.float32
        )
        row_dot = jnp.sum(probs_full * prob_grad, axis=-1, keepdims=True)
        score_grad = (probs_full * (prob_grad - row_dot)).astype(jnp.bfloat16)
        query_grad = jnp.einsum(
            "hqk,khd->qhd", score_grad, key_rows, preferred_element_type=jnp.float32
        )
        key_grad = key_grad + jnp.einsum(
            "hqk,qhd->khd", score_grad, queries, preferred_element_type=jnp.float32
        )
        value_grad = value_grad + jnp.einsum(
            "hqk,qhd->khd", probs_low, attended_grad, preferred_element_type=jnp.float32
        )
        return ((key_grad, value_grad), query_grad)

    zero_heads = jnp.zeros((length, heads, HEAD_DIM), jnp.float32)
    (key_grad, value_grad), query_grads = lax.scan(
        backward_block, (zero_heads, zero_heads), (starts, log_totals)
    )
    query_grad = query_grads.reshape(length, heads, HEAD_DIM)
    qkv_grad = (
        jnp.stack(
            [
                rotate_back(query_grad * query_scale, cosine, sine),
                rotate_back(key_grad, cosine, sine),
                value_grad,
            ],
            axis=1,
        )
        .reshape(length, 3 * width)
        .astype(jnp.bfloat16)
    )
    qkv_weight_grad = jnp.einsum("ld,le->de", normed, qkv_grad, preferred_element_type=jnp.float32)
    normed_one_grad = jnp.einsum(
        "le,de->ld", qkv_grad, qkv_back, preferred_element_type=jnp.float32
    )
    input_part, gain_one_grad = norm_backward(
        inputs, inverse_one, gain_one.astype(jnp.float32), normed_one_grad
    )
    tokens_grad = hidden_grad + input_part
    dense_grads = (
        gain_one_grad,
        qkv_weight_grad,
        out_weight_grad,
        gain_two_grad,
        router_weight_grad,
        mix_weight_grad,
        const_weight_grad,
    )
    dense_grads = (
        lax.psum(dense_grads[0].astype(jnp.bfloat16), "expert").astype(jnp.float32),
        lax.psum(dense_grads[1].astype(jnp.bfloat16), "expert").astype(jnp.float32),
        lax.psum(dense_grads[2].astype(jnp.bfloat16), "expert").astype(jnp.float32),
        lax.psum(dense_grads[3].astype(jnp.bfloat16), "expert").astype(jnp.float32),
        lax.psum(dense_grads[4].astype(jnp.bfloat16), "expert").astype(jnp.float32),
        lax.psum(dense_grads[5].astype(jnp.bfloat16), "expert").astype(jnp.float32),
        lax.psum(dense_grads[6].astype(jnp.bfloat16), "expert").astype(jnp.float32),
    )
    dense_shards = (
        lax.psum_scatter(
            dense_grads[0].astype(jnp.bfloat16), "dp", scatter_dimension=0, tiled=True
        ).astype(jnp.float32),
        lax.psum_scatter(
            dense_grads[1].astype(jnp.bfloat16), "dp", scatter_dimension=0, tiled=True
        ).astype(jnp.float32),
        lax.psum_scatter(
            dense_grads[2].astype(jnp.bfloat16), "dp", scatter_dimension=0, tiled=True
        ).astype(jnp.float32),
        lax.psum_scatter(
            dense_grads[3].astype(jnp.bfloat16), "dp", scatter_dimension=0, tiled=True
        ).astype(jnp.float32),
        lax.psum_scatter(
            dense_grads[4].astype(jnp.bfloat16), "dp", scatter_dimension=0, tiled=True
        ).astype(jnp.float32),
        lax.psum_scatter(
            dense_grads[5].astype(jnp.bfloat16), "dp", scatter_dimension=0, tiled=True
        ).astype(jnp.float32),
        lax.psum_scatter(
            dense_grads[6].astype(jnp.bfloat16), "dp", scatter_dimension=0, tiled=True
        ).astype(jnp.float32),
    )
    return (
        layer_out,
        tokens_grad,
        prev_grad,
        dense_shards[0],
        dense_shards[1],
        dense_shards[2],
        dense_shards[3],
        dense_shards[4],
        dense_shards[5],
        dense_shards[6],
        expert_shards[0],
        expert_shards[1],
    )


def solution(mesh):
    in_specs = (
        P(("dp", "expert"), None),
        P(("dp", "expert"), None),
        P(("dp", "expert"), None),
        P(("dp", "expert"), None),
        P(("dp", "expert"), None, None),
        P(("dp", "expert"), None),
        P(("dp", "expert"), None),
        P("dp"),
        P("dp", None),
        P("dp", None),
        P("dp"),
        P("dp", None),
        P("dp", None),
        P("dp", None),
        P("expert", "dp", None),
        P("expert", "dp", None),
    )
    out_specs = (
        P(("dp", "expert"), None),
        P(("dp", "expert"), None),
        P(("dp", "expert"), None),
        P("dp"),
        P("dp", None),
        P("dp", None),
        P("dp"),
        P("dp", None),
        P("dp", None),
        P("dp", None),
        P("expert", "dp", None),
        P("expert", "dp", None),
    )
    return jax.shard_map(
        per_device, mesh=mesh, in_specs=in_specs, out_specs=out_specs, check_vma=False
    )
```

profile of v0, /device:TPU:0, one launch (start us, length us, event | category | flops | bytes accessed | tf_op | source)
XLA Modules:
  0.0 1046.8 jit_solution(2367103785212867927)
XLA Ops:
  18.9 23.4 %all-reduce.7 = (bf16[768]{0:T(1024)(128)(2,1)S(1)}, bf16[768]{0:T(1024)(128)(2,1)S(1)}) all-reduce(bf16[768]{0:T(1024)(128)(2,1)S(1)} %dynamic-update-slice, bf16[768]{0:T(1024)(128)(2,1)S(1)} %dynamic-update-slice.1), channel_id=1, replica_groups=mesh['dp'=8,'expert'=4] {'dp'}, use_global_device_ids=true, to_apply=%add.2 | all-reduce | flops 1536 | bytes 6144
  42.8 16.6 %all-gather.2 = bf16[8,96,2]{1,2,0:T(2,128)(2,1)S(1)} all-gather(bf16[1,96,2]{1,2,0:T(2,128)(2,1)} %bitcast.165), channel_id=1, replica_groups=mesh['dp'=8,'expert'=4] {'dp'}, dimensions={0}, use_global_device_ids=true | all-gather | bytes 3456 | tf_op jit(solution)/shard_map/all_gather | solution.py:103
  60.8 18.6 %all-gather.1 = bf16[8,96,4]{1,2,0:T(4,128)(2,1)S(1)} all-gather(bf16[1,96,4]{1,2,0:T(4,128)(2,1)} %bitcast.164), channel_id=1, replica_groups=mesh['dp'=8,'expert'=4] {'dp'}, dimensions={0}, use_global_device_ids=true | all-gather | bytes 6912 | tf_op jit(solution)/shard_map/all_gather | solution.py:102
  80.1 26.1 %all-gather = bf16[8,96,8]{1,2,0:T(8,128)(2,1)S(1)} all-gather(bf16[1,96,8]{1,2,0:T(8,128)(2,1)S(1)} %bitcast.163), channel_id=1, replica_groups=mesh['dp'=8,'expert'=4] {'dp'}, dimensions={0}, use_global_device_ids=true | all-gather | bytes 13824 | tf_op jit(solution)/shard_map/all_gather | solution.py:101
  160.7 12.0 %select_reduce_fusion = (f32[12,768]{1,0:T(8,128)S(1)}, f32[12,768,768]{1,2,0:T(8,128)}) fusion(pred[768,768]{0,1:T(8,128)(4,1)S(1)} %fusion.36, bf16[768,12,32]{0,2,1:T(8,128)(2,1)S(1)} %get-tuple-element.157, bf16[768,12,32]{0,2,1:T(8,128)(2,1)S(1)} %get-tuple-element.158, f32[768,12,32]{0,2,1:T(8,128)S(1)} %get-tuple-element.152, ...), kind=kOutput, calls=%fused_computation.14 | convolution fusion | flops 924244992 | bytes 32477184 | tf_op jit(solution)/shard_map/while/body/eval_jaxpr/qhd,khd->hqk/dot_general | solution.py:40
  172.8 12.3 %fusion = f32[12,768]{1,0:T(8,128)S(1)} fusion(f32[12,768,768]{1,2,0:T(8,128)} %get-tuple-element.164, f32[12,768]{1,0:T(8,128)S(1)} %get-tuple-element.163, pred[768,768]{0,1:T(8,128)(4,1)S(1)} %fusion.36), kind=kLoop, calls=%fused_computation.13 | loop fusion | flops 21224448 | bytes 28975104 | tf_op jit(solution)/shard_map/while/body/eval_jaxpr/reduce_sum | solution.py:129
  185.8 14.3 %fusion.47 = bf16[12,64,768]{2,1,0:T(8,128)(2,1)} fusion(f32[12,768,768]{1,2,0:T(8,128)} %get-tuple-element.164, f32[12,768]{1,0:T(8,128)S(1)} %fusion, f32[12,768]{1,0:T(8,128)S(1)} %get-tuple-element.163, pred[768,768]{0,1:T(8,128)(4,1)S(1)} %fusion.36, f32[768,3,12,64]{0,3,2,1:T(8,128)} %bitcast.145), kind=kOutput, calls=%fused_computation.89 | convolution fusion | flops 934871040 | bytes 31334400 | tf_op jit(solution)/shard_map/while/body/eval_jaxpr/hqk,khd->qhd/dot_general | solution.py:131
  208.3 9.0 scatter_custom_fusion.3
  227.4 14.5 %all-to-all-done = bf16[4,192,768]{2,1,0:T(8,128)(2,1)S(1)} async-done(((bf16[4,192,768]{2,1,0:T(8,128)(2,1)}), bf16[4,192,768]{2,1,0:T(8,128)(2,1)S(1)}, u32[]{:S(2)}, u32[]{:S(2)}) %all-to-all-start) | async-done | bytes 1179680 | tf_op jit(solution)/shard_map/all_to_all | solution.py:177
  245.7 10.6 %fusion.8 = f32[768,4096]{1,0:T(8,128)} fusion(bf16[768,768]{1,0:T(8,128)(2,1)S(1)} %bitcast.153, bf16[1,768,4096]{2,1,0:T(8,128)(2,1)} %all-gather.12.cloned.1.call-done), kind=kOutput, calls=%fused_computation.23 | convolution fusion | flops 4831838208 | bytes 20054016 | tf_op jit(solution)/shard_map/dot_general | solution.py:179
  256.3 25.0 %all-gather.14.cloned.1.call-done = bf16[1,2048,768]{2,1,0:T(8,128)(2,1)} async-done(((bf16[1,256,768]{2,1,0:T(8,128)(2,1)}), bf16[1,2048,768]{2,1,0:T(8,128)(2,1)}) %all-gather.14.cloned.1.call-update) | async-done | bytes 3145744 | tf_op jit(solution)/shard_map/all_gather | solution.py:107
  281.3 10.1 multiply_convert_fusion.2
  307.6 9.3 all-to-all-done.3
  322.0 14.2 %all-to-all-done.1 = bf16[4,192,768]{2,1,0:T(8,128)(2,1)S(1)} async-done(((bf16[4,192,768]{2,1,0:T(8,128)(2,1)}), bf16[4,192,768]{2,1,0:T(8,128)(2,1)S(1)}, u32[]{:S(2)}, u32[]{:S(2)}) %all-to-all-start.1) | async-done | bytes 1179680 | tf_op jit(solution)/shard_map/all_to_all | solution.py:188
  353.8 7.9 reduce_sum.225
  370.1 13.9 %multiply_reduce_fusion.1 = (f32[768,2]{1,0:T(8,128)}, f32[768,768]{1,0:T(8,128)}) fusion(f32[768,2,768]{2,1,0:T(2,128)} %reshape.549, f32[768,768]{1,0:T(8,128)S(1)} %copy-done.7, f32[768,2]{1,0:T(8,128)} %copy-done.24), kind=kLoop, calls=%fused_computation.31 | loop fusion | flops 4127232 | bytes 9449472 | tf_op jit(solution)/shard_map/reduce_sum | solution.py:269
  399.8 23.6 %multiply_reduce_fusion = (f32[12,768]{1,0:T(8,128)S(1)}, f32[12,768,768]{1,2,0:T(8,128)}) fusion(f32[12,768,768]{1,2,0:T(8,128)} %get-tuple-element.164, f32[12,768]{1,0:T(8,128)S(1)} %copy-done.33, pred[768,768]{0,1:T(8,128)(4,1)S(1)} %copy-done.9, bf16[768,12,64]{0,2,1:T(8,128)(2,1)S(1)} %bitcast.157, f32[768,3,12,64]{0,3,2,1:T(8,128)} %bitcast.146), kind=kOutput, calls=%fused_computation.9 | convolution fusion | flops 934272000 | bytes 59645952 | tf_op jit(solution)/shard_map/while/body/eval_jaxpr/qhd,khd->hqk/dot_general | solution.py:322
  423.4 23.2 %multiply_convert_fusion = bf16[12,768,768]{1,2,0:T(8,128)(2,1)} fusion(f32[12,768,768]{1,2,0:T(8,128)} %get-tuple-element.171, f32[12,768,768]{1,2,0:T(8,128)} %get-tuple-element.164, f32[12,768]{1,0:T(8,128)S(1)} %get-tuple-element.170, f32[12,768]{1,0:T(8,128)S(1)} %copy-done.33, pred[768,768]{0,1:T(8,128)(4,1)S(1)} %copy-done.9), kind=kLoop, calls=%fused_computation.8 | loop fusion | flops 35389440 | bytes 71442432 | tf_op jit(solution)/shard_map/while/body/eval_jaxpr/convert_element_type | solution.py:326
  446.6 11.7 %convolution_bitcast_fusion = f32[768,12,64]{0,2,1:T(8,128)} fusion(bf16[12,768,768]{1,2,0:T(8,128)(2,1)} %multiply_convert_fusion, f32[768,12,32]{0,2,1:T(8,128)} %copy-done.11, f32[768,12,32]{0,2,1:T(8,128)} %copy-done.10), kind=kOutput, calls=%fused_computation.83 | convolution fusion | flops 907739136 | bytes 18874368 | tf_op jit(solution)/shard_map/while/body/eval_jaxpr/hqk,qhd->khd/dot_general | solution.py:330
  458.3 9.2 multiply_bitcast_fusion
  471.6 13.4 %fusion.48 = bf16[768,1,12,64]{0,3,2,1:T(8,128)(2,1)} fusion(bf16[768,12,64]{0,2,1:T(8,128)(2,1)} %bitcast.158, f32[12,768,768]{1,2,0:T(8,128)} %get-tuple-element.164, f32[12,768]{1,0:T(8,128)S(1)} %copy-done.34, pred[768,768]{0,1:T(8,128)(4,1)S(1)} %copy-done.9), kind=kOutput, calls=%fused_computation.90 | convolution fusion | flops 927793152 | bytes 31297536 | tf_op jit(solution)/shard_map/while/body/eval_jaxpr/hqk,qhd->khd/dot_general | solution.py:333
  510.7 18.7 %reduce-scatter.20.cloned.1.call-done = bf16[96,768]{1,0:T(8,128)(2,1)} async-done(((bf16[768,768]{1,0:T(8,128)(2,1)}), bf16[96,768]{1,0:T(8,128)(2,1)}) %reduce-scatter.20.cloned.1.call-update) | async-done | bytes 147472 | tf_op jit(solution)/shard_map/reduce_scatter | solution.py:388
  529.4 81.6 %reduce-scatter.18.cloned.1.call-done = bf16[96,2304]{1,0:T(8,128)(2,1)} async-done(((bf16[768,2304]{1,0:T(8,128)(2,1)}), bf16[96,2304]{1,0:T(8,128)(2,1)}) %reduce-scatter.18.cloned.1.call-update) | async-done | bytes 442384 | tf_op jit(solution)/shard_map/reduce_scatter | solution.py:385
  611.4 11.0 %fusion.10 = bf16[1,768,4096]{2,1,0:T(8,128)(2,1)} fusion(bf16[768,768]{1,0:T(8,128)(2,1)} %bitcast.154, bf16[768,2048]{1,0:T(8,128)(2,1)} %copy-done.87, bf16[768,2048]{1,0:T(8,128)(2,1)} %copy-done.86), kind=kOutput, calls=%fused_computation.29 | convolution fusion | flops 4847566848 | bytes 13762560 | tf_op jit(solution)/shard_map/rd,rf->df/dot_general | solution.py:244
  623.0 52.5 %reduce-scatter.26.cloned.1.call-done = bf16[96,2]{1,0:T(8,128)(2,1)} async-done(((bf16[768,2]{1,0:T(8,128)(2,1)}), bf16[96,2]{1,0:T(8,128)(2,1)}) %reduce-scatter.26.cloned.1.call-update) | async-done | bytes 400
  676.9 62.6 %reduce-scatter.24.cloned.1.call-done = bf16[96,4]{1,0:T(8,128)(2,1)} async-done(((bf16[768,4]{1,0:T(8,128)(2,1)}), bf16[96,4]{1,0:T(8,128)(2,1)}) %reduce-scatter.24.cloned.1.call-update) | async-done | bytes 784
  750.5 7.6 fusion.31
  758.1 19.5 %all-reduce.6 = (bf16[768]{0:T(1024)(128)(2,1)S(1)}, bf16[768]{0:T(1024)(128)(2,1)S(1)}) all-reduce(bf16[768]{0:T(1024)(128)(2,1)S(1)} %get-tuple-element.121, bf16[768]{0:T(1024)(128)(2,1)S(1)} %copy-done.77), channel_id=2, replica_groups=mesh['dp'=8,'expert'=4] {'dp'}, use_global_device_ids=true, to_apply=%region_32.33.clone | all-reduce | flops 1536 | bytes 6144
  782.9 20.6 %reduce-scatter.22.cloned.1.call-done = bf16[96,8]{1,0:T(8,128)(2,1)} async-done(((bf16[768,8]{1,0:T(8,128)(2,1)}), bf16[96,8]{1,0:T(8,128)(2,1)}) %reduce-scatter.22.cloned.1.call-update) | async-done | bytes 1552
  812.8 67.6 %reduce-scatter.16.cloned.1.call-done = bf16[1,256,768]{2,1,0:T(8,128)(2,1)} async-done(((bf16[1,2048,768]{2,1,0:T(8,128)(2,1)}), bf16[1,256,768]{2,1,0:T(8,128)(2,1)}) %reduce-scatter.16.cloned.1.call-update) | async-done | bytes 393232 | tf_op jit(solution)/shard_map/reduce_scatter | solution.py:263
  882.3 33.3 %all-reduce.12.cloned.1.call-done = (bf16[96,2304]{1,0:T(8,128)(2,1)}, bf16[96,768]{1,0:T(8,128)(2,1)}) async-done(((bf16[96,2304]{1,0:T(8,128)(2,1)}, bf16[96,768]{1,0:T(8,128)(2,1)}), (bf16[96,2304]{1,0:T(8,128)(2,1)}, bf16[96,768]{1,0:T(8,128)(2,1)})) %all-reduce.12.cloned.1.call-update) | async-done | bytes 589840 | tf_op jit(solution)/shard_map/psum | solution.py:374
  919.3 117.8 %reduce-scatter.14.cloned.1.call-done = bf16[1,96,4096]{2,1,0:T(8,128)(2,1)} async-done(((bf16[1,768,4096]{2,1,0:T(8,128)(2,1)}), bf16[1,96,4096]{2,1,0:T(8,128)(2,1)}) %reduce-scatter.14.cloned.1.call-update) | async-done | bytes 786448 | tf_op jit(solution)/shard_map/reduce_scatter | solution.py:260
  (353 shorter events, 217.9 us)
Async XLA Ops:
  7.2 72.9 %copy-start.81 = (bf16[96,8]{0,1:T(8,128)(2,1)S(1)}, bf16[96,8]{0,1:T(8,128)(2,1)}, u32[]{:S(2)}) copy-start(bf16[96,8]{0,1:T(8,128)(2,1)} %param.27) | copy-start | bytes 4612
  7.2 100.3 %copy-start.80 = (s32[1,768]{1,0:T(1,128)S(1)}, s32[1,768]{1,0:T(1,128)}, u32[]{:S(2)}) copy-start(s32[1,768]{1,0:T(1,128)} %param.18) | copy-start | bytes 9220
  7.2 144.0 %all-gather.8.cloned.1.call-start = ((), (), s32[]{:S(2)}) async-start(), calls=%async_computation.11 | async-start | bytes 3981312 | tf_op jit(solution)/shard_map/all_gather | solution.py:98
  7.9 192.1 %all-gather.10.cloned.1.call-start = ((), (), s32[]{:S(2)}) async-start(), calls=%async_computation.12 | async-start | bytes 1327104 | tf_op jit(solution)/shard_map/all_gather | solution.py:99
  8.7 237.0 %all-gather.12.cloned.1.call-start = ((), (), s32[]{:S(2)}) async-start(), calls=%async_computation.13 | async-start | bytes 7077888 | tf_op jit(solution)/shard_map/all_gather | solution.py:106
  9.4 271.8 %all-gather.14.cloned.1.call-start = ((), (), s32[]{:S(2)}) async-start(), calls=%async_computation.14 | async-start | bytes 3538944 | tf_op jit(solution)/shard_map/all_gather | solution.py:107
  42.8 160.3 %copy-start.57 = (f32[768]{0:T(1024)}, f32[768]{0:T(1024)S(1)}, u32[]{:S(2)}) copy-start(f32[768]{0:T(1024)S(1)} %convert_element_type.277) | copy-start | bytes 9220
  106.3 99.3 %copy-start.49 = (bf16[768,8]{0,1:T(8,128)(2,1)}, bf16[768,8]{0,1:T(8,128)(2,1)S(1)}, u32[]{:S(2)}) copy-start(bf16[768,8]{0,1:T(8,128)(2,1)S(1)} %reshape.623) | copy-start | bytes 36868
  118.4 18.5 %copy-start.16 = (bf16[768,768]{1,0:T(8,128)(2,1)S(1)}, bf16[768,768]{1,0:T(8,128)(2,1)}, u32[]{:S(2)}) copy-start(bf16[768,768]{1,0:T(8,128)(2,1)} %param.22) | copy-start | bytes 3538948
  118.9 17.9 %copy-start.68 = (s32[1536]{0:T(1024)}, s32[1536]{0:T(1024)S(1)}, u32[]{:S(2)}) copy-start(s32[1536]{0:T(1024)S(1)} %fusion.77) | copy-start | bytes 18436
  137.5 65.6 %copy-start.4 = (bf16[768,768]{0,1:T(8,128)(2,1)}, bf16[768,768]{0,1:T(8,128)(2,1)S(1)}, u32[]{:S(2)}) copy-start(bf16[768,768]{0,1:T(8,128)(2,1)S(1)} %copy.147) | copy-start | bytes 3538948
  151.2 33.9 %copy-start.8 = (pred[768,768]{0,1:T(8,128)(4,1)}, pred[768,768]{0,1:T(8,128)(4,1)S(1)}, u32[]{:S(2)}) copy-start(pred[768,768]{0,1:T(8,128)(4,1)S(1)} %fusion.36) | copy-start | bytes 1769476
  205.5 20.6 %copy-start.35 = (f32[768,2,2]{0,2,1:T(2,128)}, f32[768,2,2]{0,2,1:T(2,128)S(1)}, u32[]{:S(2)}) copy-start(f32[768,2,2]{0,2,1:T(2,128)S(1)} %reshape.543) | copy-start | bytes 36868
  205.5 20.6 %copy-start.47 = (f32[768,2]{0,1:T(2,128)}, f32[768,2]{0,1:T(2,128)S(1)}, u32[]{:S(2)}) copy-start(f32[768,2]{0,1:T(2,128)S(1)} %reduce_max.30) | copy-start | bytes 18436
  222.4 19.5 %all-to-all-start = ((bf16[4,192,768]{2,1,0:T(8,128)(2,1)}), bf16[4,192,768]{2,1,0:T(8,128)(2,1)S(1)}, u32[]{:S(2)}, u32[]{:S(2)}) async-start(bf16[4,192,768]{2,1,0:T(8,128)(2,1)} %broadcast_select_fusion), calls=%async_computation | async-start | bytes 2359296 | tf_op jit(solution)/shard_map/all_to_all | solution.py:177
  226.2 30.1 %copy-start.50 = (f32[768,2,2]{0,1,2:T(2,128)}, f32[768,2,2]{0,1,2:T(2,128)S(1)}, u32[]{:S(2)}) copy-start(f32[768,2,2]{0,1,2:T(2,128)S(1)} %broadcast_divide_fusion) | copy-start | bytes 36868
  227.4 73.6 %copy-start.44 = (f32[768,2]{0,1:T(2,128)}, f32[768,2]{0,1:T(2,128)S(1)}, u32[]{:S(2)}) copy-start(f32[768,2]{0,1:T(2,128)S(1)} %get-tuple-element.124) | copy-start | bytes 18436
  241.9 39.4 %all-to-all-start.2 = ((bf16[4,192,768]{2,1,0:T(8,128)(2,1)}), bf16[4,192,768]{2,1,0:T(8,128)(2,1)S(1)}, u32[]{:S(2)}, u32[]{:S(2)}) async-start(bf16[4,192,768]{2,1,0:T(8,128)(2,1)} %bitcast.24), calls=%async_computation.2 | async-start | bytes 2359296 | tf_op jit(solution)/shard_map/all_to_all | solution.py:231
  297.5 19.4 %all-to-all-start.3 = ((bf16[4,192,768]{2,1,0:T(8,128)(2,1)}), bf16[4,192,768]{2,1,0:T(8,128)(2,1)S(1)}, u32[]{:S(2)}, u32[]{:S(2)}) async-start(bf16[4,192,768]{2,1,0:T(8,128)(2,1)} %bitcast.26), calls=%async_computation.3 | async-start | bytes 2359296 | tf_op jit(solution)/shard_map/all_to_all | solution.py:250
  316.9 19.4 %all-to-all-start.1 = ((bf16[4,192,768]{2,1,0:T(8,128)(2,1)}), bf16[4,192,768]{2,1,0:T(8,128)(2,1)S(1)}, u32[]{:S(2)}, u32[]{:S(2)}) async-start(bf16[4,192,768]{2,1,0:T(8,128)(2,1)} %bitcast.18), calls=%async_computation.1 | async-start | bytes 2359296 | tf_op jit(solution)/shard_map/all_to_all | solution.py:188
  320.4 209.0 %reduce-scatter.20.cloned.1.call-start = ((), (), s32[]{:S(2)}) async-start(), calls=%async_computation.18 | async-start | bytes 1327104 | tf_op jit(solution)/shard_map/reduce_scatter | solution.py:388
  370.1 18.6 %copy-start.5 = (bf16[768,768]{0,1:T(8,128)(2,1)S(1)}, bf16[768,768]{0,1:T(8,128)(2,1)}, u32[]{:S(2)}) copy-start(bf16[768,768]{0,1:T(8,128)(2,1)} %copy-done.4) | copy-start | bytes 3538948
  399.7 23.6 %copy-start.28 = (bf16[768,768]{0,1:T(8,128)(2,1)}, bf16[768,768]{0,1:T(8,128)(2,1)S(1)}, u32[]{:S(2)}) copy-start(bf16[768,768]{0,1:T(8,128)(2,1)S(1)} %convolution_convert_fusion.3) | copy-start | bytes 3538948
  467.5 143.6 %reduce-scatter.18.cloned.1.call-start = ((), (), s32[]{:S(2)}) async-start(), calls=%async_computation.17 | async-start | bytes 3981312 | tf_op jit(solution)/shard_map/reduce_scatter | solution.py:385
  493.2 182.3 %reduce-scatter.26.cloned.1.call-start = ((), (), s32[]{:S(2)}) async-start(), calls=%async_computation.21 | async-start | bytes 221184
  497.9 241.6 %reduce-scatter.24.cloned.1.call-start = ((), (), s32[]{:S(2)}) async-start(), calls=%async_computation.20 | async-start | bytes 221184
  500.6 302.9 %reduce-scatter.22.cloned.1.call-start = ((), (), s32[]{:S(2)}) async-start(), calls=%async_computation.19 | async-start | bytes 221184
  504.0 376.4 %reduce-scatter.16.cloned.1.call-start = ((), (), s32[]{:S(2)}) async-start(), calls=%async_computation.16 | async-start | bytes 3538944 | tf_op jit(solution)/shard_map/reduce_scatter | solution.py:263
  510.6 405.0 %all-reduce.12.cloned.1.call-start = ((), (), s32[]{:S(2)}) async-start(), calls=%async_computation.22 | async-start | bytes 1179648 | tf_op jit(solution)/shard_map/psum | solution.py:374
  611.1 426.1 %reduce-scatter.14.cloned.1.call-start = ((), (), s32[]{:S(2)}) async-start(), calls=%async_computation.15 | async-start | bytes 7077888 | tf_op jit(solution)/shard_map/reduce_scatter | solution.py:260
  780.9 23.4 %copy-start.79 = (bf16[96,4]{0,1:T(4,128)(2,1)S(1)}, bf16[96,4]{0,1:T(4,128)(2,1)}, u32[]{:S(2)}) copy-start(bf16[96,4]{0,1:T(4,128)(2,1)} %copy.177) | copy-start | bytes 2308
  780.9 23.4 %copy-start.82 = (bf16[96,2]{0,1:T(2,128)(2,1)S(1)}, bf16[96,2]{0,1:T(2,128)(2,1)}, u32[]{:S(2)}) copy-start(bf16[96,2]{0,1:T(2,128)(2,1)} %copy.179) | copy-start | bytes 1156
  (72 other events, 414.9 us)
Sparse Core Ops, SparseCore 0:
  10.2 68.4 all-gather.7
  80.9 39.5 all-gather.9
  122.6 97.8 all-gather.11
  222.5 58.6 all-gather.13
  467.6 61.8 reduce-scatter.19
  532.9 78.0 reduce-scatter.17
  614.9 60.6 reduce-scatter.25
  679.4 60.0 reduce-scatter.23
  743.3 60.1 reduce-scatter.21
  806.9 73.4 reduce-scatter.15
  882.9 32.7 all-reduce.11
  919.1 117.9 reduce-scatter.13
where the time goes:
time: 1050 us
  waiting for transfers between devices  521 us (50%)
  matrix products  177 us (17%)
  other arithmetic  111 us (11%)
  blocking collectives  110 us (10%)
  local copies, waits for them, and re-layouts  96.5 us (9%)
  between operations  17.2 us (2%)
  starting transfers between devices  15.4 us (1%)
    unnamed x15, waiting for transfers between devices  138 us
    reduce_scatter x1, waiting for transfers between devices, per_device(): lax.psum_scatter(gate_up_weight_grad[None].astype(jnp.bfloat16), 'dp', sc...  118 us
    reduce_scatter x1, waiting for transfers between devices, per_device(): lax.psum_scatter(dense_grads[1].astype(jnp.bfloat16), 'dp', scatter_dimen...  81.6 us
    reduce_scatter x1, waiting for transfers between devices, per_device(): lax.psum_scatter(down_weight_grad[None].astype(jnp.bfloat16), 'dp', scatt...  67.6 us
    unnamed x2, blocking collectives  42.9 us
    psum x1, waiting for transfers between devices, per_device(): lax.psum(dense_grads[1].astype(jnp.bfloat16), 'expert').astype(jnp.float32)  33.3 us
    unnamed x197, local copies, waits for them, and re-layouts  31.9 us
    all_gather x1, blocking collectives, per_device(): lax.all_gather(dense_parts[4], 'dp', axis=0, tiled=True)  26.1 us
  transfers between devices with their start and end apart: 16, of which 12 were waited for; matrix products, arithmetic and copies ran while one was open for 21% of the time, Pallas kernels for 0%

commit v1 on v0

--- a/solution.py
+++ b/solution.py
@@ -1,9 +1,488 @@
+import functools
 import jax
 import jax.numpy as jnp
 from jax import lax
+from jax.experimental import pallas as pl
+from jax.experimental.pallas import tpu as pltpu
 from jax.sharding import PartitionSpec as P
 
 HEAD_DIM = 64
+
+MESH = pl.DeviceIdType.MESH
+
+
+class Spot:
+    def __init__(self, sizes):
+        self.nz, self.nx, self.ny, self.nc = sizes
+        self.dp, self.ex = lax.axis_index("dp"), lax.axis_index("expert")
+        self.z, self.x = lax.div(self.dp, self.nx), lax.rem(self.dp, self.nx)
+        self.y, self.core = lax.div(self.ex, self.nc), lax.rem(self.ex, self.nc)
+
+    def device(self, z=None, x=None, y=None, core=None):
+        z, x = self.z if z is None else z, self.x if x is None else x
+        y, core = self.y if y is None else y, self.core if core is None else core
+        return {"dp": z * self.nx + x, "expert": y * self.nc + core}
+
+
+def between(value, size):
+    return jnp.logical_and(value >= 0, value < size)
+
+
+class Flood:
+    def __init__(self, spot, number, own, view, sends, recvs, z_first, mate=None):
+        self.s, self.n, self.own, self.view = spot, number, own, view
+        self.sends, self.recvs, self.z_first, self.mate = sends, recvs, z_first, mate
+        if z_first:
+            self.na, self.nb, self.a, self.b = spot.nz, spot.nx, spot.z, spot.x
+        else:
+            self.na, self.nb, self.a, self.b = spot.nx, spot.nz, spot.x, spot.z
+        self.drains = []
+
+    def origin(self, a, b):
+        return a * self.s.nx + b if self.z_first else b * self.s.nx + a
+
+    def along(self, which, value):
+        zed = (which == 0) == self.z_first
+        return self.s.device(z=value) if zed else self.s.device(x=value)
+
+    def push(self, cond, src, o, way, device, recvs=None):
+        copy = pltpu.make_async_remote_copy(
+            src_ref=src, dst_ref=self.view(o),
+            send_sem=self.sends.at[way, self.n, o],
+            recv_sem=(self.recvs if recvs is None else recvs).at[self.n, o],
+            device_id=device, device_id_type=MESH)
+        if cond is None:
+            copy.start()
+            self.drains.append(copy.wait_send)
+        else:
+            pl.when(cond)(lambda: copy.start())
+            self.drains.append(lambda: pl.when(cond)(lambda: copy.wait_send()))
+
+    def share(self, cond, src, o):
+        if self.mate is not None:
+            self.push(cond, src, o, 4, self.s.device(core=1 - self.s.core), self.mate)
+
+    def mates(self, view):
+        def one(o, carry):
+            pltpu.make_async_remote_copy(
+                src_ref=view(o), dst_ref=view(o), send_sem=self.sends.at[0, self.n, o], recv_sem=self.mate.at[self.n, o],
+                device_id=self.s.device(), device_id_type=MESH).wait_recv()
+            return carry
+        lax.fori_loop(0, self.s.nz * self.s.nx, one, 0)
+
+    def arrive(self, o):
+        pltpu.make_async_remote_copy(
+            src_ref=self.view(o), dst_ref=self.view(o),
+            send_sem=self.sends.at[0, self.n, o], recv_sem=self.recvs.at[self.n, o],
+            device_id=self.s.device(), device_id_type=MESH).wait_recv()
+
+    def second(self, cond, src, o):
+        for j, sign in enumerate((1, -1)):
+            to = self.b + sign
+            if self.nb > 1:
+                ok = between(to, self.nb)
+                self.push(ok if cond is None else jnp.logical_and(cond, ok), src, o, 2 + j, self.along(1, to))
+
+    def levels(self):
+        out = [[] for _ in range(self.na + self.nb - 1)]
+
+        def begin():
+            o = self.origin(self.a, self.b)
+            for j, sign in enumerate((1, -1)):
+                if self.na > 1:
+                    self.push(between(self.a + sign, self.na), self.own, o, j, self.along(0, self.a + sign))
+            self.second(None, self.own, o)
+            self.share(None, self.own, o)
+
+        out[0].append(begin)
+        for k in range(1, self.na):
+            for j, sign in enumerate((1, -1)):
+                def step(k=k, j=j, sign=sign):
+                    a = self.a - sign * k
+                    here = between(a, self.na)
+                    o = self.origin(a, self.b)
+                    pl.when(here)(lambda: self.arrive(o))
+                    on = jnp.logical_and(here, between(self.a + sign, self.na))
+                    if self.na > 2 or k == 0:
+                        self.push(on, self.view(o), o, j, self.along(0, self.a + sign))
+                    self.second(here, self.view(o), o)
+                    self.share(here, self.view(o), o)
+                out[k].append(step)
+        for d in range(1, self.nb):
+            for da in range(-(self.na - 1), self.na):
+                for j, sign in enumerate((1, -1)):
+                    def step(d=d, da=da, j=j, sign=sign):
+                        a, b = self.a + da, self.b - sign * d
+                        here = jnp.logical_and(between(a, self.na), between(b, self.nb))
+                        o = self.origin(a, b)
+                        pl.when(here)(lambda: self.arrive(o))
+                        if self.nb > 2:
+                            on = jnp.logical_and(here, between(self.b + sign, self.nb))
+                            self.push(on, self.view(o), o, 2 + j, self.along(1, self.b + sign))
+                        self.share(here, self.view(o), o)
+                    out[abs(da) + d].append(step)
+        return out
+
+
+def enter(spot, devices):
+    barrier = pltpu.get_barrier_semaphore()
+    count = jnp.int32(0)
+    for cond, device in devices:
+        def hail(device=device):
+            pl.semaphore_signal(barrier, inc=1, device_id=device, device_id_type=MESH)
+        if cond is None:
+            hail()
+            count = count + 1
+        else:
+            pl.when(cond)(hail)
+            count = count + cond.astype(jnp.int32)
+    pl.semaphore_wait(barrier, count)
+
+
+def line_neighbours(spot):
+    out = []
+    for sign in (1, -1):
+        out.append((between(spot.z + sign, spot.nz), spot.device(z=spot.z + sign)))
+        out.append((between(spot.x + sign, spot.nx), spot.device(x=spot.x + sign)))
+    return out
+
+
+def gather_kernel(sizes, chunks, qkv_ref, rest_ref, gu_ref, dn_ref, qkv_out, rest_out, gu_out, dn_out,
+                  sends, recvs, mates, local):
+    spot = Spot(sizes)
+    enter(spot, line_neighbours(spot) + [(None, spot.device(core=1 - spot.core))])
+    rows = qkv_ref.shape[0]
+    rows_d, width = dn_ref.shape
+    first, later = [], []
+    for src, out in ((qkv_ref, qkv_out), (rest_ref, rest_out)):
+        part = src.shape[1] // 2
+        def half(o, core, out=out, part=part):
+            return out.at[pl.ds(pl.multiple_of(o * rows, 8), rows), pl.ds(pl.multiple_of(core * part, 128), part)]
+        first.append((src.at[:, pl.ds(pl.multiple_of(spot.core * part, 128), part)],
+                      lambda o, half=half: half(o, spot.core), True, lambda o, half=half: half(o, 1 - spot.core)))
+    part = rows_d // 2
+    for p, zf in ((0, True), (1, False)):
+        later.append((dn_ref.at[pl.ds(p * part, part)],
+                      lambda o, p=p: dn_out.at[pl.ds(pl.multiple_of(o * rows_d + p * part, 8), part)], zf, None))
+    wide = gu_ref.shape[1] // chunks
+    for c in range(chunks):
+        later.append((gu_ref.at[:, pl.ds(c * wide, wide)],
+                      lambda o, c=c: gu_out.at[pl.ds(pl.multiple_of(o * rows, 8), rows), pl.ds(c * wide, wide)], True, None))
+    keeps = []
+    for n, (own, view, zf, other) in enumerate(first + later):
+        keep = pltpu.make_async_copy(own, view(spot.dp), local.at[n])
+        keep.start()
+        keeps.append(keep)
+    number = 0
+    drains = []
+    for group in (first, later):
+        floods = []
+        for own, view, zf, other in group:
+            floods.append(Flood(spot, number, own, view, sends, recvs, zf, None if other is None else mates))
+            number += 1
+        levels = [f.levels() for f in floods]
+        for level in range(max(map(len, levels))):
+            for ls in levels:
+                if level < len(ls):
+                    for step in ls[level]:
+                        step()
+        for f, (own, view, zf, other) in zip(floods, group):
+            if other is not None:
+                f.mates(other)
+            drains += f.drains
+    for drain in drains:
+        drain()
+    for keep in keeps:
+        keep.wait()
+
+
+def gather_weights(sizes, qkv, rest, gu, dn, chunks=4):
+    n_dp = sizes[0] * sizes[1]
+    items = 4 + chunks
+    arrays = (qkv, rest, gu, dn)
+    return pl.pallas_call(
+        functools.partial(gather_kernel, sizes, chunks),
+        out_shape=tuple(jax.ShapeDtypeStruct((a.shape[0] * n_dp, a.shape[1]), a.dtype) for a in arrays),
+        in_specs=[pl.BlockSpec(memory_space=pltpu.VMEM)] * 4,
+        out_specs=(pl.BlockSpec(memory_space=pl.ANY),) * 4,
+        scratch_shapes=[pltpu.SemaphoreType.DMA((5, items, n_dp)), pltpu.SemaphoreType.DMA((items, n_dp)),
+                        pltpu.SemaphoreType.DMA((2, n_dp)), pltpu.SemaphoreType.DMA((items,))],
+        compiler_params=pltpu.CompilerParams(collective_id=1, has_side_effects=True),
+    )(*arrays)
+
+
+def add_into(view, more):
+    view[...] = (view[...].astype(jnp.float32) + more[...].astype(jnp.float32)).astype(view.dtype)
+
+
+class Reduce:
+    def __init__(self, spot, number, view, one, two, sends, recv_one, recv_two, x_first):
+        self.s, self.n, self.view, self.one, self.two = spot, number, view, one, two
+        self.sends, self.recv_one, self.recv_two, self.x_first = sends, recv_one, recv_two, x_first
+        if x_first:
+            self.np, self.nq, self.p, self.q = spot.nx, spot.nz, spot.x, spot.z
+        else:
+            self.np, self.nq, self.p, self.q = spot.nz, spot.nx, spot.z, spot.x
+        self.drains = []
+
+    def owner(self, p, q):
+        return q * self.s.nx + p if self.x_first else p * self.s.nx + q
+
+    def along(self, first, value):
+        return self.s.device(x=value) if first == self.x_first else self.s.device(z=value)
+
+    def push(self, cond, o, dst, recv, device):
+        copy = pltpu.make_async_remote_copy(
+            src_ref=self.view(o), dst_ref=dst, send_sem=self.sends.at[self.n, o], recv_sem=recv,
+            device_id=device, device_id_type=MESH)
+        pl.when(cond)(lambda: copy.start())
+        self.drains.append(lambda: pl.when(cond)(lambda: copy.wait_send()))
+
+    def take(self, cond, o, slot, recv):
+        def run():
+            pltpu.make_async_remote_copy(
+                src_ref=slot, dst_ref=slot, send_sem=self.sends.at[self.n, o], recv_sem=recv,
+                device_id=self.s.device(), device_id_type=MESH).wait_recv()
+            add_into(self.view(o), slot)
+        pl.when(cond)(run)
+
+    def order(self):
+        return sorted(range(-(self.nq - 1), self.nq), key=lambda d: (-abs(d), d))
+
+    def phase_one(self):
+        steps = []
+        for turn in range(2):
+            sign = jnp.where(self.p * 2 < self.np, 1, -1) * (1 if turn == 0 else -1)
+            for k in range(self.np - 1, 0, -1):
+                for dq in self.order():
+                    def step(sign=sign, k=k, dq=dq):
+                        p, q = self.p + sign * k, self.q + dq
+                        here = jnp.logical_and(between(p, self.np), between(q, self.nq))
+                        o = self.owner(p, q)
+                        if self.np > 2:
+                            behind = jnp.logical_and(here, between(self.p - sign, self.np))
+                            self.take(behind, o, self.one.at[p, q], self.recv_one.at[self.n, p, q])
+                        last = jnp.logical_and(k == 1, sign < 0)
+                        slot = jnp.where(last, self.np, p)
+                        self.push(here, o, self.one.at[slot, q], self.recv_one.at[self.n, slot, q],
+                                  self.along(True, self.p + sign))
+                    steps.append(step)
+        return steps
+
+    def settle(self, cond, q):
+        o = self.owner(self.p, q)
+        below = self.p > 0
+        above = self.p < self.np - 1
+        if cond is not None:
+            below, above = jnp.logical_and(cond, below), jnp.logical_and(cond, above)
+        self.take(below, o, self.one.at[self.p, q], self.recv_one.at[self.n, self.p, q])
+        self.take(above, o, self.one.at[self.np, q], self.recv_one.at[self.n, self.np, q])
+
+    def phase_two(self):
+        steps = []
+        for turn in range(2):
+            sign = jnp.where(self.q * 2 < self.nq, 1, -1) * (1 if turn == 0 else -1)
+            for k in range(self.nq - 1, 0, -1):
+                def step(sign=sign, k=k):
+                    q = self.q + sign * k
+                    here = between(q, self.nq)
+                    o = self.owner(self.p, q)
+                    self.settle(here, q)
+                    behind = jnp.logical_and(here, between(self.q - sign, self.nq))
+                    self.take(behind, o, self.two.at[q], self.recv_two.at[self.n, q])
+                    last = jnp.logical_and(k == 1, sign < 0)
+                    slot = jnp.where(last, self.nq, q)
+                    self.push(here, o, self.two.at[slot], self.recv_two.at[self.n, slot], self.along(False, self.q + sign))
+                steps.append(step)
+        return steps
+
+    def finish(self, out):
+        o = self.owner(self.p, self.q)
+        self.settle(None, self.q)
+        out[...] = self.view(o)[...].astype(jnp.float32)
+        for cond, slot in ((self.q > 0, self.q), (self.q < self.nq - 1, self.nq)):
+            def run(slot=slot):
+                two = self.two.at[slot]
+                pltpu.make_async_remote_copy(
+                    src_ref=two, dst_ref=two, send_sem=self.sends.at[self.n, o], recv_sem=self.recv_two.at[self.n, slot],
+                    device_id=self.s.device(), device_id_type=MESH).wait_recv()
+                out[...] += two[...].astype(jnp.float32)
+            pl.when(cond)(run)
+
+
+def reduce_kernel(sizes, chunks, gu_in, dn_in, gu_out, dn_out, gu_ref, dn_ref, g1, g2, d1a, d2a, d1b, d2b,
+                  sends, r1, r2, local):
+    spot = Spot(sizes)
+    loads = [pltpu.make_async_copy(dn_in, dn_ref, local.at[0]), pltpu.make_async_copy(gu_in, gu_ref, local.at[1])]
+    for l in loads:
+        l.start()
+    enter(spot, line_neighbours(spot))
+    n_dp, rows_g, cols = gu_ref.shape
+    _, rows_d, width = dn_ref.shape
+    half = rows_d // 2
+    wide = cols // chunks
+    items, outs = [], []
+    for p, xf in ((0, True), (1, False)):
+        one, two = (d1a, d2a) if p == 0 else (d1b, d2b)
+        items.append(Reduce(spot, p, lambda o, p=p: dn_ref.at[o, pl.ds(p * half, half)], one, two, sends, r1, r2, xf))
+        outs.append(dn_out.at[pl.ds(p * half, half)])
+    for c in range(chunks):
+        cut = pl.ds(c * wide, wide)
+        items.append(Reduce(spot, 2 + c, lambda o, c=c: gu_ref.at[o, :, pl.ds(c * wide, wide)],
+                            g1.at[c], g2.at[c], sends, r1, r2, True))
+        outs.append(gu_out.at[:, cut])
+    for l in loads:
+        l.wait()
+    for item in items:
+        for step in item.phase_one():
+            step()
+    lists = [item.phase_two() for item in items]
+    for turn in range(2):
+        for l in lists:
+            for step in l[turn * len(l) // 2:(turn + 1) * len(l) // 2]:
+                step()
+    for item, out in zip(items, outs):
+        item.finish(out)
+    for item in items:
+        for drain in item.drains:
+            drain()
+
+
+def reduce_experts(sizes, gu, dn, chunks=4):
+    nz, nx = sizes[:2]
+    n_dp = nz * nx
+    big = max(nz, nx)
+    gu = gu.reshape(n_dp, gu.shape[0] // n_dp, gu.shape[1])
+    dn = dn.reshape(n_dp, dn.shape[0] // n_dp, dn.shape[1])
+    items = 2 + chunks
+    half = (dn.shape[1] // 2, dn.shape[2])
+    wide = (gu.shape[1], gu.shape[2] // chunks)
+    bf = gu.dtype
+    return pl.pallas_call(
+        functools.partial(reduce_kernel, sizes, chunks),
+        out_shape=(jax.ShapeDtypeStruct(gu.shape[1:], jnp.float32), jax.ShapeDtypeStruct(dn.shape[1:], jnp.float32)),
+        in_specs=[pl.BlockSpec(memory_space=pl.ANY)] * 2,
+        out_specs=(pl.BlockSpec(memory_space=pltpu.VMEM),) * 2,
+        scratch_shapes=[
+            pltpu.VMEM(gu.shape, bf), pltpu.VMEM(dn.shape, bf),
+            pltpu.VMEM((chunks, nx + 1, nz) + wide, bf), pltpu.VMEM((chunks, nz + 1) + wide, bf),
+            pltpu.VMEM((nx + 1, nz) + half, bf), pltpu.VMEM((nz + 1,) + half, bf),
+            pltpu.VMEM((nz + 1, nx) + half, bf), pltpu.VMEM((nx + 1,) + half, bf),
+            pltpu.SemaphoreType.DMA((items, n_dp)), pltpu.SemaphoreType.DMA((items, big + 1, big)),
+            pltpu.SemaphoreType.DMA((items, big + 1)), pltpu.SemaphoreType.DMA((2,))],
+        compiler_params=pltpu.CompilerParams(collective_id=2, has_side_effects=True, vmem_limit_bytes=60 << 20),
+    )(gu, dn)
+
+
+def dense_kernel(sizes, cuts, *refs):
+    n_in = len(cuts)
+    ins, outs, rest = refs[:n_in], refs[n_in:2 * n_in], list(refs[2 * n_in:])
+    spot = Spot(sizes)
+    mate = spot.device(core=1 - spot.core)
+    others = []
+    for d in range(1, spot.ny):
+        others.append((None, spot.device(y=lax.rem(spot.y + d, spot.ny))))
+    enter(spot, line_neighbours(spot) + [(None, mate)] + others)
+    sends, r1, r2, mate_sem, y_sem, out_sem, local = rest[-7:]
+    pieces, drains = [], []
+    number = 0
+    for a in range(n_in):
+        mine, one, two, ybuf, final = rest[5 * a:5 * a + 5]
+        chunks = cuts[a]
+        half = ins[a].shape[2] // 2
+        wide = half // chunks
+        for c in range(chunks):
+            def cols(core, half=half, wide=wide, c=c):
+                return pl.ds(pl.multiple_of(core * half + c * wide, 128), wide)
+            pieces.append((number, a, c, wide, cols, mine, one, two, ybuf, final))
+            number += 1
+    reduces = []
+    n_dp = spot.nz * spot.nx
+
+    def to_mate(number, a, c, wide, cols, mine):
+        return pltpu.make_async_remote_copy(
+            src_ref=ins[a].at[:, :, cols(1 - spot.core)], dst_ref=mine.at[c], send_sem=mate_sem.at[0, number],
+            recv_sem=mate_sem.at[1, number], device_id=mate, device_id_type=MESH)
+
+    for number, a, c, wide, cols, mine, one, two, ybuf, final in pieces:
+        to_mate(number, a, c, wide, cols, mine).start()
+    for number, a, c, wide, cols, mine, one, two, ybuf, final in pieces:
+        to_mate(number, a, c, wide, cols, mine).wait()
+        own = ins[a]
+
+        def add(o, carry, own=own, mine=mine, c=c, cols=cols):
+            mine[c, o] = (mine[c, o].astype(jnp.float32) + own[o, :, cols(spot.core)].astype(jnp.float32)).astype(mine.dtype)
+            return carry
+        lax.fori_loop(0, n_dp, add, 0)
+        r = Reduce(spot, number, lambda o, mine=mine, c=c: mine.at[c, o], one.at[c], two.at[c], sends, r1, r2, True)
+        reduces.append(r)
+        for step in r.phase_one():
+            step()
+    lists = [r.phase_two() for r in reduces]
+    for turn in range(2):
+        for l in lists:
+            for step in l[turn * len(l) // 2:(turn + 1) * len(l) // 2]:
+                step()
+    for r, (number, a, c, wide, cols, mine, one, two, ybuf, final) in zip(reduces, pieces):
+        r.finish(final.at[c])
+        ybuf[c, spot.y] = final[c].astype(ybuf.dtype)
+        for d in range(1, spot.ny):
+            copy = pltpu.make_async_remote_copy(
+                src_ref=ybuf.at[c, spot.y], dst_ref=ybuf.at[c, spot.y], send_sem=y_sem.at[0, number, d],
+                recv_sem=y_sem.at[1, number, spot.y], device_id=spot.device(y=lax.rem(spot.y + d, spot.ny)),
+                device_id_type=MESH)
+            copy.start()
+            drains.append(copy.wait_send)
+    for number, a, c, wide, cols, mine, one, two, ybuf, final in pieces:
+        for d in range(1, spot.ny):
+            y = lax.rem(spot.y + d, spot.ny)
+            pltpu.make_async_remote_copy(
+                src_ref=ybuf.at[c, y], dst_ref=ybuf.at[c, y], send_sem=y_sem.at[0, number, d],
+                recv_sem=y_sem.at[1, number, y], device_id=mate, device_id_type=MESH).wait_recv()
+        total = ybuf[c, 0].astype(jnp.float32)
+        for y in range(1, spot.ny):
+            total = total + ybuf[c, y].astype(jnp.float32)
+        final[c] = total
+        outs[a][:, cols(spot.core)] = total
+        copy = pltpu.make_async_remote_copy(
+            src_ref=final.at[c], dst_ref=outs[a].at[:, cols(spot.core)], send_sem=out_sem.at[0, number],
+            recv_sem=out_sem.at[1, number], device_id=mate, device_id_type=MESH)
+        copy.start()
+        drains.append(copy.wait_send)
+    for number, a, c, wide, cols, mine, one, two, ybuf, final in pieces:
+        pltpu.make_async_remote_copy(
+            src_ref=final.at[c], dst_ref=outs[a].at[:, cols(1 - spot.core)], send_sem=out_sem.at[0, number],
+            recv_sem=out_sem.at[1, number], device_id=mate, device_id_type=MESH).wait_recv()
+    for r in reduces:
+        drains += r.drains
+    for drain in drains:
+        drain()
+
+
+def reduce_dense(sizes, arrays, cuts):
+    nz, nx, ny = sizes[:3]
+    n_dp = nz * nx
+    big = max(nz, nx)
+    arrays = [a.reshape(n_dp, a.shape[0] // n_dp, a.shape[1]) for a in arrays]
+    items = sum(cuts)
+    scratch = []
+    for a, cut in zip(arrays, cuts):
+        block = (a.shape[1], a.shape[2] // 2 // cut)
+        scratch += [pltpu.VMEM((cut, n_dp) + block, a.dtype), pltpu.VMEM((cut, nx + 1, nz) + block, a.dtype),
+                    pltpu.VMEM((cut, nz + 1) + block, a.dtype), pltpu.VMEM((cut, ny) + block, a.dtype),
+                    pltpu.VMEM((cut,) + block, jnp.float32)]
+    scratch += [pltpu.SemaphoreType.DMA((items, n_dp)), pltpu.SemaphoreType.DMA((items, big + 1, big)),
+                pltpu.SemaphoreType.DMA((items, big + 1)), pltpu.SemaphoreType.DMA((2, items)),
+                pltpu.SemaphoreType.DMA((2, items, ny)), pltpu.SemaphoreType.DMA((2, items)),
+                pltpu.SemaphoreType.DMA((2,))]
+    return pl.pallas_call(
+        functools.partial(dense_kernel, sizes, tuple(cuts)),
+        out_shape=tuple(jax.ShapeDtypeStruct(a.shape[1:], jnp.float32) for a in arrays),
+        in_specs=[pl.BlockSpec(memory_space=pltpu.VMEM)] * len(arrays),
+        out_specs=(pl.BlockSpec(memory_space=pltpu.VMEM),) * len(arrays),
+        scratch_shapes=scratch,
+        compiler_params=pltpu.CompilerParams(collective_id=3, has_side_effects=True, vmem_limit_bytes=60 << 20),
+    )(*arrays)
 
 
 epsilon = 1e-06
@@ -58,6 +537,7 @@
 
 
 def per_device(
+    sizes,
     tokens,
     prev_logits,
     segment_ids,
@@ -84,31 +564,19 @@
     block_rows = min(length, 768)
     starts = jnp.arange(length // block_rows) * block_rows
     query_scale = HEAD_DIM ** (-0.5)
-    dense_parts = (
-        attn_gain,
-        qkv_weight,
-        out_weight,
-        ffn_gain,
-        router_weight,
-        mix_weight,
-        const_weight,
-    )
-    dense_full = (
-        lax.all_gather(dense_parts[0], "dp", axis=0, tiled=True),
-        lax.all_gather(dense_parts[1], "dp", axis=0, tiled=True),
-        lax.all_gather(dense_parts[2], "dp", axis=0, tiled=True),
-        lax.all_gather(dense_parts[3], "dp", axis=0, tiled=True),
-        lax.all_gather(dense_parts[4], "dp", axis=0, tiled=True),
-        lax.all_gather(dense_parts[5], "dp", axis=0, tiled=True),
-        lax.all_gather(dense_parts[6], "dp", axis=0, tiled=True),
-    )
-    expert_full = (
-        lax.all_gather(gate_up_weight, "dp", axis=1, tiled=True),
-        lax.all_gather(down_weight, "dp", axis=1, tiled=True),
-    )
-    gain_one, qkv_full, out_full, gain_two, router_full, mix_full, const_full = dense_full
-    gate_up_local = expert_full[0][0]
-    down_local = expert_full[1][0]
+    rows = qkv_weight.shape[0]
+    small = jnp.concatenate(
+        [attn_gain[:, None], ffn_gain[:, None], mix_weight, const_weight, router_weight], axis=1
+    )
+    rest = jnp.concatenate([out_weight, jnp.pad(small, ((0, 0), (0, 256 - small.shape[1])))], axis=1)
+    qkv_full, rest_full, gate_up_local, down_local = gather_weights(
+        sizes, qkv_weight, rest, gate_up_weight[0], down_weight[0]
+    )
+    out_full = rest_full[:, :width]
+    small_full = rest_full[:, width:]
+    gain_one, gain_two = small_full[:, 0], small_full[:, 1]
+    mix_full, const_full = small_full[:, 2:6], small_full[:, 6:8]
+    router_full = small_full[:, 8 : 8 + router_weight.shape[1]]
     inputs = tokens.astype(jnp.float32)
     inverse_one = lax.rsqrt(jnp.mean(inputs * inputs, axis=-1, keepdims=True) + epsilon)
     normed = (inputs * inverse_one * gain_one.astype(jnp.float32)).astype(jnp.bfloat16)
@@ -197,25 +665,8 @@
         + jnp.dot(const_coef, const_float.T, precision=highest)
     )
     layer_out = (hidden_state + branch_out).astype(jnp.bfloat16)
-    dense_back = (
-        lax.all_gather(dense_parts[0], "dp", axis=0, tiled=True),
-        lax.all_gather(dense_parts[1], "dp", axis=0, tiled=True),
-        lax.all_gather(dense_parts[2], "dp", axis=0, tiled=True),
-        lax.all_gather(dense_parts[3], "dp", axis=0, tiled=True),
-        lax.all_gather(dense_parts[4], "dp", axis=0, tiled=True),
-        lax.all_gather(dense_parts[5], "dp", axis=0, tiled=True),
-        lax.all_gather(dense_parts[6], "dp", axis=0, tiled=True),
-    )
-    expert_back = (
-        lax.all_gather(gate_up_weight, "dp", axis=1, tiled=True),
-        lax.all_gather(down_weight, "dp", axis=1, tiled=True),
-    )
-    qkv_back = dense_back[1]
-    out_back = dense_back[2]
-    router_back = dense_back[4]
-    mix_back = dense_back[5]
-    gate_up_back = expert_back[0][0]
-    down_back = expert_back[1][0]
+    qkv_back, out_back, router_back, mix_back = qkv_full, out_full, router_full, mix_full
+    gate_up_back, down_back = gate_up_local, down_local
     out_grad = cotangent.astype(jnp.float32)
     pair_grad = (
         (gate_weights[:, :, None] * out_grad[:, None, :])
@@ -256,13 +707,8 @@
     routed_grad = jnp.sum(
         back_padded[flat_slot].astype(jnp.float32).reshape(length, 2, width), axis=1
     )
-    expert_shards = (
-        lax.psum_scatter(
-            gate_up_weight_grad[None].astype(jnp.bfloat16), "dp", scatter_dimension=1, tiled=True
-        ).astype(jnp.float32),
-        lax.psum_scatter(
-            down_weight_grad[None].astype(jnp.bfloat16), "dp", scatter_dimension=1, tiled=True
-        ).astype(jnp.float32),
+    gate_up_shard, down_shard = reduce_experts(
+        sizes, gate_up_weight_grad.astype(jnp.bfloat16), down_weight_grad.astype(jnp.bfloat16)
     )
     grad_dot_normed = jnp.sum(out_grad * ffn_float, axis=-1)
     grad_dot_const = jnp.dot(out_grad, const_float, precision=highest)
@@ -360,61 +806,37 @@
         inputs, inverse_one, gain_one.astype(jnp.float32), normed_one_grad
     )
     tokens_grad = hidden_grad + input_part
-    dense_grads = (
-        gain_one_grad,
-        qkv_weight_grad,
-        out_weight_grad,
-        gain_two_grad,
-        router_weight_grad,
-        mix_weight_grad,
-        const_weight_grad,
-    )
-    dense_grads = (
-        lax.psum(dense_grads[0].astype(jnp.bfloat16), "expert").astype(jnp.float32),
-        lax.psum(dense_grads[1].astype(jnp.bfloat16), "expert").astype(jnp.float32),
-        lax.psum(dense_grads[2].astype(jnp.bfloat16), "expert").astype(jnp.float32),
-        lax.psum(dense_grads[3].astype(jnp.bfloat16), "expert").astype(jnp.float32),
-        lax.psum(dense_grads[4].astype(jnp.bfloat16), "expert").astype(jnp.float32),
-        lax.psum(dense_grads[5].astype(jnp.bfloat16), "expert").astype(jnp.float32),
-        lax.psum(dense_grads[6].astype(jnp.bfloat16), "expert").astype(jnp.float32),
-    )
-    dense_shards = (
-        lax.psum_scatter(
-            dense_grads[0].astype(jnp.bfloat16), "dp", scatter_dimension=0, tiled=True
-        ).astype(jnp.float32),
-        lax.psum_scatter(
-            dense_grads[1].astype(jnp.bfloat16), "dp", scatter_dimension=0, tiled=True
-        ).astype(jnp.float32),
-        lax.psum_scatter(
-            dense_grads[2].astype(jnp.bfloat16), "dp", scatter_dimension=0, tiled=True
-        ).astype(jnp.float32),
-        lax.psum_scatter(
-            dense_grads[3].astype(jnp.bfloat16), "dp", scatter_dimension=0, tiled=True
-        ).astype(jnp.float32),
-        lax.psum_scatter(
-            dense_grads[4].astype(jnp.bfloat16), "dp", scatter_dimension=0, tiled=True
-        ).astype(jnp.float32),
-        lax.psum_scatter(
-            dense_grads[5].astype(jnp.bfloat16), "dp", scatter_dimension=0, tiled=True
-        ).astype(jnp.float32),
-        lax.psum_scatter(
-            dense_grads[6].astype(jnp.bfloat16), "dp", scatter_dimension=0, tiled=True
-        ).astype(jnp.float32),
-    )
+    small_grad = jnp.concatenate(
+        [gain_one_grad[:, None], gain_two_grad[:, None], mix_weight_grad, const_weight_grad, router_weight_grad], axis=1
+    )
+    rest_grad = jnp.concatenate(
+        [out_weight_grad, jnp.pad(small_grad, ((0, 0), (0, 256 - small_grad.shape[1])))], axis=1
+    )
+    qkv_shard, rest_shard = reduce_dense(
+        sizes, [qkv_weight_grad.astype(jnp.bfloat16), rest_grad.astype(jnp.bfloat16)], [3, 1]
+    )
+    small_shard = rest_shard[:, width:]
     return (
         layer_out,
         tokens_grad,
         prev_grad,
-        dense_shards[0],
-        dense_shards[1],
-        dense_shards[2],
-        dense_shards[3],
-        dense_shards[4],
-        dense_shards[5],
-        dense_shards[6],
-        expert_shards[0],
-        expert_shards[1],
-    )
+        small_shard[:, 0],
+        qkv_shard,
+        rest_shard[:, :width],
+        small_shard[:, 1],
+        small_shard[:, 8 : 8 + router_weight.shape[1]],
+        small_shard[:, 2:6],
+        small_shard[:, 6:8],
+        gate_up_shard[None],
+        down_shard[None],
+    )
+
+
+def grid_sizes(mesh):
+    along_dp, along_expert = mesh.devices[:, 0], mesh.devices[0]
+    nx = len({d.coords[0] for d in along_dp})
+    ny = len({d.coords[1] for d in along_expert})
+    return (len(along_dp) // nx, nx, ny, len(along_expert) // ny)
 
 
 def solution(mesh):
@@ -451,5 +873,5 @@
         P("expert", "dp", None),
     )
     return jax.shard_map(
-        per_device, mesh=mesh, in_specs=in_specs, out_specs=out_specs, check_vma=False
-    )
+        functools.partial(per_device, grid_sizes(mesh)), mesh=mesh, in_specs=in_specs, out_specs=out_specs, check_vma=False
+    )

time: 1050 us -> 731 us (0.70)
  waiting for transfers between devices: 521 us -> 5.82 us
  Pallas kernels: 0 us -> 299 us
  blocking collectives: 110 us -> 0 us
  local copies, waits for them, and re-layouts: 96.5 us -> 114 us
  between operations: 17.2 us -> 2.14 us
    pallas_call x0 -> x3, Pallas kernels: none -> 299 us  [the longest x1 131 us: gather_weights(): pl.pallas_call(functools.partial(gather_kernel, sizes, chunks), out_shape...]
    reduce_scatter x4 -> x0, waiting for transfers between devices: 286 us -> none  [the longest x1 118 us: per_device(): lax.psum_scatter(gate_up_weight_grad[None].astype(jnp.bfloat16), 'dp', sc...]
    unnamed x15 -> x0, waiting for transfers between devices: 138 us -> none
    all_gather x3 -> x0, blocking collectives: 61.2 us -> none  [the longest x1 26.1 us: per_device(): lax.all_gather(dense_parts[4], 'dp', axis=0, tiled=True)]
    unnamed x2 -> x0, blocking collectives: 42.9 us -> none
    psum x1 -> x0, waiting for transfers between devices: 33.3 us -> none  [per_device(): lax.psum(dense_grads[1].astype(jnp.bfloat16), 'expert').astype(jnp.float32)]
    all_gather x4 -> x0, waiting for transfers between devices: 25 us -> none  [the longest x1 25 us: per_device(): lax.all_gather(down_weight, 'dp', axis=1, tiled=True)]
    all_to_all x1, waiting for transfers between devices: 14.5 us -> 0.01 us  [per_device(): lax.all_to_all(send_rows, 'expert', split_axis=0, concat_axis=0, tiled=True)]
  transfers between devices with their start and end apart: 16 -> 4, of which waited for: 12 -> 1; matrix products, arithmetic and copies ran while one was open for 21% -> 16% of each run, Pallas kernels for 0% -> 16%
where the time goes in v1:
time: 731 us; the launch traced here: 722 us
  Pallas kernels  299 us (41%)
  matrix products  172 us (24%)
  local copies, waits for them, and re-layouts  114 us (16%)
  other arithmetic  112 us (15%)
  starting transfers between devices  16.6 us (2%)
    pallas_call x1, Pallas kernels, gather_weights(): pl.pallas_call(functools.partial(gather_kernel, sizes, chunks), out_shape...  131 us
    pallas_call x1, Pallas kernels, reduce_experts(): pl.pallas_call(functools.partial(reduce_kernel, sizes, chunks), out_shape...  117 us
    pallas_call x1, Pallas kernels, reduce_dense(): pl.pallas_call(functools.partial(dense_kernel, sizes, tuple(cuts)), out_s...  51.1 us
    dot_general x1, matrix products, backward_block(): jnp.einsum('qhd,khd->hqk', attended_grad, value_rows, preferred_element_t...  24.1 us
    convert_element_type x1, other arithmetic, backward_block(): score_grad = (probs_full * (prob_grad - row_dot)).astype(jnp.bfloat16)  23.5 us
    unnamed x176, local copies, waits for them, and re-layouts  19.6 us
  transfers between devices with their start and end apart: 4, of which 1 were waited for; matrix products, arithmetic and copies ran while one was open for 16% of the time, Pallas kernels for 16%

profile of v1, /device:TPU:0, one launch (start us, length us, event | category | flops | bytes accessed | tf_op | source)
XLA Modules:
  0.0 722.0 jit_solution(9751183797520327649)
XLA Ops:
  11.9 5.3 scatter_custom_fusion
  22.8 6.3 scatter_custom_fusion.2
  29.1 6.2 scatter_custom_fusion.1
  40.2 131.1 %shard_map.247 = (bf16[768,2304]{1,0:T(8,128)(2,1)}, bf16[768,1024]{1,0:T(8,128)(2,1)}, bf16[768,4096]{1,0:T(8,128)(2,1)}, bf16[2048,768]{1,0:T(8,128)(2,1)}) custom-call(bf16[96,2304]{1,0:T(8,128)(2,1)} %qkv_ref.1, bf16[96,1024]{1,0:T(8,128)(2,1)} %fusion.57.rest_ref, bf16[96,4096]{1,0:T(8,128)(2,1)} %bitcast.142, bf16[256,768]{1,0:T(8,128)(2,1)} %bitcast.144), custom_call_target="tpu_custom_call" | custom-call | tf_op jit(solution)/shard_map/pallas_call | solution.py:203
  172.6 5.2 fusion.55
  182.5 11.6 %select_reduce_fusion = (f32[12,768]{1,0:T(8,128)S(1)}, f32[12,768,768]{1,2,0:T(8,128)}) fusion(pred[768,768]{0,1:T(8,128)(4,1)S(1)} %fusion.27, bf16[768,12,32]{0,2,1:T(8,128)(2,1)S(1)} %get-tuple-element.166, bf16[768,12,32]{0,2,1:T(8,128)(2,1)S(1)} %get-tuple-element.167, f32[768,12,32]{0,2,1:T(8,128)S(1)} %get-tuple-element.161, ...), kind=kOutput, calls=%fused_computation.14 | convolution fusion | flops 924244992 | bytes 32477184 | tf_op jit(solution)/shard_map/while/body/eval_jaxpr/qhd,khd->hqk/dot_general | solution.py:519
  194.1 12.1 %fusion = f32[12,768]{1,0:T(8,128)S(1)} fusion(f32[12,768,768]{1,2,0:T(8,128)} %get-tuple-element.171, f32[12,768]{1,0:T(8,128)S(1)} %get-tuple-element.170, pred[768,768]{0,1:T(8,128)(4,1)S(1)} %fusion.27), kind=kLoop, calls=%fused_computation.13 | loop fusion | flops 21224448 | bytes 28975104 | tf_op jit(solution)/shard_map/while/body/eval_jaxpr/reduce_sum | solution.py:597
  206.3 13.7 %fusion.33 = bf16[12,64,768]{2,1,0:T(8,128)(2,1)S(1)} fusion(f32[12,768,768]{1,2,0:T(8,128)} %get-tuple-element.171, f32[12,768]{1,0:T(8,128)S(1)} %fusion, f32[12,768]{1,0:T(8,128)S(1)} %get-tuple-element.170, pred[768,768]{0,1:T(8,128)(4,1)S(1)} %fusion.27, f32[768,3,12,64]{0,3,2,1:T(8,128)} %bitcast.126), kind=kOutput, calls=%fused_computation.81 | convolution fusion | flops 934871040 | bytes 31334400 | tf_op jit(solution)/shard_map/while/body/eval_jaxpr/hqk,khd->qhd/dot_general | solution.py:599
  229.3 4.9 all-to-all-start
  260.4 5.5 mul.623
  265.9 6.9 mul.624
  273.6 8.7 %scatter_custom_fusion.3 = bf16[769,768]{1,0:T(8,128)(2,1)S(1)} fusion(s32[1536]{0:T(1024)} %copy-done.63, f32[1536,768]{1,0:T(8,128)} %mul.624, f32[1536]{0:T(1024)} %div.115, bf16[]{:T(256)} %constant.59.clone.1), kind=kCustom, calls=%fused_computation.55 | custom fusion | flops 2359296 | bytes 5908480 | tf_op jit(solution)/shard_map/scatter | solution.py:679
  290.7 10.0 %fusion.101 = f32[768,4096]{1,0:T(8,128)} fusion(bf16[768,768]{1,0:T(8,128)(2,1)} %bitcast.17, bf16[768,4096]{1,0:T(8,128)(2,1)} %get-tuple-element.79), kind=kOutput, calls=%fused_computation.213 | convolution fusion | flops 4831838208 | bytes 20054016 | tf_op jit(solution)/shard_map/dot_general | solution.py:647
  300.7 5.8 all-to-all-done.2
  306.5 10.3 %multiply_convert_fusion.2 = (bf16[768,2048]{1,0:T(8,128)(2,1)}, bf16[768,2048]{1,0:T(8,128)(2,1)}, bf16[768,2048]{1,0:T(8,128)(2,1)S(1)}) fusion(f32[768,4096]{1,0:T(8,128)} %fusion.101, bf16[768,768]{1,0:T(8,128)(2,1)S(1)} %bitcast.138, bf16[2048,768]{1,0:T(8,128)(2,1)} %get-tuple-element.80), kind=kOutput, calls=%fused_computation.22 | convolution fusion | flops 2441084928 | bytes 26345472 | tf_op jit(solution)/shard_map/rd,fd->rf/dot_general | solution.py:685
  328.2 10.9 %convolution_convert_fusion = bf16[768,4096]{1,0:T(8,128)(2,1)} fusion(bf16[768,768]{1,0:T(8,128)(2,1)} %bitcast.17, bf16[768,2048]{1,0:T(8,128)(2,1)} %get-tuple-element.152, bf16[768,2048]{1,0:T(8,128)(2,1)} %get-tuple-element.151), kind=kOutput, calls=%fused_computation.19 | convolution fusion | flops 4847566848 | bytes 13762560 | tf_op jit(solution)/shard_map/rd,rf->df/dot_general | solution.py:695
  339.1 116.9 %shard_map.249 = (f32[96,4096]{1,0:T(8,128)}, f32[256,768]{1,0:T(8,128)}) custom-call(bf16[8,96,4096]{2,1,0:T(8,128)(2,1)} %bitcast.129, bf16[8,256,768]{2,1,0:T(8,128)(2,1)} %bitcast.135), custom_call_target="tpu_custom_call" | custom-call | tf_op jit(solution)/shard_map/pallas_call | solution.py:361
  456.0 9.9 %fusion.29 = bf16[768,768]{1,0:T(8,128)(2,1)} fusion(bf16[768,4096]{1,0:T(8,128)(2,1)} %get-tuple-element.79, bf16[768,2048]{1,0:T(8,128)(2,1)} %get-tuple-element.152, bf16[768,2048]{1,0:T(8,128)(2,1)} %get-tuple-element.151), kind=kOutput, calls=%fused_computation.76 | convolution fusion | flops 4845010944 | bytes 13762560 | tf_op jit(solution)/shard_map/rf,df->rd/dot_general | solution.py:698
  470.3 5.8 gather_fusion.2
  476.1 6.3 reshape.578
  482.4 13.6 %multiply_reduce_fusion.1 = (f32[768,2]{1,0:T(8,128)}, f32[768,768]{1,0:T(8,128)}) fusion(f32[768,2,768]{2,1,0:T(2,128)} %reshape.578, f32[768,768]{1,0:T(8,128)S(1)} %copy-done.4, f32[768,2]{1,0:T(8,128)} %copy-done.20), kind=kLoop, calls=%fused_computation.26 | loop fusion | flops 4127232 | bytes 9449472 | tf_op jit(solution)/shard_map/reduce_sum | solution.py:715
  504.6 5.7 gather_fusion.3
  510.2 6.3 reshape.579
  516.6 9.4 %reduce_sum.225 = f32[768,768]{1,0:T(8,128)} reduce(f32[768,2,768]{2,1,0:T(2,128)} %reshape.579, f32[]{:T(128)} %constant.53.clone.1), dimensions={1}, to_apply=%region_20.21 | reduce | flops 589824 | bytes 7077892 | tf_op jit(solution)/shard_map/reduce_sum | solution.py:707
  537.4 13.4 %fusion.34 = bf16[768,1,12,64]{0,3,2,1:T(8,128)(2,1)} fusion(bf16[768,12,64]{0,2,1:T(8,128)(2,1)} %bitcast.140, f32[12,768,768]{1,2,0:T(8,128)} %get-tuple-element.171, f32[12,768]{1,0:T(8,128)S(1)} %copy-done.33, pred[768,768]{0,1:T(8,128)(4,1)S(1)} %copy-done.6), kind=kOutput, calls=%fused_computation.82 | convolution fusion | flops 927793152 | bytes 31297536 | tf_op jit(solution)/shard_map/while/body/eval_jaxpr/hqk,qhd->khd/dot_general | solution.py:779
  550.8 24.1 %multiply_reduce_fusion = (f32[12,768]{1,0:T(8,128)}, f32[12,768,768]{1,2,0:T(8,128)}) fusion(f32[12,768,768]{1,2,0:T(8,128)} %get-tuple-element.171, f32[12,768]{1,0:T(8,128)S(1)} %copy-done.33, pred[768,768]{0,1:T(8,128)(4,1)S(1)} %copy-done.6, bf16[768,12,64]{0,2,1:T(8,128)(2,1)S(1)} %bitcast.141, f32[768,3,12,64]{0,3,2,1:T(8,128)} %bitcast.127), kind=kOutput, calls=%fused_computation.9 | convolution fusion | flops 934272000 | bytes 59645952 | tf_op jit(solution)/shard_map/while/body/eval_jaxpr/qhd,khd->hqk/dot_general | solution.py:768
  574.9 23.5 %multiply_convert_fusion = bf16[12,768,768]{1,2,0:T(8,128)(2,1)} fusion(f32[12,768,768]{1,2,0:T(8,128)} %get-tuple-element.178, f32[12,768,768]{1,2,0:T(8,128)} %get-tuple-element.171, f32[12,768]{1,0:T(8,128)} %get-tuple-element.177, f32[12,768]{1,0:T(8,128)} %log_add_fusion, pred[768,768]{0,1:T(8,128)(4,1)} %copy-done.5), kind=kLoop, calls=%fused_computation.8 | loop fusion | flops 35389440 | bytes 71442432 | tf_op jit(solution)/shard_map/while/body/eval_jaxpr/convert_element_type | solution.py:772
  598.4 11.5 %convolution_bitcast_fusion = f32[768,12,64]{0,2,1:T(8,128)} fusion(bf16[12,768,768]{1,2,0:T(8,128)(2,1)} %multiply_convert_fusion, f32[768,12,32]{0,2,1:T(8,128)} %copy-done.8, f32[768,12,32]{0,2,1:T(8,128)} %copy-done.7), kind=kOutput, calls=%fused_computation.74 | convolution fusion | flops 907739136 | bytes 18874368 | tf_op jit(solution)/shard_map/while/body/eval_jaxpr/hqk,qhd->khd/dot_general | solution.py:776
  609.9 8.1 %multiply_bitcast_fusion = f32[768,12,64]{0,2,1:T(8,128)S(1)} fusion(bf16[12,768,768]{1,2,0:T(8,128)(2,1)} %multiply_convert_fusion, bf16[768,12,32]{0,2,1:T(8,128)(2,1)} %copy-done.18, bf16[768,12,32]{0,2,1:T(8,128)(2,1)} %copy-done.19), kind=kOutput, calls=%fused_computation.62 | convolution fusion | flops 908918784 | bytes 17694720 | tf_op jit(solution)/shard_map/while/body/eval_jaxpr/hqk,khd->qhd/dot_general | solution.py:773
  622.4 5.1 fusion.22
  627.6 4.9 convolution_convert_fusion.1
  642.9 51.1 %shard_map.248 = (f32[96,2304]{1,0:T(8,128)}, f32[96,1024]{1,0:T(8,128)}) custom-call(bf16[8,96,2304]{2,1,0:T(8,128)(2,1)} %bitcast.132, bf16[8,96,1024]{2,1,0:T(8,128)(2,1)} %pad_maximum_fusion.4.refs_1_), custom_call_target="tpu_custom_call" | custom-call | tf_op jit(solution)/shard_map/pallas_call | solution.py:478
  (293 shorter events, 149.7 us)
Async XLA Ops:
  19.6 16.4 %copy-start.25 = (bf16[768,768]{1,0:T(8,128)(2,1)S(1)}, bf16[768,768]{1,0:T(8,128)(2,1)}, u32[]{:S(2)}) copy-start(bf16[768,768]{1,0:T(8,128)(2,1)} %param.16) | copy-start | bytes 3538948
  22.2 15.4 %copy-start.12 = (bf16[768,768]{1,0:T(8,128)(2,1)S(1)}, bf16[768,768]{1,0:T(8,128)(2,1)}, u32[]{:S(2)}) copy-start(bf16[768,768]{1,0:T(8,128)(2,1)} %param.22) | copy-start | bytes 3538948
  22.8 15.5 %copy-start.63 = (s32[1536]{0:T(1024)}, s32[1536]{0:T(1024)S(1)}, u32[]{:S(2)}) copy-start(s32[1536]{0:T(1024)S(1)} %fusion.76) | copy-start | bytes 18436
  36.7 183.4 %copy-start.9 = (bf16[768,768]{0,1:T(8,128)(2,1)}, bf16[768,768]{0,1:T(8,128)(2,1)S(1)}, u32[]{:S(2)}) copy-start(bf16[768,768]{0,1:T(8,128)(2,1)S(1)} %copy.151) | copy-start | bytes 3538948
  38.3 220.1 %copy-start.2 = (bf16[768,768]{0,1:T(8,128)(2,1)}, bf16[768,768]{0,1:T(8,128)(2,1)S(1)}, u32[]{:S(2)}) copy-start(bf16[768,768]{0,1:T(8,128)(2,1)S(1)} %copy.165) | copy-start | bytes 3538948
  38.3 134.3 %copy-start.69 = (f32[768]{0:T(1024)S(1)}, f32[768]{0:T(1024)}, u32[]{:S(2)}) copy-start(f32[768]{0:T(1024)} %add_rsqrt_fusion.1) | copy-start | bytes 9220
  172.6 48.7 %copy-start.53 = (f32[768]{0:T(1024)}, f32[768]{0:T(1024)S(1)}, u32[]{:S(2)}) copy-start(f32[768]{0:T(1024)S(1)} %get-tuple-element.139) | copy-start | bytes 9220
  181.6 24.6 %copy-start.5 = (pred[768,768]{0,1:T(8,128)(4,1)}, pred[768,768]{0,1:T(8,128)(4,1)S(1)}, u32[]{:S(2)}) copy-start(pred[768,768]{0,1:T(8,128)(4,1)S(1)} %fusion.27) | copy-start | bytes 1769476
  182.4 11.6 %copy-start.7 = (f32[768,12,32]{0,2,1:T(8,128)}, f32[768,12,32]{0,2,1:T(8,128)S(1)}, u32[]{:S(2)}) copy-start(f32[768,12,32]{0,2,1:T(8,128)S(1)} %get-tuple-element.160) | copy-start | bytes 3538948
  182.4 11.6 %copy-start.8 = (f32[768,12,32]{0,2,1:T(8,128)}, f32[768,12,32]{0,2,1:T(8,128)S(1)}, u32[]{:S(2)}) copy-start(f32[768,12,32]{0,2,1:T(8,128)S(1)} %get-tuple-element.161) | copy-start | bytes 3538948
  182.5 11.6 %copy-start.18 = (bf16[768,12,32]{0,2,1:T(8,128)(2,1)}, bf16[768,12,32]{0,2,1:T(8,128)(2,1)S(1)}, u32[]{:S(2)}) copy-start(bf16[768,12,32]{0,2,1:T(8,128)(2,1)S(1)} %get-tuple-element.166) | copy-start | bytes 1769476
  182.5 11.6 %copy-start.19 = (bf16[768,12,32]{0,2,1:T(8,128)(2,1)}, bf16[768,12,32]{0,2,1:T(8,128)(2,1)S(1)}, u32[]{:S(2)}) copy-start(bf16[768,12,32]{0,2,1:T(8,128)(2,1)S(1)} %get-tuple-element.167) | copy-start | bytes 1769476
  194.1 12.2 %copy-start.34 = (f32[12,768]{1,0:T(8,128)}, f32[12,768]{1,0:T(8,128)S(1)}, u32[]{:S(2)}) copy-start(f32[12,768]{1,0:T(8,128)S(1)} %get-tuple-element.170) | copy-start | bytes 110596
  206.3 13.7 %copy-start.39 = (f32[12,768]{1,0:T(8,128)}, f32[12,768]{1,0:T(8,128)S(1)}, u32[]{:S(2)}) copy-start(f32[12,768]{1,0:T(8,128)S(1)} %fusion) | copy-start | bytes 110596
  206.3 13.7 %copy-start.22 = (bf16[768,1024]{1,0:T(8,128)(2,1)S(1)}, bf16[768,1024]{1,0:T(8,128)(2,1)}, u32[]{:S(2)}) copy-start(bf16[768,1024]{1,0:T(8,128)(2,1)} %get-tuple-element.77) | copy-start | bytes 4718596
  229.3 10.8 %copy-start.13 = (bf16[768,768]{1,0:T(8,128)(2,1)S(1)}, bf16[768,768]{1,0:T(8,128)(2,1)}, u32[]{:S(2)}) copy-start(bf16[768,768]{1,0:T(8,128)(2,1)} %param.22) | copy-start | bytes 3538948
  229.3 57.7 %all-to-all-start = ((bf16[4,192,768]{2,1,0:T(8,128)(2,1)}), bf16[4,192,768]{2,1,0:T(8,128)(2,1)}, u32[]{:S(2)}, u32[]{:S(2)}) async-start(bf16[4,192,768]{2,1,0:T(8,128)(2,1)} %broadcast_select_fusion), calls=%async_computation | async-start | bytes 2359296 | tf_op jit(solution)/shard_map/all_to_all | solution.py:645
  250.0 15.9 %copy-start.49 = (f32[768]{0:T(1024)}, f32[768]{0:T(1024)S(1)}, u32[]{:S(2)}) copy-start(f32[768]{0:T(1024)S(1)} %reduce_max.29) | copy-start | bytes 9220
  260.4 12.4 %copy-start.20 = (f32[768,2]{1,0:T(8,128)}, f32[768,2]{1,0:T(8,128)S(1)}, u32[]{:S(2)}) copy-start(f32[768,2]{1,0:T(8,128)S(1)} %copy.155) | copy-start | bytes 18436
  286.9 19.5 %all-to-all-start.2 = ((bf16[4,192,768]{2,1,0:T(8,128)(2,1)}), bf16[4,192,768]{2,1,0:T(8,128)(2,1)S(1)}, u32[]{:S(2)}, u32[]{:S(2)}) async-start(bf16[4,192,768]{2,1,0:T(8,128)(2,1)} %bitcast.22), calls=%async_computation.2 | async-start | bytes 2359296 | tf_op jit(solution)/shard_map/all_to_all | solution.py:682
  306.5 10.3 %copy-start.79 = (bf16[2048,768]{1,0:T(8,128)(2,1)S(1)}, bf16[2048,768]{1,0:T(8,128)(2,1)}, u32[]{:S(2)}) copy-start(bf16[2048,768]{1,0:T(8,128)(2,1)} %get-tuple-element.80) | copy-start | bytes 9437188
  324.4 141.4 %all-to-all-start.1 = ((bf16[4,192,768]{2,1,0:T(8,128)(2,1)}), bf16[4,192,768]{2,1,0:T(8,128)(2,1)S(1)}, u32[]{:S(2)}, u32[]{:S(2)}) async-start(bf16[4,192,768]{2,1,0:T(8,128)(2,1)} %bitcast.18), calls=%async_computation.1 | async-start | bytes 2359296 | tf_op jit(solution)/shard_map/all_to_all | solution.py:656
  465.9 37.3 %all-to-all-start.3 = ((bf16[4,192,768]{2,1,0:T(8,128)(2,1)}), bf16[4,192,768]{2,1,0:T(8,128)(2,1)}, u32[]{:S(2)}, u32[]{:S(2)}) async-start(bf16[4,192,768]{2,1,0:T(8,128)(2,1)} %bitcast.24), calls=%async_computation.3 | async-start | bytes 2359296 | tf_op jit(solution)/shard_map/all_to_all | solution.py:701
  476.1 6.4 copy-start.4
  482.4 14.8 %copy-start.36 = (s32[1,768,2]{1,2,0:T(2,128)S(1)}, s32[1,768,2]{1,2,0:T(2,128)}, u32[]{:S(2)}) copy-start(s32[1,768,2]{1,2,0:T(2,128)} %param.20) | copy-start | bytes 18436
  482.4 14.8 %copy-start.38 = (f32[768,2]{0,1:T(2,128)S(1)}, f32[768,2]{0,1:T(2,128)}, u32[]{:S(2)}) copy-start(f32[768,2]{0,1:T(2,128)} %select_reduce_fusion.3) | copy-start | bytes 18436
  537.3 13.4 %copy-start.26 = (bf16[768,768]{0,1:T(8,128)(2,1)S(1)}, bf16[768,768]{0,1:T(8,128)(2,1)}, u32[]{:S(2)}) copy-start(bf16[768,768]{0,1:T(8,128)(2,1)} %convolution_convert_fusion.3) | copy-start | bytes 3538948
  609.9 8.1 %copy-start.14 = (f32[768,12,64]{0,2,1:T(8,128)S(1)}, f32[768,12,64]{0,2,1:T(8,128)}, u32[]{:S(2)}) copy-start(f32[768,12,64]{0,2,1:T(8,128)} %convolution_bitcast_fusion) | copy-start | bytes 7077892
  609.9 8.1 %copy-start.28 = (f32[768,32]{0,1:T(8,128)S(1)}, f32[768,32]{0,1:T(8,128)}, u32[]{:S(2)}) copy-start(f32[768,32]{0,1:T(8,128)} %copy-done.27) | copy-start | bytes 294916
  609.9 8.1 %copy-start.30 = (f32[768,32]{0,1:T(8,128)S(1)}, f32[768,32]{0,1:T(8,128)}, u32[]{:S(2)}) copy-start(f32[768,32]{0,1:T(8,128)} %copy-done.29) | copy-start | bytes 294916
  627.6 5.5 copy-start.16
  627.6 5.5 copy-start.81
  (54 other events, 136.7 us)

commit v2 on v1

--- a/solution.py
+++ b/solution.py
@@ -4,9 +4,14 @@
 from jax import lax
 from jax.experimental import pallas as pl
 from jax.experimental.pallas import tpu as pltpu
+import numpy as np
 from jax.sharding import PartitionSpec as P
 
 HEAD_DIM = 64
+BLOCK = 256
+LONGEST = 384
+epsilon = 1e-06
+
 
 MESH = pl.DeviceIdType.MESH
 
@@ -147,14 +152,243 @@
     return out
 
 
-def gather_kernel(sizes, chunks, qkv_ref, rest_ref, gu_ref, dn_ref, qkv_out, rest_out, gu_out, dn_out,
-                  sends, recvs, mates, local):
+def dot(a, b, ca=1, cb=0):
+    return lax.dot_general(a, b, (((ca,), (cb,)), ((), ())), preferred_element_type=jnp.float32)
+
+
+def turned(columns):
+    eye = lax.broadcasted_iota(jnp.int32, (128, 128), 0) == lax.broadcasted_iota(jnp.int32, (128, 128), 1)
+    return dot(jnp.where(eye, 1.0, 0.0).astype(jnp.bfloat16), columns, 1, 1)
+
+
+def spread(columns):
+    lane = lax.broadcasted_iota(jnp.int32, (columns[0].shape[0], 128), 1)
+    out = jnp.zeros(lane.shape, jnp.float32)
+    for j, c in enumerate(columns):
+        out = jnp.where(lane == j, c, out)
+    return out
+
+
+def swap_halves(v):
+    half = HEAD_DIM // 2
+    lane = lax.broadcasted_iota(jnp.int32, v.shape, 1)
+    return jnp.where(lax.rem(lane, HEAD_DIM) < half, pltpu.roll(v, v.shape[1] - half, 1), pltpu.roll(v, half, 1))
+
+
+def head_masks():
+    lane = lax.broadcasted_iota(jnp.int32, (1, 128), 1)
+    low = jnp.where(lane < HEAD_DIM, 1.0, 0.0).astype(jnp.bfloat16)
+    high = jnp.where(lane < HEAD_DIM, 0.0, 1.0).astype(jnp.bfloat16)
+    return low, high
+
+
+def key_range(i):
+    return max(0, i * BLOCK - LONGEST), (i + 1) * BLOCK
+
+
+class Front:
+    def __init__(self, spot, experts, r):
+        self.spot, self.experts, self.r = spot, experts, r
+        self.length, self.width = r["tokens"].shape
+        self.capacity = 2 * self.length // (experts + 4)
+        self.blocks = self.length // BLOCK
+
+    def ranks(self):
+        r, n = self.r, self.length
+        order = [r["order"][:, k : k + 1] for k in range(2)]
+        route = [r["routes"][:, k : k + 1] for k in range(2)]
+        parts = []
+        for k in range(2):
+            parts += [lax.div(order[k], 256).astype(jnp.float32), lax.rem(order[k], 256).astype(jnp.float32)]
+        parts += [route[k].astype(jnp.float32) for k in range(2)]
+        side = turned(spread(parts).astype(jnp.bfloat16))
+        order_row = [side[2 * k : 2 * k + 1] * 256.0 + side[2 * k + 1 : 2 * k + 2] for k in range(2)]
+        route_row = [side[4 + k : 5 + k] for k in range(2)]
+        out = []
+        for k in range(2):
+            for i in range(self.blocks):
+                rows = slice(i * BLOCK, (i + 1) * BLOCK)
+                mine, kind = order[k][rows].astype(jnp.float32), route[k][rows].astype(jnp.float32)
+                ahead = jnp.zeros((BLOCK, n), jnp.float32)
+                for other in range(2):
+                    ahead += jnp.where(
+                        jnp.logical_and(order_row[other] < mine, route_row[other] == kind), 1.0, 0.0)
+                rank = jnp.sum(ahead, axis=1, keepdims=True)
+                kept = jnp.logical_and(kind < self.experts, rank < self.capacity)
+                r["scal"][pl.ds(i * BLOCK, BLOCK), 8 + k : 9 + k] = jnp.where(
+                    kept, kind * self.capacity + rank, float(self.experts * self.capacity))
+                r["scal"][pl.ds(i * BLOCK, BLOCK), 10 + k : 11 + k] = jnp.where(kept, kind, 255.0)
+                r["scal"][pl.ds(i * BLOCK, BLOCK), 12 + k : 13 + k] = jnp.where(kept, rank, 0.0)
+
+    def flat_rows(self):
+        r = self.r
+        side = turned(r["scal"][...].astype(jnp.bfloat16))
+        for k in range(2):
+            kind, rank = side[10 + k : 11 + k], side[12 + k : 13 + k]
+            r["flat"][k : k + 1] = jnp.where(
+                kind < 255.0, kind * self.capacity + rank, float(self.experts * self.capacity))
+
+    def first_norm(self):
+        r = self.r
+        for i in range(self.blocks):
+            rows = pl.ds(i * BLOCK, BLOCK)
+            x = r["tokens"][rows].astype(jnp.float32)
+            r["scal"][rows, 0:1] = lax.rsqrt(jnp.mean(x * x, axis=1, keepdims=True) + epsilon)
+
+    def masks(self):
+        r, n = self.r, self.length
+        segment = r["segments"][...].astype(jnp.float32)
+        padding = r["padding"][...]
+        column = jnp.transpose(jnp.broadcast_to(segment, (128, n)))[:, 0:1]
+        for i in range(self.blocks):
+            k0, k1 = key_range(i)
+            row = lax.broadcasted_iota(jnp.int32, (BLOCK, k1 - k0), 0) + i * BLOCK
+            col = lax.broadcasted_iota(jnp.int32, (BLOCK, k1 - k0), 1) + k0
+            same = column[i * BLOCK : (i + 1) * BLOCK] == segment[:, k0:k1]
+            real = jnp.broadcast_to(padding[:, k0:k1], row.shape) == 1
+            fine = jnp.logical_and(jnp.logical_and(col <= row, same), jnp.logical_or(real, col == row))
+            r["bias"][pl.ds(i * BLOCK, BLOCK), pl.ds(0, k1 - k0)] = jnp.where(fine, 0.0, -1e30)
+
+    def small_rows(self):
+        r = self.r
+        side = turned(r["rest"][:, pl.ds(self.width, 128)])
+        r["rows"][...] = side[: r["rows"].shape[0]]
+
+    def project(self, i):
+        r, w = self.r, self.width
+        rows = pl.ds(i * BLOCK, BLOCK)
+        x = r["tokens"][rows].astype(jnp.float32)
+        normed = (x * r["scal"][rows, 0:1] * r["rows"][0:1]).astype(jnp.bfloat16)
+        r["normed"][rows] = normed
+        cosine, sine = r["cosine"][rows], r["sine"][rows]
+        for part, name in enumerate(("q", "k")):
+            full = dot(normed, r["qkv"][:, pl.ds(part * w, w)])
+            for pair in range(w // 128):
+                v = full[:, pair * 128 : pair * 128 + 128]
+                v = v * cosine + swap_halves(v) * sine
+                if part == 0:
+                    v = v * HEAD_DIM ** (-0.5)
+                r[name][rows, pl.ds(pair * 128, 128)] = v.astype(jnp.bfloat16)
+        r["v"][rows] = dot(normed, r["qkv"][:, pl.ds(2 * w, w)]).astype(jnp.bfloat16)
+
+    def attend(self, i, pair):
+        r = self.r
+        k0, k1 = key_range(i)
+        rows, keys, lanes = pl.ds(i * BLOCK, BLOCK), pl.ds(k0, k1 - k0), pl.ds(pair * 128, 128)
+        q, k, v = r["q"][rows, lanes], r["k"][keys, lanes], r["v"][keys, lanes]
+        bias = r["bias"][rows, pl.ds(0, k1 - k0)]
+        out = jnp.zeros((BLOCK, 128), jnp.float32)
+        for s, mask in enumerate(head_masks()):
+            scores = dot(q * mask, k, 1, 1) + bias
+            top = jnp.max(scores, axis=1, keepdims=True)
+            e = jnp.exp(scores - top)
+            total = jnp.sum(e, axis=1, keepdims=True)
+            probs = (e * (1.0 / total)).astype(jnp.bfloat16)
+            out = out + dot(probs, v * mask)
+            r["lse"][rows, 2 * pair + s : 2 * pair + s + 1] = top + jnp.log(total)
+        r["attended"][rows, lanes] = out.astype(jnp.bfloat16)
+
+    def gate(self, i):
+        r, w, e = self.r, self.width, self.experts
+        rows = pl.ds(i * BLOCK, BLOCK)
+        h = r["tokens"][rows].astype(jnp.float32) + dot(r["attended"][rows], r["rest"][:, pl.ds(0, w)])
+        r["h"][rows] = h
+        inverse = lax.rsqrt(jnp.mean(h * h, axis=1, keepdims=True) + epsilon)
+        hn = (h * inverse * r["rows"][1:2]).astype(jnp.bfloat16)
+        r["hn"][rows] = hn
+        small = dot(hn, r["rest"][:, pl.ds(w, 128)])
+        lane = lax.broadcasted_iota(jnp.int32, small.shape, 1)
+        prev = r["prev"][rows].astype(jnp.float32)
+        prev_lane = lax.broadcasted_iota(jnp.int32, prev.shape, 1)
+        picked = []
+        for k in range(2):
+            route = r["routes"][rows, k : k + 1]
+            picked.append(jnp.sum(jnp.where(lane == route + 8, small, 0.0), axis=1, keepdims=True)
+                          + jnp.sum(jnp.where(prev_lane == route, prev, 0.0), axis=1, keepdims=True))
+        def soft(a, b):
+            top = jnp.maximum(a, b)
+            ea, eb = jnp.exp(a - top), jnp.exp(b - top)
+            return ea / (ea + eb), eb / (ea + eb)
+        gates = soft(*picked)
+        mix = soft(small[:, 2:3], small[:, 3:4]) + soft(small[:, 4:5], small[:, 5:6])
+        r["scal"][rows, 1:2] = inverse
+        for j, c in enumerate(gates + mix):
+            r["scal"][rows, 2 + j : 3 + j] = c
+        cot = r["cot"][rows].astype(jnp.float32)
+        for k in range(2):
+            r["gcot"][k, rows] = (gates[k] * cot).astype(jnp.bfloat16)
+
+    def slots(self, d):
+        r, n = self.r, self.length
+        e = lax.rem(self.spot.ex + d, self.experts)
+        slot = (lax.broadcasted_iota(jnp.int32, (self.capacity, n), 0) + e * self.capacity).astype(jnp.float32)
+        at = [jnp.where(r["flat"][k : k + 1] == slot, 1.0, 0.0) for k in range(2)]
+        x = dot((at[0] + at[1]).astype(jnp.bfloat16), r["hn"][...]).astype(jnp.bfloat16)
+        g = (dot(at[0].astype(jnp.bfloat16), r["gcot"][0]) + dot(at[1].astype(jnp.bfloat16), r["gcot"][1]))
+        g = g.astype(jnp.bfloat16)
+        if d == 0:
+            r["xin"][self.spot.ex], r["gin"][self.spot.ex] = x, g
+        else:
+            r["sendx"][d - 1], r["sendg"][d - 1] = x, g
+
+
+def expert_device(spot, e):
+    return {"dp": spot.dp, "expert": e}
+
+
+class Exchange:
+    def __init__(self, spot, experts, number, out, into, sems):
+        self.spot, self.experts, self.n, self.out, self.into, self.sems = spot, experts, number, out, into, sems
+
+    def send(self, d):
+        e = lax.rem(self.spot.ex + d, self.experts)
+        pltpu.make_async_remote_copy(
+            src_ref=self.out(d), dst_ref=self.into.at[self.spot.ex], send_sem=self.sems.at[0, self.n, d],
+            recv_sem=self.sems.at[1, self.n, self.spot.ex], device_id=expert_device(self.spot, e),
+            device_id_type=MESH).start()
+
+    def receive(self, d):
+        e = lax.rem(self.spot.ex + d, self.experts)
+        pltpu.make_async_remote_copy(
+            src_ref=self.into.at[e], dst_ref=self.into.at[e], send_sem=self.sems.at[0, self.n, d],
+            recv_sem=self.sems.at[1, self.n, e], device_id=expert_device(self.spot, e),
+            device_id_type=MESH).wait_recv()
+
+    def drain(self, d):
+        pltpu.make_async_remote_copy(
+            src_ref=self.out(d), dst_ref=self.into.at[self.spot.ex], send_sem=self.sems.at[0, self.n, d],
+            recv_sem=self.sems.at[1, self.n, self.spot.ex], device_id=expert_device(self.spot, self.spot.ex),
+            device_id_type=MESH).wait_send()
+
+
+def woven(work, events):
+    done = 0
+    for j, piece in enumerate(work):
+        piece()
+        upto = (j + 1) * len(events) // len(work)
+        for event in events[done:upto]:
+            event()
+        done = upto
+
+
+FRONT_INS = ("tokens", "prev", "segments", "padding", "routes", "order", "cot", "cosine", "sine",
+             "qkv_own", "rest_own", "gu_own", "dn_own")
+FRONT_OUTS = ("gu", "dn", "qkv", "rest", "q", "k", "v", "normed", "attended", "hn", "h", "lse", "scal", "rows", "flat",
+              "xin", "gin")
+FRONT_SCRATCH = ("bias", "gcot", "sendx", "sendg", "sends", "recvs", "mates", "local", "trade")
+
+
+def front_kernel(sizes, experts, chunks, *refs):
+    r = dict(zip(FRONT_INS + FRONT_OUTS + FRONT_SCRATCH, refs))
     spot = Spot(sizes)
-    enter(spot, line_neighbours(spot) + [(None, spot.device(core=1 - spot.core))])
-    rows = qkv_ref.shape[0]
-    rows_d, width = dn_ref.shape
+    front = Front(spot, experts, r)
+    enter(spot, line_neighbours(spot)
+          + [(None, expert_device(spot, lax.rem(spot.ex + d, experts))) for d in range(1, experts)])
+    rows = r["qkv_own"].shape[0]
+    rows_d = r["dn_own"].shape[0]
     first, later = [], []
-    for src, out in ((qkv_ref, qkv_out), (rest_ref, rest_out)):
+    for name in ("qkv", "rest"):
+        src, out = r[name + "_own"], r[name]
         part = src.shape[1] // 2
         def half(o, core, out=out, part=part):
             return out.at[pl.ds(pl.multiple_of(o * rows, 8), rows), pl.ds(pl.multiple_of(core * part, 128), part)]
@@ -162,53 +396,99 @@
                       lambda o, half=half: half(o, spot.core), True, lambda o, half=half: half(o, 1 - spot.core)))
     part = rows_d // 2
     for p, zf in ((0, True), (1, False)):
-        later.append((dn_ref.at[pl.ds(p * part, part)],
-                      lambda o, p=p: dn_out.at[pl.ds(pl.multiple_of(o * rows_d + p * part, 8), part)], zf, None))
-    wide = gu_ref.shape[1] // chunks
+        later.append((r["dn_own"].at[pl.ds(p * part, part)],
+                      lambda o, p=p: r["dn"].at[pl.ds(pl.multiple_of(o * rows_d + p * part, 8), part)], zf, None))
+    wide = r["gu_own"].shape[1] // chunks
     for c in range(chunks):
-        later.append((gu_ref.at[:, pl.ds(c * wide, wide)],
-                      lambda o, c=c: gu_out.at[pl.ds(pl.multiple_of(o * rows, 8), rows), pl.ds(c * wide, wide)], True, None))
-    keeps = []
-    for n, (own, view, zf, other) in enumerate(first + later):
-        keep = pltpu.make_async_copy(own, view(spot.dp), local.at[n])
+        later.append((r["gu_own"].at[:, pl.ds(c * wide, wide)],
+                      lambda o, c=c: r["gu"].at[pl.ds(pl.multiple_of(o * rows, 8), rows), pl.ds(c * wide, wide)], True, None))
+    floods = [Flood(spot, n, own, view, r["sends"], r["recvs"], zf, None if other is None else r["mates"])
+              for n, (own, view, zf, other) in enumerate(first + later)]
+    levels = [f.levels() for f in floods]
+    dense, experts_levels = levels[:2], levels[2:]
+    keeps = [pltpu.make_async_copy(own, view(spot.dp), r["local"].at[n])
+             for n, (own, view, zf, other) in enumerate(first + later)]
+    for ls in dense:
+        for step in ls[0]:
+            step()
+    for keep in keeps:
         keep.start()
-        keeps.append(keep)
-    number = 0
-    drains = []
-    for group in (first, later):
-        floods = []
-        for own, view, zf, other in group:
-            floods.append(Flood(spot, number, own, view, sends, recvs, zf, None if other is None else mates))
-            number += 1
-        levels = [f.levels() for f in floods]
-        for level in range(max(map(len, levels))):
-            for ls in levels:
-                if level < len(ls):
-                    for step in ls[level]:
-                        step()
-        for f, (own, view, zf, other) in zip(floods, group):
-            if other is not None:
-                f.mates(other)
-            drains += f.drains
-    for drain in drains:
-        drain()
-    for keep in keeps:
+    front.ranks()
+    front.flat_rows()
+    front.first_norm()
+    front.masks()
+    depth = max(map(len, levels))
+    events = [step for level in range(depth) for ls in experts_levels if level < len(ls) for step in ls[level]]
+    n_start = sum(len(ls[0]) for ls in experts_levels)
+    for level in range(1, depth):
+        if level == depth - 1:
+            for event in events[:n_start]:
+                event()
+        for ls in dense:
+            if level < len(ls):
+                for step in ls[level]:
+                    step()
+    for keep in keeps[:2]:
         keep.wait()
-
-
-def gather_weights(sizes, qkv, rest, gu, dn, chunks=4):
+    for f, (own, view, zf, other) in zip(floods, first):
+        f.mates(other)
+    trades = [Exchange(spot, experts, 0, lambda d: r["sendx"].at[d - 1], r["xin"], r["trade"]),
+              Exchange(spot, experts, 1, lambda d: r["sendg"].at[d - 1], r["gin"], r["trade"])]
+    work = [front.small_rows]
+    work += [functools.partial(front.project, i) for i in range(front.blocks)]
+    for pair in range(front.width // 128):
+        work += [functools.partial(front.attend, i, pair) for i in range(front.blocks)]
+    work += [functools.partial(front.gate, i) for i in range(front.blocks)]
+    def dispatch(d):
+        front.slots(d)
+        if d:
+            for t in trades:
+                t.send(d)
+    work += [functools.partial(dispatch, d) for d in list(range(1, experts)) + [0]]
+    rest = events[n_start:]
+    cut = len(rest) * 3 // 5
+    woven(work, rest[:cut])
+    for event in rest[cut:]:
+        event()
+    for d in range(1, experts):
+        for t in trades:
+            t.receive(d)
+            t.drain(d)
+    for f in floods:
+        for drain in f.drains:
+            drain()
+    for keep in keeps[2:]:
+        keep.wait()
+
+
+def run_front(sizes, experts, ins, chunks=4):
+    tokens, qkv, rest, gu, dn = ins[0], ins[9], ins[10], ins[11], ins[12]
+    length, width = tokens.shape
     n_dp = sizes[0] * sizes[1]
+    capacity = 2 * length // (experts + 4)
+    bf, f4 = jnp.bfloat16, jnp.float32
+    S = jax.ShapeDtypeStruct
+    token = S((length, width), bf)
+    outs = [S((a.shape[0] * n_dp, a.shape[1]), bf) for a in (gu, dn, qkv, rest)]
+    outs += [token] * 6 + [S((length, width), f4), S((length, 128), f4), S((length, 128), f4), S((16, width), f4),
+                           S((8, length), f4)]
+    outs += [S((experts, capacity, width), bf)] * 2
     items = 4 + chunks
-    arrays = (qkv, rest, gu, dn)
+    dma = pltpu.SemaphoreType.DMA
+    vmem = pl.BlockSpec(memory_space=pltpu.VMEM)
+    hbm = pl.BlockSpec(memory_space=pl.ANY)
     return pl.pallas_call(
-        functools.partial(gather_kernel, sizes, chunks),
-        out_shape=tuple(jax.ShapeDtypeStruct((a.shape[0] * n_dp, a.shape[1]), a.dtype) for a in arrays),
-        in_specs=[pl.BlockSpec(memory_space=pltpu.VMEM)] * 4,
-        out_specs=(pl.BlockSpec(memory_space=pl.ANY),) * 4,
-        scratch_shapes=[pltpu.SemaphoreType.DMA((5, items, n_dp)), pltpu.SemaphoreType.DMA((items, n_dp)),
-                        pltpu.SemaphoreType.DMA((2, n_dp)), pltpu.SemaphoreType.DMA((items,))],
-        compiler_params=pltpu.CompilerParams(collective_id=1, has_side_effects=True),
-    )(*arrays)
+        functools.partial(front_kernel, sizes, experts, chunks),
+        out_shape=tuple(outs),
+        in_specs=[vmem] * 13,
+        out_specs=(hbm, hbm) + (vmem,) * (len(outs) - 2),
+        scratch_shapes=[
+            pltpu.VMEM((length, BLOCK + LONGEST), f4), pltpu.VMEM((2, length, width), bf),
+            pltpu.VMEM((experts - 1, capacity, width), bf), pltpu.VMEM((experts - 1, capacity, width), bf),
+            dma((5, items, n_dp)), dma((items, n_dp)), dma((2, n_dp)), dma((items,)), dma((2, 2, experts))],
+        compiler_params=pltpu.CompilerParams(collective_id=1, has_side_effects=True, vmem_limit_bytes=62 << 20),
+        name="front",
+    )(*ins)
 
 
 def add_into(view, more):
@@ -484,8 +764,14 @@
         compiler_params=pltpu.CompilerParams(collective_id=3, has_side_effects=True, vmem_limit_bytes=60 << 20),
     )(*arrays)
 
-
-epsilon = 1e-06
+def pair_tables(length):
+    half = HEAD_DIM // 2
+    inverse = np.float32(10000.0) ** (-(np.arange(half, dtype=np.float32) / np.float32(half)))
+    angles = (np.arange(length, dtype=np.float32)[:, None] * inverse[None]).astype(np.float64)
+    cosine, sine = np.cos(angles).astype(np.float32), np.sin(angles).astype(np.float32)
+    return jnp.asarray(np.tile(cosine, (1, 4))), jnp.asarray(np.tile(np.concatenate([-sine, sine], 1), (1, 2)))
+
+
 highest = lax.Precision.HIGHEST
 
 
@@ -564,62 +850,37 @@
     block_rows = min(length, 768)
     starts = jnp.arange(length // block_rows) * block_rows
     query_scale = HEAD_DIM ** (-0.5)
-    rows = qkv_weight.shape[0]
     small = jnp.concatenate(
         [attn_gain[:, None], ffn_gain[:, None], mix_weight, const_weight, router_weight], axis=1
     )
     rest = jnp.concatenate([out_weight, jnp.pad(small, ((0, 0), (0, 256 - small.shape[1])))], axis=1)
-    qkv_full, rest_full, gate_up_local, down_local = gather_weights(
-        sizes, qkv_weight, rest, gate_up_weight[0], down_weight[0]
-    )
+    cos_table, sin_table = pair_tables(length)
+    (gate_up_local, down_local, qkv_full, rest_full, qf, kf, vf, normed, attended, ffn_normed, hidden_state, lse, scal,
+     rows, flat, xin, gin) = run_front(
+        sizes, real_count,
+        (tokens, prev_logits, segment_ids, pad_mask, routes[0], slot_order.reshape(length, 2), cotangent,
+         cos_table, sin_table, qkv_weight, rest, gate_up_weight[0], down_weight[0]))
     out_full = rest_full[:, :width]
     small_full = rest_full[:, width:]
     gain_one, gain_two = small_full[:, 0], small_full[:, 1]
     mix_full, const_full = small_full[:, 2:6], small_full[:, 6:8]
     router_full = small_full[:, 8 : 8 + router_weight.shape[1]]
     inputs = tokens.astype(jnp.float32)
-    inverse_one = lax.rsqrt(jnp.mean(inputs * inputs, axis=-1, keepdims=True) + epsilon)
-    normed = (inputs * inverse_one * gain_one.astype(jnp.float32)).astype(jnp.bfloat16)
-    qkv = jnp.dot(normed, qkv_full, preferred_element_type=jnp.float32).reshape(
-        length, 3, heads, HEAD_DIM
-    )
+    inverse_one = scal[:, 0:1]
     cosine, sine = rope_tables(length, HEAD_DIM // 2)
-    queries = (rotate(qkv[:, 0], cosine, sine) * query_scale).astype(jnp.bfloat16)
-    key_rows = rotate(qkv[:, 1], cosine, sine).astype(jnp.bfloat16)
-    value_rows = qkv[:, 2].astype(jnp.bfloat16)
+    queries, key_rows, value_rows = (t.reshape(length, heads, HEAD_DIM) for t in (qf, kf, vf))
+    log_totals = lse[:, :heads].T[None]
     segments = segment_ids[0]
     padding = pad_mask[0]
 
-    def forward_block(block_start):
-        scores = masked_scores(queries, key_rows, block_start, segments, padding)
-        highest_score = jnp.max(scores, axis=-1, keepdims=True)
-        exponent = jnp.exp(scores - highest_score)
-        denominator = jnp.sum(exponent, axis=-1, keepdims=True)
-        probabilities = (exponent / denominator).astype(jnp.bfloat16)
-        attended_block = jnp.einsum(
-            "hqk,khd->qhd", probabilities, value_rows, preferred_element_type=jnp.float32
-        )
-        return (attended_block.astype(jnp.bfloat16), (highest_score + jnp.log(denominator))[..., 0])
-
-    attended_blocks, log_totals = lax.map(forward_block, starts)
-    attended = attended_blocks.reshape(length, width)
-    hidden_state = inputs + jnp.dot(attended, out_full, preferred_element_type=jnp.float32)
-    inverse_two = lax.rsqrt(jnp.mean(hidden_state * hidden_state, axis=-1, keepdims=True) + epsilon)
     gain_float = gain_two.astype(jnp.float32)
-    ffn_normed = (hidden_state * inverse_two * gain_float).astype(jnp.bfloat16)
+    inverse_two = scal[:, 1:2]
     ffn_float = ffn_normed.astype(jnp.float32)
-    logits = jnp.dot(
-        ffn_normed, router_full, preferred_element_type=jnp.float32
-    ) + prev_logits.astype(jnp.float32)
     route_rows = routes[0]
     route_ids = jnp.arange(real_count + 4)
     chosen = (route_rows[:, :, None] == route_ids[None, None, :]).astype(jnp.float32)
-    picked = jnp.sum(chosen * logits[:, None, :], axis=-1)
-    gate_weights = jax.nn.softmax(picked, axis=-1)
-    mix = jax.nn.softmax(
-        jnp.dot(ffn_normed, mix_full, preferred_element_type=jnp.float32).reshape(length, 2, 2),
-        axis=-1,
-    )
+    gate_weights = scal[:, 2:4]
+    mix = scal[:, 4:8].reshape(length, 2, 2)
     is_copy = (route_rows == real_count + 1).astype(jnp.float32)
     const_ids = real_count + 2 + jnp.arange(2)
     is_const = (route_rows[:, :, None] == const_ids[None, None, :]).astype(jnp.float32)
@@ -627,23 +888,9 @@
     copy_coef = jnp.sum(gate_weights * route_copy, axis=-1)
     const_select = jnp.sum(gate_weights[:, :, None] * is_const, axis=1)
     const_coef = const_select * mix[:, :, 1]
-    pair_expert = route_rows.reshape(2 * length)
-    order = slot_order[0]
-    expert_range = jnp.arange(real_count)
-    onehot = (pair_expert[:, None] == expert_range[None, :]).astype(jnp.int32)
-    placed = jnp.zeros_like(onehot).at[order].set(onehot)
-    before = jnp.cumsum(placed, axis=0) - placed
-    slot_rank = jnp.sum(before[order] * onehot, axis=1)
-    is_kept = (pair_expert < real_count) & (slot_rank < capacity)
-    flat_slot = jnp.where(is_kept, pair_expert * capacity + slot_rank, real_count * capacity)
-    pair_token = jnp.arange(2 * length) // 2
-    slot_token = jnp.zeros(real_count * capacity + 1, jnp.int32).at[flat_slot].set(pair_token)[:-1]
-    slot_valid = jnp.zeros(real_count * capacity + 1, jnp.int32).at[flat_slot].set(1)[:-1]
-    send_rows = jnp.where(
-        slot_valid[:, None] > 0, ffn_normed[slot_token], jnp.zeros((), jnp.bfloat16)
-    ).reshape(real_count, capacity, width)
-    received = lax.all_to_all(send_rows, "expert", split_axis=0, concat_axis=0, tiled=True)
-    expert_input = received.reshape(-1, width)
+    flat_slot = scal[:, 8:10].astype(jnp.int32).reshape(2 * length)
+    received = xin
+    expert_input = xin.reshape(-1, width)
     projected = jnp.dot(expert_input, gate_up_local, preferred_element_type=jnp.float32)
     gate_part = projected[:, :hidden_units]
     up_part = projected[:, hidden_units:]
@@ -668,20 +915,7 @@
     qkv_back, out_back, router_back, mix_back = qkv_full, out_full, router_full, mix_full
     gate_up_back, down_back = gate_up_local, down_local
     out_grad = cotangent.astype(jnp.float32)
-    pair_grad = (
-        (gate_weights[:, :, None] * out_grad[:, None, :])
-        .astype(jnp.bfloat16)
-        .reshape(2 * length, width)
-    )
-    slot_grad = (
-        jnp.zeros((real_count * capacity + 1, width), jnp.bfloat16)
-        .at[flat_slot]
-        .set(pair_grad)[:-1]
-    )
-    slot_grad = slot_grad.reshape(real_count, capacity, width)
-    expert_out_grad = lax.all_to_all(
-        slot_grad, "expert", split_axis=0, concat_axis=0, tiled=True
-    ).reshape(-1, width)
+    expert_out_grad = gin.reshape(-1, width)
     activated_grad = jnp.einsum(
         "rd,fd->rf", expert_out_grad, down_back, preferred_element_type=jnp.float32
     )

time: 731 us -> 609 us (0.83)
  local copies, waits for them, and re-layouts: 114 us -> 74.3 us
  other arithmetic: 112 us -> 73.2 us
  matrix products: 172 us -> 137 us
  Pallas kernels: 299 us -> 308 us
    dot_general x5 -> x0, matrix products: 23.4 us -> none  [the longest x1 13.7 us: forward_block(): jnp.einsum('hqk,khd->qhd', probabilities, value_rows, preferred_element_t...]
    reduce_sum x6 -> x0, other arithmetic: 15.7 us -> none  [the longest x1 12.1 us: forward_block(): denominator = jnp.sum(exponent, axis=-1, keepdims=True)]
    scatter x2 -> x0, other arithmetic: 14 us -> none  [the longest x1 8.67 us: per_device(): slot_grad = jnp.zeros((real_count * capacity + 1, width), jnp.bfloat16).a...]
    mul x5 -> x1, local copies, waits for them, and re-layouts: 14 us -> 0.15 us  [per_device(): gate_weights * (gate_grads - jnp.sum(gate_weights * gate_grads, axis=-1,...]
    scatter x2 -> x0, local copies, waits for them, and re-layouts: 12.5 us -> none  [the longest x1 6.34 us: per_device(): jnp.zeros(real_count * capacity + 1, jnp.int32).at[flat_slot]]
    all_to_all x2 -> x0, starting transfers between devices: 8.59 us -> none  [the longest x1 4.89 us: per_device(): lax.all_to_all(send_rows, 'expert', split_axis=0, concat_axis=0, tiled=True)]
    unnamed x176 -> x132, local copies, waits for them, and re-layouts: 19.6 us -> 14.4 us
  transfers between devices with their start and end apart: 4 -> 2, of which waited for: 1 -> 0; matrix products, arithmetic and copies ran while one was open for 16% -> 18% of each run, Pallas kernels for 16% -> 19%
where the time goes in v2:
time: 609 us; the launch traced here: 603 us
  Pallas kernels  308 us (51%)
  matrix products  137 us (22%)
  local copies, waits for them, and re-layouts  74.3 us (12%)
  other arithmetic  73.2 us (12%)
  starting transfers between devices  9.31 us (2%)
    pallas_call x1, Pallas kernels, run_front(): pl.pallas_call(functools.partial(front_kernel, sizes, experts, chunks), o...  138 us
    pallas_call x1, Pallas kernels, reduce_experts(): pl.pallas_call(functools.partial(reduce_kernel, sizes, chunks), out_shape...  117 us
    pallas_call x1, Pallas kernels, reduce_dense(): pl.pallas_call(functools.partial(dense_kernel, sizes, tuple(cuts)), out_s...  52.1 us
    dot_general x1, matrix products, backward_block(): jnp.einsum('qhd,khd->hqk', attended_grad, value_rows, preferred_element_t...  23.6 us
    convert_element_type x1, other arithmetic, backward_block(): score_grad = (probs_full * (prob_grad - row_dot)).astype(jnp.bfloat16)  23.4 us
    unnamed x132, local copies, waits for them, and re-layouts  14.4 us
    reduce_sum x1, other arithmetic, per_device(): grad_dot_pairs = jnp.sum(out_grad[:, None, :] * pair_rows, axis=-1)  13.6 us
    dot_general x1, matrix products, backward_block(): jnp.einsum('hqk,qhd->khd', probs_low, attended_grad, preferred_element_ty...  13.6 us
  transfers between devices with their start and end apart: 2, of which 0 were waited for; matrix products, arithmetic and copies ran while one was open for 18% of the time, Pallas kernels for 19%

profile of v2, /device:TPU:0, one launch (start us, length us, event | category | flops | bytes accessed | tf_op | source)
XLA Modules:
  0.0 603.1 jit_solution(8702966804848040941)
XLA Ops:
  8.7 138.3 %front.1 = (bf16[768,4096]{1,0:T(8,128)(2,1)}, bf16[2048,768]{1,0:T(8,128)(2,1)}, bf16[768,2304]{1,0:T(8,128)(2,1)}, bf16[768,1024]{1,0:T(8,128)(2,1)}, bf16[768...) custom-call(bf16[768,768]{1,0:T(8,128)(2,1)} %refs_0_.1, ...), custom_call_target="tpu_custom_call" | custom-call | tf_op jit(solution)/shard_map/front/pallas_call | solution.py:480
  147.0 7.6 %fusion.53 = f32[768,4096]{1,0:T(8,128)S(1)} fusion(bf16[768,768]{1,0:T(8,128)(2,1)} %bitcast.119, bf16[768,4096]{1,0:T(8,128)(2,1)} %get-tuple-element.67), kind=kOutput, calls=%fused_computation.126 | convolution fusion | flops 4831838208 | bytes 20054016 | tf_op jit(solution)/shard_map/dot_general | solution.py:894
  154.7 6.9 %multiply_convert_fusion.2 = (bf16[768,2048]{1,0:T(8,128)(2,1)}, bf16[768,2048]{1,0:T(8,128)(2,1)}, bf16[768,2048]{1,0:T(8,128)(2,1)S(1)}) fusion(f32[768,4096]{1,0:T(8,128)S(1)} %fusion.53, bf16[768,768]{1,0:T(8,128)(2,1)S(1)} %bitcast.117, bf16[2048,768]{1,0:T(8,128)(2,1)S(1)} %copy-done.51), kind=kOutput, calls=%fused_computation.11 | convolution fusion | flops 2441084928 | bytes 26345472 | tf_op jit(solution)/shard_map/rd,fd->rf/dot_general | solution.py:919
  161.6 3.6 convolution_convert_fusion.5
  165.2 4.6 all-to-all-start
  176.4 10.0 %fusion.21 = bf16[768,768]{1,0:T(8,128)(2,1)} fusion(bf16[768,4096]{1,0:T(8,128)(2,1)} %get-tuple-element.67, bf16[768,2048]{1,0:T(8,128)(2,1)} %get-tuple-element.162, bf16[768,2048]{1,0:T(8,128)(2,1)} %get-tuple-element.161), kind=kOutput, calls=%fused_computation.50 | convolution fusion | flops 4845010944 | bytes 13762560 | tf_op jit(solution)/shard_map/rf,df->rd/dot_general | solution.py:932
  186.5 7.3 %convolution_convert_fusion = bf16[768,4096]{1,0:T(8,128)(2,1)} fusion(bf16[768,768]{1,0:T(8,128)(2,1)S(1)} %bitcast.120, bf16[768,2048]{1,0:T(8,128)(2,1)S(1)} %copy-done.60, bf16[768,2048]{1,0:T(8,128)(2,1)S(1)} %copy-done.59), kind=kOutput, calls=%fused_computation.8 | convolution fusion | flops 4847566848 | bytes 13762560 | tf_op jit(solution)/shard_map/rd,rf->df/dot_general | solution.py:929
  193.8 4.1 convolution_convert_fusion.2
  198.3 2.2 convert_reduce_fusion
  224.9 2.8 copy.141
  227.8 2.4 copy.143
  230.1 117.4 %shard_map.266 = (f32[96,4096]{1,0:T(8,128)}, f32[256,768]{1,0:T(8,128)}) custom-call(bf16[8,96,4096]{2,1,0:T(8,128)(2,1)} %bitcast.98, bf16[8,256,768]{2,1,0:T(8,128)(2,1)} %bitcast.106), custom_call_target="tpu_custom_call" | custom-call | tf_op jit(solution)/shard_map/pallas_call | solution.py:641
  350.0 12.6 %fusion.54 = f32[12,768,768]{1,2,0:T(8,128)} fusion(bf16[768,12,64]{0,2,1:T(8,128)(2,1)} %bitcast.95, bf16[768,12,64]{0,2,1:T(8,128)(2,1)S(1)} %bitcast.93), kind=kOutput, calls=%fused_computation.127 | convolution fusion | flops 905969664 | bytes 30670848 | tf_op jit(solution)/shard_map/while/body/eval_jaxpr/qhd,khd->hqk/dot_general | solution.py:805
  362.7 4.7 all-to-all-start.1
  368.7 5.7 gather_fusion
  374.5 6.2 %reshape.356 = f32[768,2,768]{2,1,0:T(2,128)} reshape(bf16[1536,768]{1,0:T(8,128)(2,1)} %gather_fusion) | data formatting | bytes 7077888 | tf_op jit(solution)/shard_map/convert_element_type | solution.py:907
  380.7 13.6 %multiply_reduce_fusion.1 = (f32[768,2]{1,0:T(8,128)S(1)}, f32[768,768]{1,0:T(8,128)}) fusion(f32[768,2,768]{2,1,0:T(2,128)} %reshape.356, f32[768,768]{1,0:T(8,128)} %convert_element_type.158, f32[768,2]{1,0:T(8,128)S(1)} %get-tuple-element.168), kind=kLoop, calls=%fused_computation.15 | loop fusion | flops 4127232 | bytes 9449472 | tf_op jit(solution)/shard_map/reduce_sum | solution.py:949
  395.8 3.0 fusion.35
  400.2 5.7 gather_fusion.1
  405.9 6.3 %reshape.358 = f32[768,2,768]{2,1,0:T(2,128)} reshape(bf16[1536,768]{1,0:T(8,128)(2,1)} %gather_fusion.1) | data formatting | bytes 7077888 | tf_op jit(solution)/shard_map/convert_element_type | solution.py:942
  412.3 9.5 %reduce_sum.151 = f32[768,768]{1,0:T(8,128)} reduce(f32[768,2,768]{2,1,0:T(2,128)} %reshape.358, f32[]{:T(128)} %constant.50.clone.1), dimensions={1}, to_apply=%region_4.5 | reduce | flops 589824 | bytes 7077892 | tf_op jit(solution)/shard_map/reduce_sum | solution.py:941
  421.7 4.4 multiply_reduce_fusion.3
  429.0 13.6 %fusion.25 = bf16[768,1,12,64]{0,3,2,1:T(8,128)(2,1)} fusion(bf16[768,12,64]{0,2,1:T(8,128)(2,1)S(1)} %bitcast.101, f32[12,768,768]{1,2,0:T(8,128)} %fusion.54, f32[12,768]{1,0:T(8,128)S(1)} %copy-done.19, pred[768,768]{0,1:T(8,128)(4,1)S(1)} %copy-done.12), kind=kOutput, calls=%fused_computation.55 | convolution fusion | flops 927793152 | bytes 31297536 | tf_op jit(solution)/shard_map/while/body/eval_jaxpr/hqk,qhd->khd/dot_general | solution.py:1013
  442.6 23.6 %multiply_reduce_fusion = (f32[12,768]{1,0:T(8,128)}, f32[12,768,768]{1,2,0:T(8,128)}) fusion(f32[12,768,768]{1,2,0:T(8,128)} %fusion.54, f32[12,768]{1,0:T(8,128)S(1)} %copy-done.19, pred[768,768]{0,1:T(8,128)(4,1)S(1)} %copy-done.12, bf16[768,12,64]{0,2,1:T(8,128)(2,1)S(1)} %bitcast.102, bf16[768,12,64]{0,2,1:T(8,128)(2,1)S(1)} %bitcast.97), kind=kOutput, calls=%fused_computation.3 | convolution fusion | flops 934272000 | bytes 59645952 | tf_op jit(solution)/shard_map/while/body/eval_jaxpr/qhd,khd->hqk/dot_general | solution.py:1002
  466.2 23.4 %multiply_convert_fusion = bf16[12,768,768]{1,2,0:T(8,128)(2,1)} fusion(f32[12,768,768]{1,2,0:T(8,128)} %get-tuple-element.178, f32[12,768,768]{1,2,0:T(8,128)} %fusion.54, f32[12,768]{1,0:T(8,128)} %get-tuple-element.177, f32[12,768]{1,0:T(8,128)} %copy.142, pred[768,768]{0,1:T(8,128)(4,1)} %fusion.19), kind=kLoop, calls=%fused_computation.2 | loop fusion | flops 35389440 | bytes 71442432 | tf_op jit(solution)/shard_map/while/body/eval_jaxpr/convert_element_type | solution.py:1006
  489.6 9.5 %convolution_bitcast_fusion = f32[768,12,64]{0,2,1:T(8,128)S(1)} fusion(bf16[768,12,64]{0,2,1:T(8,128)(2,1)S(1)} %bitcast.96, bf16[12,768,768]{1,2,0:T(8,128)(2,1)} %multiply_convert_fusion), kind=kOutput, calls=%fused_computation.48 | convolution fusion | flops 905969664 | bytes 17694720 | tf_op jit(solution)/shard_map/while/body/eval_jaxpr/hqk,qhd->khd/dot_general | solution.py:1010
  499.1 7.8 %multiply_bitcast_fusion = f32[768,12,64]{0,2,1:T(8,128)S(1)} fusion(bf16[768,12,64]{0,2,1:T(8,128)(2,1)S(1)} %bitcast.94, bf16[12,768,768]{1,2,0:T(8,128)(2,1)} %multiply_convert_fusion), kind=kOutput, calls=%fused_computation.39 | convolution fusion | flops 906559488 | bytes 17694720 | tf_op jit(solution)/shard_map/while/body/eval_jaxpr/hqk,khd->qhd/dot_general | solution.py:1007
  513.0 4.7 convolution_convert_fusion.1
  517.8 5.3 fusion.17
  529.5 52.1 %shard_map.265 = (f32[96,2304]{1,0:T(8,128)}, f32[96,1024]{1,0:T(8,128)}) custom-call(bf16[8,96,2304]{2,1,0:T(8,128)(2,1)} %bitcast.103, bf16[8,96,1024]{2,1,0:T(8,128)(2,1)} %pad_maximum_fusion.4.refs_1_), custom_call_target="tpu_custom_call" | custom-call | tf_op jit(solution)/shard_map/pallas_call | solution.py:758
  587.6 4.4 fusion.8
  594.0 5.0 fusion.14
  (203 shorter events, 73.1 us)
Async XLA Ops:
  147.0 7.7 %copy-start.51 = (bf16[2048,768]{1,0:T(8,128)(2,1)S(1)}, bf16[2048,768]{1,0:T(8,128)(2,1)}, u32[]{:S(2)}) copy-start(bf16[2048,768]{1,0:T(8,128)(2,1)} %get-tuple-element.68) | copy-start | bytes 9437188
  147.0 7.7 %copy-start.54 = (bf16[4,192,768]{2,1,0:T(8,128)(2,1)S(1)}, bf16[4,192,768]{2,1,0:T(8,128)(2,1)}, u32[]{:S(2)}) copy-start(bf16[4,192,768]{2,1,0:T(8,128)(2,1)} %get-tuple-element.71) | copy-start | bytes 3538948
  165.2 6.9 %copy-start.13 = (s32[1,768,2]{2,1,0:T(8,128)S(1)}, s32[1,768,2]{2,1,0:T(8,128)}, u32[]{:S(2)}) copy-start(s32[1,768,2]{2,1,0:T(8,128)} %copy.125) | copy-start | bytes 18436
  165.2 7.6 %copy-start = (bf16[768,768]{1,0:T(8,128)(2,1)S(1)}, bf16[768,768]{1,0:T(8,128)(2,1)}, u32[]{:S(2)}) copy-start(bf16[768,768]{1,0:T(8,128)(2,1)} %refs_6_.1) | copy-start | bytes 3538948
  165.2 197.4 %all-to-all-start = ((bf16[4,192,768]{2,1,0:T(8,128)(2,1)}), bf16[4,192,768]{2,1,0:T(8,128)(2,1)}, u32[]{:S(2)}, u32[]{:S(2)}) async-start(bf16[4,192,768]{2,1,0:T(8,128)(2,1)} %bitcast.6), calls=%async_computation | async-start | bytes 2359296 | tf_op jit(solution)/shard_map/all_to_all | solution.py:903
  174.8 11.6 %copy-start.31 = (f32[768,2,2]{0,2,1:T(2,128)}, f32[768,2,2]{0,2,1:T(2,128)S(1)}, u32[]{:S(2)}) copy-start(f32[768,2,2]{0,2,1:T(2,128)S(1)} %reshape.345) | copy-start | bytes 36868
  176.4 10.0 %copy-start.56 = (bf16[4,192,768]{2,1,0:T(8,128)(2,1)S(1)}, bf16[4,192,768]{2,1,0:T(8,128)(2,1)}, u32[]{:S(2)}) copy-start(bf16[4,192,768]{2,1,0:T(8,128)(2,1)} %get-tuple-element.66) | copy-start | bytes 3538948
  176.4 10.0 %copy-start.59 = (bf16[768,2048]{1,0:T(8,128)(2,1)S(1)}, bf16[768,2048]{1,0:T(8,128)(2,1)}, u32[]{:S(2)}) copy-start(bf16[768,2048]{1,0:T(8,128)(2,1)} %get-tuple-element.161) | copy-start | bytes 9437188
  176.4 10.0 %copy-start.60 = (bf16[768,2048]{1,0:T(8,128)(2,1)S(1)}, bf16[768,2048]{1,0:T(8,128)(2,1)}, u32[]{:S(2)}) copy-start(bf16[768,2048]{1,0:T(8,128)(2,1)} %get-tuple-element.162) | copy-start | bytes 9437188
  186.4 7.3 %copy-start.55 = (bf16[4,192,768]{2,1,0:T(8,128)(2,1)S(1)}, bf16[4,192,768]{2,1,0:T(8,128)(2,1)}, u32[]{:S(2)}) copy-start(bf16[4,192,768]{2,1,0:T(8,128)(2,1)} %get-tuple-element.71) | copy-start | bytes 3538948
  186.5 7.3 %copy-start.58 = (bf16[768,2048]{1,0:T(8,128)(2,1)S(1)}, bf16[768,2048]{1,0:T(8,128)(2,1)}, u32[]{:S(2)}) copy-start(bf16[768,2048]{1,0:T(8,128)(2,1)} %copy-done.57) | copy-start | bytes 9437188
  198.3 15.3 %copy-start.37 = (f32[768]{0:T(1024)}, f32[768]{0:T(1024)S(1)}, u32[]{:S(2)}) copy-start(f32[768]{0:T(1024)S(1)} %fusion.9) | copy-start | bytes 9220
  211.1 12.3 %copy-start.29 = (f32[768,2]{0,1:T(2,128)}, f32[768,2]{0,1:T(2,128)S(1)}, u32[]{:S(2)}) copy-start(f32[768,2]{0,1:T(2,128)S(1)} %get-tuple-element.158) | copy-start | bytes 18436
  224.9 125.1 %copy-start.6 = (bf16[768,768]{0,1:T(8,128)(2,1)}, bf16[768,768]{0,1:T(8,128)(2,1)S(1)}, u32[]{:S(2)}) copy-start(bf16[768,768]{0,1:T(8,128)(2,1)S(1)} %copy.140) | copy-start | bytes 3538948
  230.1 117.5 %copy-start.43 = (f32[768]{0:T(1024)S(1)}, f32[768]{0:T(1024)}, u32[]{:S(2)}) copy-start(f32[768]{0:T(1024)} %iota_convert_fusion) | copy-start | bytes 9220
  230.1 117.5 %copy-start.49 = (f32[32]{0:T(128)S(1)}, f32[32]{0:T(128)}, u32[]{:S(2)}) copy-start(f32[32]{0:T(128)} %negate_power_fusion) | copy-start | bytes 388
  230.1 118.6 %copy-start.47 = (pred[768]{0:T(1024)(128)(4,1)S(1)}, pred[768]{0:T(1024)(128)(4,1)}, u32[]{:S(2)}) copy-start(pred[768]{0:T(1024)(128)(4,1)} %compare_reduce_fusion) | copy-start | bytes 2308
  362.7 36.2 %all-to-all-start.1 = ((bf16[4,192,768]{2,1,0:T(8,128)(2,1)}), bf16[4,192,768]{2,1,0:T(8,128)(2,1)}, u32[]{:S(2)}, u32[]{:S(2)}) async-start(bf16[4,192,768]{2,1,0:T(8,128)(2,1)} %bitcast.110), calls=%async_computation.1 | async-start | bytes 2359296 | tf_op jit(solution)/shard_map/all_to_all | solution.py:935
  380.7 13.6 %copy-start.17 = (f32[768,2]{1,0:T(8,128)S(1)}, f32[768,2]{1,0:T(8,128)}, u32[]{:S(2)}) copy-start(f32[768,2]{1,0:T(8,128)} %copy.135) | copy-start | bytes 18436
  380.7 13.6 %copy-start.18 = (f32[768,2]{1,0:T(8,128)S(1)}, f32[768,2]{1,0:T(8,128)}, u32[]{:S(2)}) copy-start(f32[768,2]{1,0:T(8,128)} %copy.131) | copy-start | bytes 18436
  380.7 13.6 %copy-start.38 = (f32[768]{0:T(1024)S(1)}, f32[768]{0:T(1024)}, u32[]{:S(2)}) copy-start(f32[768]{0:T(1024)} %copy-done.37) | copy-start | bytes 9220
  412.3 9.5 %copy-start.2 = (f32[768,768]{1,0:T(8,128)S(1)}, f32[768,768]{1,0:T(8,128)}, u32[]{:S(2)}) copy-start(f32[768,768]{1,0:T(8,128)} %get-tuple-element.64) | copy-start | bytes 7077892
  429.0 13.6 %copy-start.9 = (bf16[768,768]{0,1:T(8,128)(2,1)S(1)}, bf16[768,768]{0,1:T(8,128)(2,1)}, u32[]{:S(2)}) copy-start(bf16[768,768]{0,1:T(8,128)(2,1)} %copy.143) | copy-start | bytes 3538948
  466.2 23.4 %copy-start.8 = (bf16[768,768]{0,1:T(8,128)(2,1)S(1)}, bf16[768,768]{0,1:T(8,128)(2,1)}, u32[]{:S(2)}) copy-start(bf16[768,768]{0,1:T(8,128)(2,1)} %copy.141) | copy-start | bytes 3538948
  489.6 9.5 %copy-start.7 = (bf16[768,768]{0,1:T(8,128)(2,1)S(1)}, bf16[768,768]{0,1:T(8,128)(2,1)}, u32[]{:S(2)}) copy-start(bf16[768,768]{0,1:T(8,128)(2,1)} %copy-done.6) | copy-start | bytes 3538948
  499.1 7.8 %copy-start.46 = (bf16[768]{0:T(1024)(128)(2,1)S(1)}, bf16[768]{0:T(1024)(128)(2,1)}, u32[]{:S(2)}) copy-start(bf16[768]{0:T(1024)(128)(2,1)} %get-tuple-element.143) | copy-start | bytes 4612
  499.1 8.4 %copy-start.11 = (f32[768,768]{1,0:T(8,128)S(1)}, f32[768,768]{1,0:T(8,128)}, u32[]{:S(2)}) copy-start(f32[768,768]{1,0:T(8,128)} %copy-done.10) | copy-start | bytes 7077892
  499.1 8.4 %copy-start.53 = (bf16[768,768]{1,0:T(8,128)(2,1)S(1)}, bf16[768,768]{1,0:T(8,128)(2,1)}, u32[]{:S(2)}) copy-start(bf16[768,768]{1,0:T(8,128)(2,1)} %get-tuple-element.78) | copy-start | bytes 3538948
  517.7 10.4 %copy-start.20 = (bf16[768,768]{1,0:T(8,128)(2,1)S(1)}, bf16[768,768]{1,0:T(8,128)(2,1)}, u32[]{:S(2)}) copy-start(bf16[768,768]{1,0:T(8,128)(2,1)} %convolution_convert_fusion.3) | copy-start | bytes 3538948
  529.5 58.0 %copy-start.5 = (bf16[768,768]{1,0:T(8,128)(2,1)S(1)}, bf16[768,768]{1,0:T(8,128)(2,1)}, u32[]{:S(2)}) copy-start(bf16[768,768]{1,0:T(8,128)(2,1)} %get-tuple-element.69) | copy-start | bytes 3538948
  529.5 58.0 %copy-start.30 = (f32[768,2]{0,1:T(2,128)S(1)}, f32[768,2]{0,1:T(2,128)}, u32[]{:S(2)}) copy-start(f32[768,2]{0,1:T(2,128)} %copy-done.29) | copy-start | bytes 18436
  529.5 58.0 %copy-start.32 = (f32[768,2,2]{0,1,2:T(2,128)S(1)}, f32[768,2,2]{0,1,2:T(2,128)}, u32[]{:S(2)}) copy-start(f32[768,2,2]{0,1,2:T(2,128)} %copy.133) | copy-start | bytes 36868
  (32 other events, 110.4 us)

commit v3 on v2

v3 whole, which is shorter than its diff:
```python
import functools
from types import SimpleNamespace
from typing import NamedTuple

import jax
import jax.numpy as jnp
from jax import lax
from jax.experimental import pallas as pl
from jax.experimental.pallas import tpu as pltpu
import numpy as np
from jax.sharding import PartitionSpec as P

HEAD_DIM = 64
BLOCK = 256
LONGEST = 384
LEVEL_STEP = 2.5
LEAD = 4.0
EARLY = 5
SHARE = 7
epsilon = 1e-06


MESH = pl.DeviceIdType.MESH


class Spot:
    def __init__(self, sizes):
        self.nz, self.nx, self.ny, self.nc = sizes
        self.dp, self.ex = lax.axis_index("dp"), lax.axis_index("expert")
        self.z, self.x = lax.div(self.dp, self.nx), lax.rem(self.dp, self.nx)
        self.y, self.core = lax.div(self.ex, self.nc), lax.rem(self.ex, self.nc)

    def device(self, z=None, x=None, y=None, core=None):
        z, x = self.z if z is None else z, self.x if x is None else x
        y, core = self.y if y is None else y, self.core if core is None else core
        return {"dp": z * self.nx + x, "expert": y * self.nc + core}


def between(value, size):
    return jnp.logical_and(value >= 0, value < size)


class Flood:
    def __init__(self, spot, number, own, view, sends, recvs, z_first, mate=None):
        self.s, self.n, self.own, self.view = spot, number, own, view
        self.sends, self.recvs, self.z_first, self.mate = sends, recvs, z_first, mate
        if z_first:
            self.na, self.nb, self.a, self.b = spot.nz, spot.nx, spot.z, spot.x
        else:
            self.na, self.nb, self.a, self.b = spot.nx, spot.nz, spot.x, spot.z
        self.drains = []

    def origin(self, a, b):
        return a * self.s.nx + b if self.z_first else b * self.s.nx + a

    def along(self, which, value):
        zed = (which == 0) == self.z_first
        return self.s.device(z=value) if zed else self.s.device(x=value)

    def push(self, cond, src, o, way, device, recvs=None):
        copy = pltpu.make_async_remote_copy(
            src_ref=src, dst_ref=self.view(o),
            send_sem=self.sends.at[way, self.n, o],
            recv_sem=(self.recvs if recvs is None else recvs).at[self.n, o],
            device_id=device, device_id_type=MESH)
        if cond is None:
            copy.start()
            self.drains.append(copy.wait_send)
        else:
            pl.when(cond)(lambda: copy.start())
            self.drains.append(lambda: pl.when(cond)(lambda: copy.wait_send()))

    def share(self, cond, src, o):
        if self.mate is not None:
            self.push(cond, src, o, 4, self.s.device(core=1 - self.s.core), self.mate)

    def mates(self, view):
        def one(o, carry):
            pltpu.make_async_remote_copy(
                src_ref=view(o), dst_ref=view(o), send_sem=self.sends.at[0, self.n, o], recv_sem=self.mate.at[self.n, o],
                device_id=self.s.device(), device_id_type=MESH).wait_recv()
            return carry
        lax.fori_loop(0, self.s.nz * self.s.nx, one, 0)

    def arrive(self, o):
        pltpu.make_async_remote_copy(
            src_ref=self.view(o), dst_ref=self.view(o),
            send_sem=self.sends.at[0, self.n, o], recv_sem=self.recvs.at[self.n, o],
            device_id=self.s.device(), device_id_type=MESH).wait_recv()

    def second(self, cond, src, o):
        for j, sign in enumerate((1, -1)):
            to = self.b + sign
            if self.nb > 1:
                ok = between(to, self.nb)
                self.push(ok if cond is None else jnp.logical_and(cond, ok), src, o, 2 + j, self.along(1, to))

    def levels(self):
        out = [[] for _ in range(self.na + self.nb - 1)]

        def begin():
            o = self.origin(self.a, self.b)
            for j, sign in enumerate((1, -1)):
                if self.na > 1:
                    self.push(between(self.a + sign, self.na), self.own, o, j, self.along(0, self.a + sign))
            self.second(None, self.own, o)
            self.share(None, self.own, o)

        out[0].append(begin)
        for k in range(1, self.na):
            for j, sign in enumerate((1, -1)):
                def step(k=k, j=j, sign=sign):
                    a = self.a - sign * k
                    here = between(a, self.na)
                    o = self.origin(a, self.b)
                    pl.when(here)(lambda: self.arrive(o))
                    on = jnp.logical_and(here, between(self.a + sign, self.na))
                    if self.na > 2 or k == 0:
                        self.push(on, self.view(o), o, j, self.along(0, self.a + sign))
                    self.second(here, self.view(o), o)
                    self.share(here, self.view(o), o)
                out[k].append(step)
        for d in range(1, self.nb):
            for da in range(-(self.na - 1), self.na):
                for j, sign in enumerate((1, -1)):
                    def step(d=d, da=da, j=j, sign=sign):
                        a, b = self.a + da, self.b - sign * d
                        here = jnp.logical_and(between(a, self.na), between(b, self.nb))
                        o = self.origin(a, b)
                        pl.when(here)(lambda: self.arrive(o))
                        if self.nb > 2:
                            on = jnp.logical_and(here, between(self.b + sign, self.nb))
                            self.push(on, self.view(o), o, 2 + j, self.along(1, self.b + sign))
                        self.share(here, self.view(o), o)
                    out[abs(da) + d].append(step)
        return out


def enter(spot, devices):
    barrier = pltpu.get_barrier_semaphore()
    count = jnp.int32(0)
    for cond, device in devices:
        def hail(device=device):
            pl.semaphore_signal(barrier, inc=1, device_id=device, device_id_type=MESH)
        if cond is None:
            hail()
            count = count + 1
        else:
            pl.when(cond)(hail)
            count = count + cond.astype(jnp.int32)
    pl.semaphore_wait(barrier, count)


def line_neighbours(spot):
    out = []
    for sign in (1, -1):
        out.append((between(spot.z + sign, spot.nz), spot.device(z=spot.z + sign)))
        out.append((between(spot.x + sign, spot.nx), spot.device(x=spot.x + sign)))
    return out


def dot(a, b, ca=1, cb=0):
    return lax.dot_general(a, b, (((ca,), (cb,)), ((), ())), preferred_element_type=jnp.float32)


def turned(columns):
    eye = lax.broadcasted_iota(jnp.int32, (128, 128), 0) == lax.broadcasted_iota(jnp.int32, (128, 128), 1)
    return dot(jnp.where(eye, 1.0, 0.0).astype(jnp.bfloat16), columns, 1, 1)


def spread(columns):
    lane = lax.broadcasted_iota(jnp.int32, (columns[0].shape[0], 128), 1)
    out = jnp.zeros(lane.shape, jnp.float32)
    for j, c in enumerate(columns):
        out = jnp.where(lane == j, c, out)
    return out


def swap_halves(v):
    half = HEAD_DIM // 2
    lane = lax.broadcasted_iota(jnp.int32, v.shape, 1)
    return jnp.where(lax.rem(lane, HEAD_DIM) < half, pltpu.roll(v, v.shape[1] - half, 1), pltpu.roll(v, half, 1))


def head_masks():
    lane = lax.broadcasted_iota(jnp.int32, (1, 128), 1)
    low = jnp.where(lane < HEAD_DIM, 1.0, 0.0).astype(jnp.bfloat16)
    high = jnp.where(lane < HEAD_DIM, 0.0, 1.0).astype(jnp.bfloat16)
    return low, high


def key_range(i):
    return max(0, i * BLOCK - LONGEST), (i + 1) * BLOCK


class Front:
    def __init__(self, spot, experts, chunks, r):
        self.spot, self.experts, self.r = spot, experts, r
        self.length, self.width = r.tokens.shape
        self.capacity = 2 * self.length // (experts + 4)
        self.blocks = self.length // BLOCK
        self.tall, self.wide = self.length // 2, r.dn.shape[0] // chunks

    def ranks(self):
        r, n = self.r, self.length
        order = [r.order[:, k : k + 1] for k in range(2)]
        route = [r.routes[:, k : k + 1] for k in range(2)]
        parts = []
        for k in range(2):
            parts += [lax.div(order[k], 256).astype(jnp.float32), lax.rem(order[k], 256).astype(jnp.float32)]
        parts += [route[k].astype(jnp.float32) for k in range(2)]
        side = turned(spread(parts).astype(jnp.bfloat16))
        order_row = [side[2 * k : 2 * k + 1] * 256.0 + side[2 * k + 1 : 2 * k + 2] for k in range(2)]
        route_row = [side[4 + k : 5 + k] for k in range(2)]
        out = []
        for k in range(2):
            for i in range(self.blocks):
                rows = slice(i * BLOCK, (i + 1) * BLOCK)
                mine, kind = order[k][rows].astype(jnp.float32), route[k][rows].astype(jnp.float32)
                ahead = jnp.zeros((BLOCK, n), jnp.float32)
                for other in range(2):
                    ahead += jnp.where(
                        jnp.logical_and(order_row[other] < mine, route_row[other] == kind), 1.0, 0.0)
                rank = jnp.sum(ahead, axis=1, keepdims=True)
                kept = jnp.logical_and(kind < self.experts, rank < self.capacity)
                r.scal[pl.ds(i * BLOCK, BLOCK), 8 + k : 9 + k] = jnp.where(
                    kept, kind * self.capacity + rank, float(self.experts * self.capacity))
                r.scal[pl.ds(i * BLOCK, BLOCK), 10 + k : 11 + k] = jnp.where(kept, kind, 255.0)
                r.scal[pl.ds(i * BLOCK, BLOCK), 12 + k : 13 + k] = jnp.where(kept, rank, 0.0)
                r.scal[pl.ds(i * BLOCK, BLOCK), 14 + k : 15 + k] = kind

    def flat_rows(self):
        r = self.r
        side = turned(r.scal[...].astype(jnp.bfloat16))
        for k in range(2):
            kind, rank = side[10 + k : 11 + k], side[12 + k : 13 + k]
            r.flat[k : k + 1] = jnp.where(
                kind < 255.0, kind * self.capacity + rank, float(self.experts * self.capacity))

    def first_norm(self):
        r = self.r
        for i in range(self.blocks):
            rows = pl.ds(i * BLOCK, BLOCK)
            x = r.tokens[rows].astype(jnp.float32)
            r.scal[rows, 0:1] = lax.rsqrt(jnp.mean(x * x, axis=1, keepdims=True) + epsilon)

    def masks(self):
        r, n = self.r, self.length
        segment = r.segments[...].astype(jnp.float32)
        padding = r.padding[...]
        column = jnp.transpose(jnp.broadcast_to(segment, (128, n)))[:, 0:1]
        for i in range(self.blocks):
            k0, k1 = key_range(i)
            row = lax.broadcasted_iota(jnp.int32, (BLOCK, k1 - k0), 0) + i * BLOCK
            col = lax.broadcasted_iota(jnp.int32, (BLOCK, k1 - k0), 1) + k0
            same = column[i * BLOCK : (i + 1) * BLOCK] == segment[:, k0:k1]
            real = jnp.broadcast_to(padding[:, k0:k1], row.shape) == 1
            fine = jnp.logical_and(jnp.logical_and(col <= row, same), jnp.logical_or(real, col == row))
            r.bias[pl.ds(i * BLOCK, BLOCK), pl.ds(0, k1 - k0)] = jnp.where(fine, 0.0, -1e30)

    def small_rows(self):
        r = self.r
        side = turned(r.rest[:, pl.ds(self.width, 128)])
        r.rows[...] = side[: r.rows.shape[0]]

    def project(self, i):
        r, w = self.r, self.width
        rows = pl.ds(i * BLOCK, BLOCK)
        x = r.tokens[rows].astype(jnp.float32)
        normed = (x * r.scal[rows, 0:1] * r.rows[0:1]).astype(jnp.bfloat16)
        r.normed[rows] = normed
        cosine, sine = r.cosine[rows], r.sine[rows]
        for part, to in enumerate((r.q, r.k)):
            full = dot(normed, r.qkv[:, pl.ds(part * w, w)])
            for pair in range(w // 128):
                v = full[:, pair * 128 : pair * 128 + 128]
                v = v * cosine + swap_halves(v) * sine
                if part == 0:
                    v = v * HEAD_DIM ** (-0.5)
                to[rows, pl.ds(pair * 128, 128)] = v.astype(jnp.bfloat16)
        r.v[rows] = dot(normed, r.qkv[:, pl.ds(2 * w, w)]).astype(jnp.bfloat16)

    def attend(self, i, pair):
        r = self.r
        k0, k1 = key_range(i)
        rows, keys, lanes = pl.ds(i * BLOCK, BLOCK), pl.ds(k0, k1 - k0), pl.ds(pair * 128, 128)
        q, k, v = r.q[rows, lanes], r.k[keys, lanes], r.v[keys, lanes]
        bias = r.bias[rows, pl.ds(0, k1 - k0)]
        out = jnp.zeros((BLOCK, 128), jnp.float32)
        for s, mask in enumerate(head_masks()):
            scores = dot(q * mask, k, 1, 1) + bias
            top = jnp.max(scores, axis=1, keepdims=True)
            e = jnp.exp(scores - top)
            total = jnp.sum(e, axis=1, keepdims=True)
            probs = (e * (1.0 / total)).astype(jnp.bfloat16)
            out = out + dot(probs, v * mask)
            r.lse[rows, 2 * pair + s : 2 * pair + s + 1] = top + jnp.log(total)
        r.attended[rows, lanes] = out.astype(jnp.bfloat16)

    def gate(self, i):
        r, w, e = self.r, self.width, self.experts
        rows = pl.ds(i * BLOCK, BLOCK)
        h = r.tokens[rows].astype(jnp.float32) + dot(r.attended[rows], r.rest[:, pl.ds(0, w)])
        r.h[rows] = h
        inverse = lax.rsqrt(jnp.mean(h * h, axis=1, keepdims=True) + epsilon)
        hn = (h * inverse * r.rows[1:2]).astype(jnp.bfloat16)
        r.hn[rows] = hn
        small = dot(hn, r.rest[:, pl.ds(w, 128)])
        lane = lax.broadcasted_iota(jnp.int32, small.shape, 1)
        prev = r.prev[rows].astype(jnp.float32)
        prev_lane = lax.broadcasted_iota(jnp.int32, prev.shape, 1)
        picked = []
        for k in range(2):
            route = r.routes[rows, k : k + 1]
            picked.append(jnp.sum(jnp.where(lane == route + 8, small, 0.0), axis=1, keepdims=True)
                          + jnp.sum(jnp.where(prev_lane == route, prev, 0.0), axis=1, keepdims=True))
        def soft(a, b):
            top = jnp.maximum(a, b)
            ea, eb = jnp.exp(a - top), jnp.exp(b - top)
            return ea / (ea + eb), eb / (ea + eb)
        gates = soft(*picked)
        mix = soft(small[:, 2:3], small[:, 3:4]) + soft(small[:, 4:5], small[:, 5:6])
        r.scal[rows, 1:2] = inverse
        for j, c in enumerate(gates + mix):
            r.scal[rows, 2 + j : 3 + j] = c
        cot = r.cot[rows].astype(jnp.float32)
        for k in range(2):
            r.gcot[k, rows] = (gates[k] * cot).astype(jnp.bfloat16)

    def slots(self, d):
        r, n = self.r, self.length
        e = lax.rem(self.spot.ex + d, self.experts)
        slot = (lax.broadcasted_iota(jnp.int32, (self.capacity, n), 0) + e * self.capacity).astype(jnp.float32)
        at = [jnp.where(r.flat[k : k + 1] == slot, 1.0, 0.0) for k in range(2)]
        x = dot((at[0] + at[1]).astype(jnp.bfloat16), r.hn[...]).astype(jnp.bfloat16)
        g = (dot(at[0].astype(jnp.bfloat16), r.gcot[0]) + dot(at[1].astype(jnp.bfloat16), r.gcot[1]))
        g = g.astype(jnp.bfloat16)
        if d == 0:
            rows = pl.ds(pl.multiple_of(e * self.capacity, 16), self.capacity)
            r.xin[rows], r.gin[rows] = x, g
        else:
            r.sendx[d - 1], r.sendg[d - 1] = x, g


    def side_rows(self):
        self.r.xt[...] = jnp.transpose(self.r.xin[...])

    def hidden(self, j, part):
        r, w = self.r, self.wide
        ff = r.gu.shape[1] // 2
        rows = pl.ds(part * self.tall, self.tall)
        x, g = r.xin[rows], r.gin[rows]
        gate = dot(x, r.gu[:, pl.ds(j * w, w)])
        up = dot(x, r.gu[:, pl.ds(ff + j * w, w)])
        back = dot(g, r.dn[pl.ds(j * w, w)], 1, 1)
        sigmoid = 1.0 / (1.0 + jnp.exp(-gate))
        silu = gate * sigmoid
        r.act[rows, pl.ds(j * w, w)] = (silu * up).astype(jnp.bfloat16)
        r.pg[rows, pl.ds(j * w, w)] = (back * up * sigmoid * (1.0 + gate * (1.0 - sigmoid))).astype(jnp.bfloat16)
        r.pg[rows, pl.ds(ff + j * w, w)] = (back * silu).astype(jnp.bfloat16)

    def outward(self, part):
        rows = pl.ds(part * self.tall, self.tall)
        self.r.yall[rows] = dot(self.r.act[rows], self.r.dn[...]).astype(jnp.bfloat16)

    def inward(self, part):
        rows = pl.ds(part * self.tall, self.tall)
        self.r.dxall[rows] = dot(self.r.pg[rows], self.r.gu[...], 1, 1).astype(jnp.bfloat16)

    def down_grad(self, j):
        r, w = self.r, self.wide
        r.dn[pl.ds(j * w, w)] = dot(r.act[:, pl.ds(j * w, w)], r.gin[...], 0, 0).astype(jnp.bfloat16)

    def up_grad(self, j):
        r, w = self.r, self.wide
        r.gu[:, pl.ds(j * w, w)] = dot(r.xt[...], r.pg[:, pl.ds(j * w, w)]).astype(jnp.bfloat16)


def expert_device(spot, e):
    return {"dp": spot.dp, "expert": e}


def slots_of(ref, capacity):
    return lambda e: ref.at[pl.ds(pl.multiple_of(e * capacity, 16), capacity)]


class Exchange:
    def __init__(self, spot, experts, number, out, into, sems):
        self.spot, self.experts, self.n, self.out, self.into, self.sems = spot, experts, number, out, into, sems

    def copy(self, d):
        e = lax.rem(self.spot.ex + d, self.experts)
        return pltpu.make_async_remote_copy(
            src_ref=self.out(d), dst_ref=self.into(self.spot.ex), send_sem=self.sems.at[0, self.n, d],
            recv_sem=self.sems.at[1, self.n, self.spot.ex], device_id=expert_device(self.spot, e),
            device_id_type=MESH)

    def send(self, d):
        self.copy(d).start()

    def drain(self, d):
        self.copy(d).wait_send()

    def receive(self, d):
        e = lax.rem(self.spot.ex + d, self.experts)
        pltpu.make_async_remote_copy(
            src_ref=self.into(e), dst_ref=self.into(e), send_sem=self.sems.at[0, self.n, d],
            recv_sem=self.sems.at[1, self.n, e], device_id=expert_device(self.spot, e),
            device_id_type=MESH).wait_recv()


def woven(work, events):
    done = 0
    for j, piece in enumerate(work):
        piece()
        upto = (j + 1) * len(events) // len(work)
        for event in events[done:upto]:
            event()
        done = upto


class FrontIns(NamedTuple):
    tokens: object
    prev: object
    segments: object
    padding: object
    routes: object
    order: object
    cot: object
    cosine: object
    sine: object
    qkv_own: object
    rest_own: object
    gu_own: object
    dn_own: object


class FrontOuts(NamedTuple):
    gu_grad: object
    dn_grad: object
    qkv_hbm: object
    rest_hbm: object
    q_hbm: object
    k_hbm: object
    v_hbm: object
    normed_hbm: object
    attended_hbm: object
    hn_hbm: object
    h_hbm: object
    lse_hbm: object
    scal_hbm: object
    rows_hbm: object
    y_hbm: object
    dx_hbm: object


class FrontScratch(NamedTuple):
    qkv: object
    rest: object
    q: object
    k: object
    v: object
    normed: object
    attended: object
    hn: object
    h: object
    lse: object
    scal: object
    rows: object
    gu: object
    dn: object
    xin: object
    gin: object
    xt: object
    act: object
    pg: object
    yall: object
    dxall: object
    flat: object
    bias: object
    gcot: object
    sendx: object
    sendg: object
    sends: object
    recvs: object
    mates: object
    local: object
    trade: object


def front_kernel(sizes, experts, chunks, *refs):
    r = SimpleNamespace(**dict(zip(FrontIns._fields + FrontOuts._fields + FrontScratch._fields, refs)))
    spot = Spot(sizes)
    front = Front(spot, experts, chunks, r)
    enter(spot, line_neighbours(spot)
          + [(None, expert_device(spot, lax.rem(spot.ex + d, experts))) for d in range(1, experts)])
    rows = r.qkv_own.shape[0]
    rows_d = r.dn_own.shape[0]
    ff = r.dn.shape[0]
    first, later = [], []
    for src, out in ((r.qkv_own, r.qkv), (r.rest_own, r.rest)):
        part = src.shape[1] // 2
        def half(o, core, out=out, part=part):
            return out.at[pl.ds(pl.multiple_of(o * rows, 8), rows), pl.ds(pl.multiple_of(core * part, 128), part)]
        first.append((src.at[:, pl.ds(pl.multiple_of(spot.core * part, 128), part)],
                      lambda o, half=half: half(o, spot.core), True, lambda o, half=half: half(o, 1 - spot.core)))
    part = rows_d // 2
    for p, zf in ((0, True), (1, False)):
        later.append((r.dn_own.at[pl.ds(p * part, part)],
                      lambda o, p=p: r.dn.at[pl.ds(pl.multiple_of(o * rows_d + p * part, 8), part)], zf, None))
    wide = ff // chunks
    for c in range(chunks):
        for side in range(2):
            cols = pl.ds(side * ff + c * wide, wide)
            later.append((r.gu_own.at[:, cols],
                          lambda o, cols=cols: r.gu.at[pl.ds(pl.multiple_of(o * rows, 8), rows), cols], True, None))
    floods = [Flood(spot, n, own, view, r.sends, r.recvs, zf, None if other is None else r.mates)
              for n, (own, view, zf, other) in enumerate(first + later)]
    levels = [f.levels() for f in floods]
    dense = levels[:2]
    keeps = [pltpu.make_async_copy(own, view(spot.dp), r.local.at[n])
             for n, (own, view, zf, other) in enumerate(first + later)]
    for ls in dense:
        for step in ls[0]:
            step()
    for keep in keeps:
        keep.start()
    front.ranks()
    front.flat_rows()
    front.first_norm()
    front.masks()
    depth = max(map(len, levels))
    keyed = []
    for n, ls in enumerate(levels[2:]):
        for level, steps in enumerate(ls):
            keyed += [(n + LEVEL_STEP * level if level else n - LEAD, n, level, step) for step in steps]
    keyed.sort(key=lambda t: t[:3])
    ahead = [t for t in keyed if t[0] <= 0]
    keyed = keyed[len(ahead):]
    for level in range(1, depth):
        if level == depth - 1:
            for t in ahead:
                t[3]()
        for ls in dense:
            if level < len(ls):
                for step in ls[level]:
                    step()
    for keep in keeps[:2]:
        keep.wait()
    for f, (own, view, zf, other) in zip(floods, first):
        f.mates(other)
    trades = [Exchange(spot, experts, n, lambda d, out=out: out.at[d - 1], slots_of(into, front.capacity), r.trade)
              for n, (out, into) in enumerate(((r.sendx, r.xin), (r.sendg, r.gin)))]
    work = [front.small_rows]
    work += [functools.partial(front.project, i) for i in range(front.blocks)]
    for pair in range(front.width // 128):
        work += [functools.partial(front.attend, i, pair) for i in range(front.blocks)]
    work += [functools.partial(front.gate, i) for i in range(front.blocks)]
    def dispatch(d):
        front.slots(d)
        if d:
            for t in trades:
                t.send(d)
    work += [functools.partial(dispatch, d) for d in list(range(1, experts)) + [0]]
    def upto(item):
        out = []
        while keyed and keyed[0][1] <= item:
            out.append(keyed.pop(0)[3])
        last = max((j for j, t in enumerate(keyed) if t[1] <= item), default=-1)
        out += [t[3] for t in keyed[: last + 1]]
        del keyed[: last + 1]
        return out
    saves = []
    def save(src, dst):
        copy = pltpu.make_async_copy(src, dst, r.local.at[len(keeps) + len(saves)])
        copy.start()
        saves.append(copy)
    def save_dense():
        for src, dst in ((r.qkv, r.qkv_hbm), (r.rest, r.rest_hbm), (r.q, r.q_hbm), (r.k, r.k_hbm), (r.v, r.v_hbm),
                         (r.normed, r.normed_hbm), (r.attended, r.attended_hbm), (r.lse, r.lse_hbm), (r.rows, r.rows_hbm),
                         (r.hn, r.hn_hbm), (r.h, r.h_hbm), (r.scal, r.scal_hbm)):
            save(src, dst)
    events = []
    early = len(keyed) * SHARE // 16
    events, keyed[:early] = [t[3] for t in keyed[:early]], []
    woven(work, events)
    save_dense()
    for event in upto(1 + 2):
        event()
    for d in range(1, experts):
        for t in trades:
            t.receive(d)
    keeps[2].wait()
    keeps[3].wait()
    front.side_rows()
    for c in range(chunks):
        for event in upto(2 + 2 * c + 1):
            event()
        keeps[4 + 2 * c].wait()
        keeps[5 + 2 * c].wait()
        for p in range(2):
            front.hidden(c, p)
    for p in range(2):
        front.outward(p)
    save(r.yall, r.y_hbm)
    for p in range(2):
        front.inward(p)
    save(r.dxall, r.dx_hbm)
    for f in floods:
        for drain in f.drains:
            drain()
    for c in range(chunks):
        front.down_grad(c)
        save(r.dn.at[pl.ds(c * wide, wide)], r.dn_grad.at[pl.ds(c * wide, wide)])
    for c in range(2 * chunks):
        front.up_grad(c)
        save(r.gu.at[:, pl.ds(c * wide, wide)], r.gu_grad.at[:, pl.ds(c * wide, wide)])
    for d in range(1, experts):
        for t in trades:
            t.drain(d)
    for copy in saves:
        copy.wait()


def run_front(sizes, experts, ins, chunks=4):
    tokens, qkv, rest, gu, dn = ins[0], ins[9], ins[10], ins[11], ins[12]
    length, width = tokens.shape
    n_dp = sizes[0] * sizes[1]
    capacity = 2 * length // (experts + 4)
    slots = experts * capacity
    bf, f4 = jnp.bfloat16, jnp.float32
    S, V = jax.ShapeDtypeStruct, pltpu.VMEM
    token = S((length, width), bf)
    gu_all, dn_all = (gu.shape[0] * n_dp, gu.shape[1]), (dn.shape[0] * n_dp, dn.shape[1])
    outs = [S(gu_all, bf), S(dn_all, bf)] + [S((a.shape[0] * n_dp, a.shape[1]), bf) for a in (qkv, rest)]
    outs += [token] * 6 + [S((length, width), f4), S((length, 128), f4), S((length, 128), f4), S((16, width), f4)]
    outs += [S((slots, width), bf)] * 2
    items = 4 + 2 * chunks
    dma = pltpu.SemaphoreType.DMA
    vmem = pl.BlockSpec(memory_space=pltpu.VMEM)
    hbm = pl.BlockSpec(memory_space=pl.ANY)
    send = V((experts - 1, capacity, width), bf)
    return pl.pallas_call(
        functools.partial(front_kernel, sizes, experts, chunks),
        out_shape=tuple(outs),
        in_specs=[vmem] * 13,
        out_specs=(hbm,) * len(outs),
        scratch_shapes=[V(o.shape, o.dtype) for o in outs[2:14]] + [
            V(gu_all, bf), V(dn_all, bf), V((slots, width), bf), V((slots, width), bf), V((width, slots), bf),
            V((slots, dn_all[0]), bf), V((slots, gu_all[1]), bf), V((slots, width), bf), V((slots, width), bf),
            V((8, length), f4), V((length, BLOCK + LONGEST), f4), V((2, length, width), bf), send, send,
            dma((5, items, n_dp)), dma((items, n_dp)), dma((2, n_dp)), dma((items + 16 + 3 * chunks,)),
            dma((2, 4, experts))],
        compiler_params=pltpu.CompilerParams(collective_id=1, has_side_effects=True, vmem_limit_bytes=63 << 20),
        name="front",
    )(*ins)


def add_into(view, more):
    view[...] = (view[...].astype(jnp.float32) + more[...].astype(jnp.float32)).astype(view.dtype)


class Reduce:
    def __init__(self, spot, number, view, one, two, sends, recv_one, recv_two, x_first):
        self.s, self.n, self.view, self.one, self.two = spot, number, view, one, two
        self.sends, self.recv_one, self.recv_two, self.x_first = sends, recv_one, recv_two, x_first
        if x_first:
            self.np, self.nq, self.p, self.q = spot.nx, spot.nz, spot.x, spot.z
        else:
            self.np, self.nq, self.p, self.q = spot.nz, spot.nx, spot.z, spot.x
        self.drains = []

    @staticmethod
    def slots(n):
        return 1 if n == 2 else n + 1

    @staticmethod
    def slot(n, place, above):
        if n == 2:
            return 0
        return jnp.where(above, n, place)

    def owner(self, p, q):
        return q * self.s.nx + p if self.x_first else p * self.s.nx + q

    def along(self, first, value):
        return self.s.device(x=value) if first == self.x_first else self.s.device(z=value)

    def push(self, cond, o, dst, recv, device):
        copy = pltpu.make_async_remote_copy(
            src_ref=self.view(o), dst_ref=dst, send_sem=self.sends.at[self.n, o], recv_sem=recv,
            device_id=device, device_id_type=MESH)
        pl.when(cond)(lambda: copy.start())
        self.drains.append(lambda: pl.when(cond)(lambda: copy.wait_send()))

    def take(self, cond, o, slot, recv):
        def run():
            pltpu.make_async_remote_copy(
                src_ref=slot, dst_ref=slot, send_sem=self.sends.at[self.n, o], recv_sem=recv,
                device_id=self.s.device(), device_id_type=MESH).wait_recv()
            add_into(self.view(o), slot)
        pl.when(cond)(run)

    def order(self):
        return sorted(range(-(self.nq - 1), self.nq), key=lambda d: (-abs(d), d))

    def phase_one(self):
        steps = []
        for turn in range(2):
            sign = jnp.where(self.p * 2 < self.np, 1, -1) * (1 if turn == 0 else -1)
            for k in range(self.np - 1, 0, -1):
                for dq in self.order():
                    def step(sign=sign, k=k, dq=dq):
                        p, q = self.p + sign * k, self.q + dq
                        here = jnp.logical_and(between(p, self.np), between(q, self.nq))
                        o = self.owner(p, q)
                        if self.np > 2:
                            behind = jnp.logical_and(here, between(self.p - sign, self.np))
                            self.take(behind, o, self.one.at[p, q], self.recv_one.at[self.n, p, q])
                        slot = self.slot(self.np, p, jnp.logical_and(k == 1, sign < 0))
                        self.push(here, o, self.one.at[slot, q], self.recv_one.at[self.n, slot, q],
                                  self.along(True, self.p + sign))
                    steps.append(step)
        return steps

    def settle(self, cond, q):
        o = self.owner(self.p, q)
        below = self.p > 0
        above = self.p < self.np - 1
        if cond is not None:
            below, above = jnp.logical_and(cond, below), jnp.logical_and(cond, above)
        for cond, top in ((below, False), (above, True)):
            slot = self.slot(self.np, self.p, top)
            self.take(cond, o, self.one.at[slot, q], self.recv_one.at[self.n, slot, q])

    def phase_two(self):
        steps = []
        for turn in range(2):
            sign = jnp.where(self.q * 2 < self.nq, 1, -1) * (1 if turn == 0 else -1)
            for k in range(self.nq - 1, 0, -1):
                def step(sign=sign, k=k):
                    q = self.q + sign * k
                    here = between(q, self.nq)
                    o = self.owner(self.p, q)
                    self.settle(here, q)
                    behind = jnp.logical_and(here, between(self.q - sign, self.nq))
                    if self.nq > 2:
                        self.take(behind, o, self.two.at[q], self.recv_two.at[self.n, q])
                    slot = self.slot(self.nq, q, jnp.logical_and(k == 1, sign < 0))
                    self.push(here, o, self.two.at[slot], self.recv_two.at[self.n, slot], self.along(False, self.q + sign))
                steps.append(step)
        return steps

    def finish(self, out):
        o = self.owner(self.p, self.q)
        self.settle(None, self.q)
        out[...] = self.view(o)[...].astype(jnp.float32)
        for cond, top in ((self.q > 0, False), (self.q < self.nq - 1, True)):
            def run(slot=self.slot(self.nq, self.q, top)):
                two = self.two.at[slot]
                pltpu.make_async_remote_copy(
                    src_ref=two, dst_ref=two, send_sem=self.sends.at[self.n, o], recv_sem=self.recv_two.at[self.n, slot],
                    device_id=self.s.device(), device_id_type=MESH).wait_recv()
                out[...] += two[...].astype(jnp.float32)
            pl.when(cond)(run)


def column_of(row):
    return jnp.transpose(jnp.broadcast_to(row, (128, row.shape[1])))


class Dense:
    def __init__(self, spot, number, own, bufs, sems, done):
        self.spot, self.n, self.own, self.done = spot, number, own, done
        self.mine, self.one, self.two, self.ybuf, self.final, self.other = bufs
        self.sends, self.recv_one, self.recv_two, self.mate, self.ys, self.outs = sems
        self.reduce = Reduce(spot, number, lambda o: self.mine.at[o], self.one, self.two, self.sends, self.recv_one,
                             self.recv_two, True)
        self.drains = []

    def swap(self):
        return pltpu.make_async_remote_copy(
            src_ref=self.own.at[1 - self.spot.core], dst_ref=self.mine, send_sem=self.mate.at[0, self.n],
            recv_sem=self.mate.at[1, self.n], device_id=self.spot.device(core=1 - self.spot.core), device_id_type=MESH)

    def begin(self):
        self.swap().start()

    def merge(self):
        self.swap().wait()
        def add(o, carry):
            add_into(self.mine.at[o], self.own.at[self.spot.core, o])
            return carry
        lax.fori_loop(0, self.mine.shape[0], add, 0)
        for step in self.reduce.phase_one():
            step()

    def across(self, d):
        y = lax.rem(self.spot.y + d, self.spot.ny)
        return pltpu.make_async_remote_copy(
            src_ref=self.ybuf.at[self.spot.y], dst_ref=self.ybuf.at[self.spot.y], send_sem=self.ys.at[0, self.n, d],
            recv_sem=self.ys.at[1, self.n, self.spot.y], device_id=self.spot.device(y=y), device_id_type=MESH)

    def settle(self):
        self.reduce.finish(self.final)
        self.ybuf[self.spot.y] = self.final[...].astype(self.ybuf.dtype)
        for d in range(1, self.spot.ny):
            copy = self.across(d)
            copy.start()
            self.drains.append(copy.wait_send)

    def hand(self):
        return pltpu.make_async_remote_copy(
            src_ref=self.final, dst_ref=self.other, send_sem=self.outs.at[0, self.n], recv_sem=self.outs.at[1, self.n],
            device_id=self.spot.device(core=1 - self.spot.core), device_id_type=MESH)

    def total(self):
        for d in range(1, self.spot.ny):
            y = lax.rem(self.spot.y + d, self.spot.ny)
            pltpu.make_async_remote_copy(
                src_ref=self.ybuf.at[y], dst_ref=self.ybuf.at[y], send_sem=self.ys.at[0, self.n, d],
                recv_sem=self.ys.at[1, self.n, y], device_id=self.spot.device(y=y), device_id_type=MESH).wait_recv()
        sum_ = self.ybuf[0].astype(jnp.float32)
        for y in range(1, self.spot.ny):
            sum_ = sum_ + self.ybuf[y].astype(jnp.float32)
        self.final[...] = sum_
        self.hand().start()

    def end(self):
        self.hand().wait()
        for half in range(2):
            pl.when(self.spot.core == half)(lambda half=half: self.done(half, self.final[...]))
            pl.when(self.spot.core != half)(lambda half=half: self.done(half, self.other[...]))

    def steps(self):
        return [self.merge] + self.reduce.phase_two() + [self.settle, self.total, self.end]


class Tail:
    def __init__(self, spot, experts, r):
        self.spot, self.experts, self.r = spot, experts, r
        self.length, self.width = r.cot.shape
        self.blocks = self.length // BLOCK
        self.pairs = self.width // 128

    def prepare(self):
        r, n = self.r, self.length
        r.lse_rows[...] = jnp.transpose(r.lse[...])[: r.lse_rows.shape[0]]
        segment = r.segments[...].astype(jnp.float32)
        seg_col = column_of(segment)[:, 0:1]
        pad_col = column_of(r.padding[...].astype(jnp.float32))[:, 0:1]
        at = 0
        for i in range(self.blocks):
            k0, k1 = key_range(i)
            key = lax.broadcasted_iota(jnp.int32, (k1 - k0, BLOCK), 0) + k0
            query = lax.broadcasted_iota(jnp.int32, (k1 - k0, BLOCK), 1) + i * BLOCK
            same = seg_col[k0:k1] == segment[:, i * BLOCK : (i + 1) * BLOCK]
            fine = jnp.logical_and(jnp.logical_and(key <= query, same),
                                   jnp.logical_or(pad_col[k0:k1] == 1.0, key == query))
            r.bias[pl.ds(at, k1 - k0)] = jnp.where(fine, 0.0, -1e30).astype(jnp.bfloat16)
            at += k1 - k0
        r.gain_rows[...] = jnp.zeros(r.gain_rows.shape, jnp.float32)

    def combine(self, i):
        r, w, e = self.r, self.width, self.experts
        rows = pl.ds(i * BLOCK, BLOCK)
        col = lambda j: r.scal[rows, j : j + 1]
        slot = lax.broadcasted_iota(jnp.int32, (BLOCK, r.y.shape[0]), 1).astype(jnp.float32)
        at = [jnp.where(col(8 + k) == slot, 1.0, 0.0).astype(jnp.bfloat16) for k in range(2)]
        pair = [dot(at[k], r.y[...]) for k in range(2)]
        routed = dot(at[0] + at[1], r.dx[...])
        cot, hn = r.cot[rows].astype(jnp.float32), r.hn[rows].astype(jnp.float32)
        h = r.tg[rows]
        gates, mix = [col(2), col(3)], [[col(4), col(5)], [col(6), col(7)]]
        route = [col(14 + k) for k in range(2)]
        one = lambda c: jnp.where(c, 1.0, 0.0)
        fixed = [[one(route[k] == e + 2 + j) for j in range(2)] for k in range(2)]
        share = [one(route[k] == e + 1) + fixed[k][0] * mix[0][0] + fixed[k][1] * mix[1][0] for k in range(2)]
        copy = gates[0] * share[0] + gates[1] * share[1]
        chosen = [gates[0] * fixed[0][j] + gates[1] * fixed[1][j] for j in range(2)]
        coef = [chosen[j] * mix[j][1] for j in range(2)]
        const = [r.rows[6 + j : 7 + j] for j in range(2)]
        branch = gates[0] * pair[0] + gates[1] * pair[1] + copy * hn + (coef[0] * const[0] + coef[1] * const[1])
        r.layer_out[rows] = (h + branch).astype(jnp.bfloat16)
        total = lambda v: jnp.sum(v, axis=1, keepdims=True)
        with_hn = total(cot * hn)
        with_const = [total(cot * const[j]) for j in range(2)]
        grads = [total(cot * pair[k]) + share[k] * with_hn
                 + fixed[k][0] * mix[0][1] * with_const[0] + fixed[k][1] * mix[1][1] * with_const[1] for k in range(2)]
        mean = gates[0] * grads[0] + gates[1] * grads[1]
        picked = [gates[k] * (grads[k] - mean) for k in range(2)]
        lane = lax.broadcasted_iota(jnp.int32, (BLOCK, r.prev_grad.shape[1]), 1).astype(jnp.float32)
        r.prev_grad[rows] = jnp.where(lane == route[0], picked[0], 0.0) + jnp.where(lane == route[1], picked[1], 0.0)
        lane = lax.broadcasted_iota(jnp.int32, (BLOCK, 128), 1).astype(jnp.float32)
        low = jnp.where(lane == route[0] + 8, picked[0], 0.0) + jnp.where(lane == route[1] + 8, picked[1], 0.0)
        for j in range(2):
            g = [chosen[j] * with_hn, chosen[j] * with_const[j]]
            m = mix[j][0] * g[0] + mix[j][1] * g[1]
            for q in range(2):
                low = jnp.where(lane == 2 + 2 * j + q, mix[j][q] * (g[q] - m), low)
        low = low.astype(jnp.bfloat16)
        r.low[rows] = low
        high = [c.astype(jnp.bfloat16).astype(jnp.float32) for c in coef]
        both = jnp.zeros(lane.shape, jnp.float32)
        for j in range(2):
            both = jnp.where(lane == 6 + j, high[j], jnp.where(lane == 70 + j, coef[j] - high[j], both))
        r.coef[rows] = both.astype(jnp.bfloat16)
        grad = routed + copy * cot + dot(low, r.rest[:, pl.ds(w, 128)], 1, 1)
        dh = cot + self.unnorm(grad, h, col(1), 1)
        r.tg[rows] = dh
        dh = dh.astype(jnp.bfloat16)
        r.dh[rows] = dh

    def unnorm(self, grad, v, inverse, gain):
        r = self.r
        scaled = r.rows[gain : gain + 1] * grad
        mean = jnp.sum(scaled * v, axis=1, keepdims=True) / v.shape[1]
        r.gain_rows[gain : gain + 1] += jnp.sum(grad * v * inverse, axis=0, keepdims=True)
        return inverse * scaled - v * (inverse * inverse * inverse * mean)

    def unproject(self, i):
        r = self.r
        rows = pl.ds(i * BLOCK, BLOCK)
        r.ag[rows] = dot(r.dh[rows], r.rest[:, pl.ds(0, self.width)], 1, 1).astype(jnp.bfloat16)

    def blocked(self, v):
        n = self.spot.nz * self.spot.nx
        return v.reshape(n, v.shape[0] // n, v.shape[1])

    def out_grad(self):
        r = self.r
        half = self.width // 2
        for c in range(2):
            g = dot(r.attended[...], r.dh[:, pl.ds(c * half, half)], 0, 0)
            r.own[self.pairs // 2, c] = self.blocked(g).astype(jnp.bfloat16)

    def small_grad(self):
        r = self.r
        g = dot(r.cot[...], r.coef[...], 0, 0)
        lane = lax.broadcasted_iota(jnp.int32, g.shape, 1)
        g = jnp.where(lane < 64, g + pltpu.roll(g, 64, 1), 0.0) + dot(r.hn[...], r.low[...], 0, 0)
        r.own_small[0] = self.blocked(g).astype(jnp.bfloat16)
        r.own_small[1] = jnp.zeros(r.own_small.shape[1:], jnp.bfloat16)

    def small_end(self):
        r = self.r
        g = r.own_small[0].astype(jnp.float32)
        lane = lax.broadcasted_iota(jnp.int32, g.shape, 2)
        for j in range(2):
            g = jnp.where(lane == j, self.blocked(column_of(r.gain_rows[j : j + 1])), g)
        r.own_small[0] = g.astype(jnp.bfloat16)

    def normed_side(self):
        self.r.nt[...] = jnp.transpose(self.r.normed[...])

    def pair_begin(self, pair):
        r = self.r
        r.kt[...] = jnp.transpose(r.k[:, pl.ds(pair * 128, 128)])
        r.dk[...] = jnp.zeros(r.dk.shape, jnp.float32)
        r.dv[...] = jnp.zeros(r.dv.shape, jnp.float32)

    def attend(self, pair, i):
        r = self.r
        k0, k1 = key_range(i)
        at = sum(key_range(j)[1] - key_range(j)[0] for j in range(i))
        rows, keys, lanes = pl.ds(i * BLOCK, BLOCK), pl.ds(k0, k1 - k0), pl.ds(pair * 128, 128)
        q, k, v, g = r.q[rows, lanes], r.k[keys, lanes], r.v[keys, lanes], r.ag[rows, lanes]
        bias = r.bias[pl.ds(at, k1 - k0)].astype(jnp.float32)
        dq = []
        for s, mask in enumerate(head_masks()):
            qs, gs = q * mask, g * mask
            head = 2 * pair + s
            probs = jnp.exp(dot(k, qs, 1, 1) + bias - r.lse_rows[head : head + 1, rows])
            grad = dot(v, gs, 1, 1)
            mean = jnp.sum(probs * grad, axis=0, keepdims=True)
            ds = (probs * (grad - mean)).astype(jnp.bfloat16)
            r.dv[keys] += dot(probs.astype(jnp.bfloat16), gs)
            r.dk[keys] += dot(ds, qs)
            dq.append(dot(r.kt[pl.ds(s * HEAD_DIM, HEAD_DIM), keys], ds))
        r.dq[rows] = jnp.transpose(jnp.concatenate(dq, axis=0))

    def pair_end(self, pair):
        r = self.r
        lanes = pl.ds(pair * 128, 128)
        cosine, sine = r.cosine[...], r.sine[...]
        dq = r.dq[...] * HEAD_DIM ** (-0.5)
        dk = r.dk[...]
        dq = (dq * cosine - swap_halves(dq) * sine).astype(jnp.bfloat16)
        dk = (dk * cosine - swap_halves(dk) * sine).astype(jnp.bfloat16)
        dv = r.dv[...].astype(jnp.bfloat16)
        r.q[:, lanes], r.k[:, lanes], r.v[:, lanes] = dq, dk, dv
        half = self.pairs // 2
        for part, d in enumerate((dq, dk, dv)):
            g = dot(r.nt[...], d)
            r.own[pair % half, pair // half, :, :, pl.ds(part * 128, 128)] = self.blocked(g).astype(jnp.bfloat16)

    def last(self, i):
        r, w = self.r, self.width
        rows = pl.ds(i * BLOCK, BLOCK)
        grad = (dot(r.q[rows], r.qkv[:, pl.ds(0, w)], 1, 1) + dot(r.k[rows], r.qkv[:, pl.ds(w, w)], 1, 1)
                + dot(r.v[rows], r.qkv[:, pl.ds(2 * w, w)], 1, 1))
        x = r.tokens[rows].astype(jnp.float32)
        r.tg[rows] += self.unnorm(grad, x, r.scal[rows, 0:1], 0)


class TailIns(NamedTuple):
    gu_hbm: object
    dn_hbm: object
    y_hbm: object
    dx_hbm: object
    h_hbm: object
    attended_hbm: object
    normed_hbm: object
    q_hbm: object
    k_hbm: object
    v_hbm: object
    hn_hbm: object
    tokens_hbm: object
    lse_hbm: object
    cot_hbm: object
    qkv_hbm: object
    rest_hbm: object
    scal_hbm: object
    rows_hbm: object
    segments: object
    padding: object
    cosine: object
    sine: object


class TailOuts(NamedTuple):
    layer_hbm: object
    gu_hbm_out: object
    dn_hbm_out: object
    tg: object
    prev_grad: object
    qkv_out: object
    out_out: object
    small_out: object


def expert_items(spot, chunks, r):
    wide, half = r.gu_src.shape[2] // chunks, r.dn_src.shape[1] // 2
    items, outs = [], []
    for p, xf in ((0, True), (1, False)):
        one, two = (r.d1a, r.d2a) if p == 0 else (r.d1b, r.d2b)
        items.append(Reduce(spot, p, lambda o, p=p: r.dn_src.at[o, pl.ds(p * half, half)], one, two,
                            r.e_sends, r.e_r1, r.e_r2, xf))
        outs.append((r.dn_out, r.dn_hbm_out.at[pl.ds(p * half, half)]))
    for c in range(chunks):
        cut = pl.ds(c * wide, wide)
        items.append(Reduce(spot, 2 + c, lambda o, cut=cut: r.gu_src.at[o, :, cut], r.g1.at[c], r.g2.at[c],
                            r.e_sends, r.e_r1, r.e_r2, True))
        outs.append((r.gu_out, r.gu_hbm_out.at[:, cut]))
    stored = {}
    def finish(n):
        stage, out = outs[n]
        kind = min(n, 2) // 2
        if kind in stored:
            stored[kind].wait()
        items[n].finish(stage)
        stored[kind] = pltpu.make_async_copy(stage, out, r.local.at[kind])
        stored[kind].start()
    lists = [item.phase_two() for item in items]
    events = []
    for n in range(len(items) + 1):
        if n < len(items):
            events += lists[n][: len(lists[n]) // 2]
        if n > 0:
            events += lists[n - 1][len(lists[n - 1]) // 2 :]
        if n > 1:
            events.append(functools.partial(finish, n - 2))
    events.append(functools.partial(finish, len(items) - 1))
    return items, events, stored


class ExpertIns(NamedTuple):
    gu_hbm: object
    dn_hbm: object


class ExpertOuts(NamedTuple):
    gu_hbm_out: object
    dn_hbm_out: object


class ExpertScratch(NamedTuple):
    gu_src: object
    dn_src: object
    gu_out: object
    dn_out: object
    g1: object
    g2: object
    d1a: object
    d2a: object
    d1b: object
    d2b: object
    e_sends: object
    e_r1: object
    e_r2: object
    local: object


def load_experts(chunks, r):
    loads = [pltpu.make_async_copy(r.dn_hbm, r.dn_src, r.local.at[3])]
    wide = r.gu_src.shape[2] // chunks
    for c in range(chunks):
        cut = pl.ds(c * wide, wide)
        loads.append(pltpu.make_async_copy(r.gu_hbm.at[:, :, cut], r.gu_src.at[:, :, cut], r.local.at[4 + c]))
    for l in loads:
        l.start()
    return loads


def start_experts(items, loads):
    for n, item in enumerate(items):
        if n != 1:
            loads[max(n - 1, 0)].wait()
        for step in item.phase_one():
            step()


def expert_kernel(sizes, chunks, *refs):
    r = SimpleNamespace(**dict(zip(ExpertIns._fields + ExpertOuts._fields + ExpertScratch._fields, refs)))
    spot = Spot(sizes)
    loads = load_experts(chunks, r)
    enter(spot, line_neighbours(spot))
    items, events, stored = expert_items(spot, chunks, r)
    start_experts(items, loads)
    for event in events:
        event()
    for copy in stored.values():
        copy.wait()
    for item in items:
        for drain in item.drains:
            drain()


def expert_scratch(sizes, gu, dn, chunks):
    nz, nx = sizes[:2]
    n_dp, big = nz * nx, max(nz, nx)
    bf, f4 = jnp.bfloat16, jnp.float32
    V, dma = pltpu.VMEM, pltpu.SemaphoreType.DMA
    rows, rows_d, width = gu.shape[1], dn.shape[1], dn.shape[2]
    wide, tall = gu.shape[2] // chunks, rows_d // 2
    sx, sz = Reduce.slots(nx), Reduce.slots(nz)
    items = 2 + chunks
    out = dict(gu_src=V(gu.shape, bf), dn_src=V(dn.shape, bf), gu_out=V((rows, wide), f4), dn_out=V((tall, width), f4),
               g1=V((chunks, sx, nz, rows, wide), bf), g2=V((chunks, sz, rows, wide), bf),
               d1a=V((sx, nz, tall, width), bf), d2a=V((sz, tall, width), bf),
               d1b=V((sz, nx, tall, width), bf), d2b=V((sx, tall, width), bf),
               e_sends=dma((items, n_dp)), e_r1=dma((items, big + 1, big)), e_r2=dma((items, big + 1)))
    shapes = (jax.ShapeDtypeStruct((rows, gu.shape[2]), f4), jax.ShapeDtypeStruct((rows_d, width), f4))
    return out, shapes


def reduce_experts(sizes, gu, dn, chunks=4):
    scratch, shapes = expert_scratch(sizes, gu, dn, chunks)
    scratch["local"] = pltpu.SemaphoreType.DMA((4 + chunks,))
    hbm = pl.BlockSpec(memory_space=pl.ANY)
    return pl.pallas_call(
        functools.partial(expert_kernel, sizes, chunks),
        out_shape=shapes, in_specs=[hbm] * 2, out_specs=(hbm,) * 2,
        scratch_shapes=[scratch[n] for n in ExpertScratch._fields],
        compiler_params=pltpu.CompilerParams(collective_id=3, has_side_effects=True, vmem_limit_bytes=60 << 20),
        name="experts",
    )(gu, dn)


def tail_kernel(sizes, experts, chunks, together, names, *refs):
    r = SimpleNamespace(**dict(zip(names, refs)))
    first = pl.ds(0, r.cot.shape[0])
    r.ag, r.dh, r.normed = r.y.at[first], r.ag_, r.dx.at[first]
    r.attended = r.nt = r.layer_out
    r.tokens, r.lse = r.hn, r.dq
    spot = Spot(sizes)
    tail = Tail(spot, experts, r)
    loads = {}
    def load(src, dst):
        copy = pltpu.make_async_copy(src, dst, r.local.at[4 + chunks + len(loads)])
        copy.start()
        loads[id(dst)] = copy
        return copy
    if together:
        loads_e = load_experts(chunks, r)
    capacity = r.y.shape[0] // experts
    own = slots_of(r.y_hbm, capacity), slots_of(r.dx_hbm, capacity)
    mine = slots_of(r.y, capacity)(spot.ex), slots_of(r.dx, capacity)(spot.ex)
    firsts = [load(own[n](spot.ex), mine[n]) for n in range(2)]
    firsts += [load(*p) for p in ((r.lse_hbm, r.lse), (r.h_hbm, r.tg), (r.hn_hbm, r.hn), (r.cot_hbm, r.cot),
                                  (r.rest_hbm, r.rest), (r.scal_hbm, r.scal), (r.rows_hbm, r.rows))]
    seconds = [load(*p) for p in ((r.q_hbm, r.q), (r.k_hbm, r.k), (r.v_hbm, r.v), (r.qkv_hbm, r.qkv))]
    enter(spot, line_neighbours(spot)
          + [(None, expert_device(spot, lax.rem(spot.ex + d, experts))) for d in range(1, experts)])
    target = lambda at: lambda d: at(lax.rem(spot.ex + d, experts))
    returns = [Exchange(spot, experts, n, target(own[n]), slots_of(into, capacity), r.trade)
               for n, into in enumerate((r.y, r.dx))]
    for t in returns:
        for d in range(1, experts):
            t.send(d)
    items, events, stored = [], [], {}
    if together:
        items, events, stored = expert_items(spot, chunks, r)
        start_experts(items, loads_e)
    sems = (r.sends, r.r1, r.r2, r.mates, r.ys, r.outs)
    dense = []
    rounds = tail.pairs // 2
    for j in range(rounds + 1):
        def done(h, v, j=j):
            if j == rounds:
                r.out_out[:, pl.ds(h * v.shape[1], v.shape[1])] = v
            else:
                for part in range(3):
                    cols = pl.ds(part * tail.width + (h * rounds + j) * 128, 128)
                    r.qkv_out[:, cols] = v[:, part * 128 : part * 128 + 128]
        bufs = [b.at[j] for b in (r.mine, r.one, r.two, r.ybuf, r.final, r.other)]
        dense.append(Dense(spot, j, r.own.at[j], bufs, sems, done))
    def done(h, v):
        r.small_out[:, pl.ds(h * 128, 128)] = v
    bufs = [r.mine_s, r.one_s, r.two_s, r.ybuf_s, r.final_s, r.other_s]
    dense.append(Dense(spot, rounds + 1, r.own_small, bufs, sems, done))
    part = functools.partial
    def arrived():
        for copy in firsts:
            copy.wait()
    def returned():
        for t in returns:
            for d in range(1, experts):
                t.receive(d)
    work = [arrived, tail.prepare, returned]
    work += [part(tail.combine, i) for i in range(tail.blocks)]
    thirds = []
    def load_more():
        seconds.append(load(r.normed_hbm, r.normed))
        copy = pltpu.make_async_copy(r.layer_out, r.layer_hbm, r.local.at[2])
        copy.start()
        copy.wait()
        thirds.append(load(r.attended_hbm, r.attended))
    work.append(load_more)
    work += [part(tail.unproject, i) for i in range(tail.blocks)]
    def outs_of():
        thirds.pop().wait()
        tail.out_grad()
        dense[rounds].begin()
    work.append(outs_of)
    def smalls():
        tail.small_grad()
        thirds.append(load(r.tokens_hbm, r.tokens))
    work.append(smalls)
    def ready():
        for copy in seconds:
            copy.wait()
        tail.normed_side()
    work.append(ready)
    later = {0: [dense[rounds].merge], }
    for j in range(rounds):
        for pair in (j, rounds + j):
            work.append(part(tail.pair_begin, pair))
            work += [part(tail.attend, pair, i) for i in range(tail.blocks)]
            work.append(part(tail.pair_end, pair))
        work.append(dense[j].begin)
        if j < rounds - 1:
            work.append(dense[j].merge)
        if j == 0:
            work.append(dense[rounds].merge)
    woven(work, events[: len(events) * EARLY // 8])
    rest = events[len(events) * EARLY // 8 :]
    thirds.pop().wait()
    woven([dense[rounds - 1].merge] + [part(tail.last, i) for i in range(tail.blocks)] + [tail.small_end, dense[-1].begin, dense[-1].merge], rest)
    stages = [d.steps()[1:] for d in dense]
    for level in range(max(map(len, stages))):
        for st in stages:
            if level < len(st):
                st[level]()
    for copy in stored.values():
        copy.wait()
    for t in returns:
        for d in range(1, experts):
            t.drain(d)
    for item in items + dense + [d.reduce for d in dense]:
        for drain in item.drains:
            drain()


def run_tail(sizes, experts, ins, routes_width, chunks=4):
    by = TailIns(*ins)
    nz, nx, ny = sizes[:3]
    n_dp = nz * nx
    length, width = by.cot_hbm.shape
    rows = by.gu_hbm.shape[1]
    slots = by.y_hbm.shape[0]
    assert length == width
    together = n_dp <= 8
    bf, f4 = jnp.bfloat16, jnp.float32
    S, V, dma = jax.ShapeDtypeStruct, pltpu.VMEM, pltpu.SemaphoreType.DMA
    e_scratch, e_shapes = expert_scratch(sizes, by.gu_hbm, by.dn_hbm, chunks)
    shapes = dict(layer_hbm=S((length, width), bf), tg=S((length, width), f4), prev_grad=S((length, routes_width), f4),
                  qkv_out=S((rows, 3 * width), f4), out_out=S((rows, width), f4), small_out=S((rows, 256), f4))
    shapes.update(zip(ExpertOuts._fields, e_shapes))
    kinds = width // 256 + 1
    token, back, pair = V((length, width), bf), V((slots, width), bf), V((length, 128), f4)
    keys = sum(key_range(i)[1] - key_range(i)[0] for i in range(length // BLOCK))
    sx, sz = Reduce.slots(nx), Reduce.slots(nz)
    big = max(nz, nx)
    def buffers(end, lead, cols):
        block = (rows, cols)
        sizes_ = ((n_dp,), (sx, nz), (sz,), (ny,), (), ())
        names = ("mine", "one", "two", "ybuf", "final", "other")
        return {n + end: V(lead + s + block, f4 if j > 3 else bf) for j, (n, s) in enumerate(zip(names, sizes_))}
    scratch = dict(y=back, dx=back, ag_=token, hn=token, q=token, k=token, v=token, layer_out=token,
                   low=V((length, 128), bf), coef=V((length, 128), bf), gain_rows=V((8, width), f4),
                   lse_rows=V((16, length), f4), bias=V((keys, BLOCK), bf), kt=V((128, length), bf), dq=pair, dk=pair,
                   dv=pair, own=V((kinds, 2, n_dp, rows, width // 2), bf), own_small=V((2, n_dp, rows, 128), bf),
                   cot=token, qkv=V(by.qkv_hbm.shape, bf), rest=V(by.rest_hbm.shape, bf), scal=pair,
                   rows=V(by.rows_hbm.shape, f4), trade=dma((2, 2, experts)))
    scratch.update(buffers("", (kinds,), width // 2))
    scratch.update(buffers("_s", (), 128))
    scratch.update(sends=dma((kinds + 1, n_dp)), r1=dma((kinds + 1, big + 1, big)), r2=dma((kinds + 1, big + 1)),
                   mates=dma((2, kinds + 1)), ys=dma((2, kinds + 1, ny)), outs=dma((2, kinds + 1)), local=dma((24 + chunks,)))
    if together:
        scratch.update(e_scratch)
    in_names = [n for n in TailIns._fields if together or n not in ExpertIns._fields]
    out_names = [n for n in TailOuts._fields if together or n not in ExpertOuts._fields]
    vmem = pl.BlockSpec(memory_space=pltpu.VMEM)
    hbm = pl.BlockSpec(memory_space=pl.ANY)
    place = lambda names: [hbm if "hbm" in n else vmem for n in names]
    outs = pl.pallas_call(
        functools.partial(tail_kernel, sizes, experts, chunks, together, in_names + out_names + list(scratch)),
        out_shape=tuple(shapes[n] for n in out_names),
        in_specs=place(in_names),
        out_specs=tuple(place(out_names)),
        scratch_shapes=list(scratch.values()),
        compiler_params=pltpu.CompilerParams(collective_id=2, has_side_effects=True, vmem_limit_bytes=67_000_000),
        name="tail",
    )(*(getattr(by, n) for n in in_names))
    out = dict(zip(out_names, outs))
    if not together:
        out.update(zip(ExpertOuts._fields, reduce_experts(sizes, by.gu_hbm, by.dn_hbm, chunks)))
    return [out[n] for n in TailOuts._fields]


def pair_tables(length):
    half = HEAD_DIM // 2
    inverse = np.float32(10000.0) ** (-(np.arange(half, dtype=np.float32) / np.float32(half)))
    angles = (np.arange(length, dtype=np.float32)[:, None] * inverse[None]).astype(np.float64)
    cosine, sine = np.cos(angles).astype(np.float32), np.sin(angles).astype(np.float32)
    return jnp.asarray(np.tile(cosine, (1, 4))), jnp.asarray(np.tile(np.concatenate([-sine, sine], 1), (1, 2)))


def per_device(
    sizes,
    tokens,
    prev_logits,
    segment_ids,
    pad_mask,
    routes,
    slot_order,
    cotangent,
    attn_gain,
    qkv_weight,
    out_weight,
    ffn_gain,
    router_weight,
    mix_weight,
    const_weight,
    gate_up_weight,
    down_weight,
):
    length, width = tokens.shape
    experts = lax.axis_size("expert") * gate_up_weight.shape[0]
    choices = router_weight.shape[1]
    n_dp = sizes[0] * sizes[1]
    small = jnp.concatenate(
        [attn_gain[:, None], ffn_gain[:, None], mix_weight, const_weight, router_weight], axis=1
    )
    rest = jnp.concatenate([out_weight, jnp.pad(small, ((0, 0), (0, 256 - small.shape[1])))], axis=1)
    cosine, sine = pair_tables(length)
    pairs = routes[0]
    f = FrontOuts(*run_front(
        sizes, experts,
        (tokens, prev_logits, segment_ids, pad_mask, pairs, slot_order.reshape(length, 2), cotangent,
         cosine, sine, qkv_weight, rest, gate_up_weight[0], down_weight[0])))
    by_owner = lambda g: g.reshape(n_dp, g.shape[0] // n_dp, g.shape[1])
    layer_out, gu_shard, dn_shard, tokens_grad, prev_grad, qkv_grad, out_grad, small_grad = run_tail(
        sizes, experts,
        (by_owner(f.gu_grad), by_owner(f.dn_grad), f.y_hbm, f.dx_hbm, f.h_hbm, f.attended_hbm, f.normed_hbm, f.q_hbm, f.k_hbm,
         f.v_hbm, f.hn_hbm, tokens, f.lse_hbm, cotangent, f.qkv_hbm, f.rest_hbm, f.scal_hbm, f.rows_hbm, segment_ids,
         pad_mask, cosine, sine), choices)
    return (
        layer_out,
        tokens_grad,
        prev_grad,
        small_grad[:, 0],
        qkv_grad,
        out_grad,
        small_grad[:, 1],
        small_grad[:, 8 : 8 + choices],
        small_grad[:, 2:6],
        small_grad[:, 6:8],
        gu_shard[None],
        dn_shard[None],
    )


def grid_sizes(mesh):
    along_dp, along_expert = mesh.devices[:, 0], mesh.devices[0]
    nx = len({d.coords[0] for d in along_dp})
    ny = len({d.coords[1] for d in along_expert})
    return (len(along_dp) // nx, nx, ny, len(along_expert) // ny)


def solution(mesh):
    in_specs = (
        P(("dp", "expert"), None),
        P(("dp", "expert"), None),
        P(("dp", "expert"), None),
        P(("dp", "expert"), None),
        P(("dp", "expert"), None, None),
        P(("dp", "expert"), None),
        P(("dp", "expert"), None),
        P("dp"),
        P("dp", None),
        P("dp", None),
        P("dp"),
        P("dp", None),
        P("dp", None),
        P("dp", None),
        P("expert", "dp", None),
        P("expert", "dp", None),
    )
    out_specs = (
        P(("dp", "expert"), None),
        P(("dp", "expert"), None),
        P(("dp", "expert"), None),
        P("dp"),
        P("dp", None),
        P("dp", None),
        P("dp"),
        P("dp", None),
        P("dp", None),
        P("dp", None),
        P("expert", "dp", None),
        P("expert", "dp", None),
    )
    return jax.shard_map(
        functools.partial(per_device, grid_sizes(mesh)), mesh=mesh, in_specs=in_specs, out_specs=out_specs, check_vma=False
    )
```

time: 609 us -> 358 us (0.59)
  matrix products: 137 us -> 0 us
  other arithmetic: 73.2 us -> 2.32 us
  local copies, waits for them, and re-layouts: 74.3 us -> 22.3 us
  Pallas kernels: 308 us -> 327 us
  starting transfers between devices: 9.31 us -> 0 us
    dot_general x22 -> x0, matrix products: 137 us -> none  [the longest x1 23.6 us: backward_block(): jnp.einsum('qhd,khd->hqk', attended_grad, value_rows, preferred_element_t...]
    convert_element_type x5 -> x0, other arithmetic: 29 us -> none  [the longest x1 23.4 us: backward_block(): score_grad = (probs_full * (prob_grad - row_dot)).astype(jnp.bfloat16)]
    reduce_sum x7 -> x0, other arithmetic: 26.2 us -> none  [the longest x1 13.6 us: per_device(): grad_dot_pairs = jnp.sum(out_grad[:, None, :] * pair_rows, axis=-1)]
    pallas_call x1, Pallas kernels: 138 us -> 155 us  [run_front(): pl.pallas_call(functools.partial(front_kernel, sizes, experts, chunks), o...]
    convert_element_type x2 -> x0, local copies, waits for them, and re-layouts: 12.5 us -> none  [the longest x1 6.34 us: per_device(): back_padded[flat_slot].astype(jnp.float32).reshape(length, 2, width)]
    gather x2 -> x0, local copies, waits for them, and re-layouts: 11.4 us -> none  [the longest x1 5.75 us: per_device(): returned_rows[flat_slot].astype(jnp.float32).reshape(length, 2, width)]
    all_to_all x2 -> x0, starting transfers between devices: 9.31 us -> none  [the longest x1 4.7 us: per_device(): lax.all_to_all(input_grad_rows.reshape(received.shape), 'expert', split_a...]
    pallas_call x3 -> x0, local copies, waits for them, and re-layouts: 6.77 us -> none  [run_front(): pl.pallas_call(functools.partial(front_kernel, sizes, experts, chunks), o...]
  transfers between devices with their start and end apart: 2 -> 0, of which waited for: 0 -> 0; matrix products, arithmetic and copies ran while one was open for 18% -> 0% of each run, Pallas kernels for 19% -> 0%
where the time goes in v3:
time: 358 us; the launch traced here: 353 us
  Pallas kernels  327 us (91%)
  local copies, waits for them, and re-layouts  22.3 us (6%)
    pallas_call x1, Pallas kernels, run_tail(): pl.pallas_call(functools.partial(tail_kernel, sizes, experts, chunks, tog...  173 us
    pallas_call x1, Pallas kernels, run_front(): pl.pallas_call(functools.partial(front_kernel, sizes, experts, chunks), o...  155 us
    unnamed x22, local copies, waits for them, and re-layouts  15.4 us

profile of v3, /device:TPU:0, one launch (start us, length us, event | category | flops | bytes accessed | tf_op | source)
XLA Modules:
  0.0 352.8 jit_solution(4740319997777923041)
XLA Ops:
  0.6 1.4 concatenate.6
  2.1 0.7 reduce
  2.8 0.1 copy.53
  2.9 1.6 fusion.1.refs_10_
  4.5 1.5 copy.54.refs_1_
  6.0 1.1 reshape.33.refs_5_
  7.1 1.6 copy.52
  8.7 154.6 %front.1 = (bf16[768,4096]{1,0:T(8,128)(2,1)}, bf16[2048,768]{1,0:T(8,128)(2,1)}, bf16[768,2304]{1,0:T(8,128)(2,1)}, bf16[768,1024]{1,0:T(8,128)(2,1)}, bf16[768...) custom-call(bf16[768,768]{1,0:T(8,128)(2,1)} %refs_11_.1, ...), custom_call_target="tpu_custom_call" | custom-call | tf_op jit(solution)/shard_map/front/pallas_call | solution.py:643
  163.4 172.7 %tail.1 = (bf16[768,768]{1,0:T(8,128)(2,1)}, f32[96,4096]{1,0:T(8,128)}, f32[256,768]{1,0:T(8,128)}, f32[768,768]{1,0:T(8,128)}, f32[768,8]{1,0:T(8,128)}, /*ind...) custom-call(bf16[8,96,4096]{2,1,0:T(8,128)(2,1)} %bitcast.9, bf16[8,256,768]{2,1,0:T(8,128)(2,1)} %bitcast.10, ...), custom_call_target="tpu_custom_call" | custom-call | tf_op jit(solution)/shard_map/tail/pallas_call | solution.py:1327
  336.1 1.6 slice_reduce_fusion
  337.7 1.7 copy.55
  339.4 0.9 slice.18
  340.3 0.7 copy.57
  340.9 0.9 slice.17
  341.8 0.9 slice.19
  342.7 0.6 copy.58
  343.3 0.7 copy.56
  344.0 0.0 copy-start
  344.0 2.5 copy.65
  346.5 0.0 copy-done
  346.5 0.0 copy-start.2
  346.5 0.0 copy-start.4
  346.5 1.4 copy.66
  347.9 0.4 copy-done.2
  348.3 0.0 copy-start.1
  348.3 0.9 copy.67
  349.2 0.0 copy-done.4
  349.2 0.7 copy.68
  349.9 0.1 copy-done.1
  350.1 1.1 copy.69
  351.2 0.5 copy-done.3
  351.7 0.9 copy.70
  (1 shorter events, 0.0 us)
Async XLA Ops:
  344.0 2.5 copy-start
  346.5 1.8 copy-start.2
  346.5 2.7 copy-start.4
  348.3 1.8 copy-start.1
  350.0 1.7 copy-start.3

commit v4 on v3

--- a/solution.py
+++ b/solution.py
@@ -15,7 +15,7 @@
 LONGEST = 384
 LEVEL_STEP = 2.5
 LEAD = 4.0
-EARLY = 5
+FIRST, EACH, LEVEL_GAP, PAIR, DENSE_EACH, HOP = 8.0, 17.0, 7.0, 8.0, 6.0, 4.0
 SHARE = 7
 epsilon = 1e-06
 
@@ -369,11 +369,11 @@
 
     def down_grad(self, j):
         r, w = self.r, self.wide
-        r.dn[pl.ds(j * w, w)] = dot(r.act[:, pl.ds(j * w, w)], r.gin[...], 0, 0).astype(jnp.bfloat16)
-
-    def up_grad(self, j):
+        r.dn_stage[j % 2] = dot(r.act[:, pl.ds(j * w, w)], r.gin[...], 0, 0).astype(jnp.bfloat16)
+
+    def up_grad(self, j, n):
         r, w = self.r, self.wide
-        r.gu[:, pl.ds(j * w, w)] = dot(r.xt[...], r.pg[:, pl.ds(j * w, w)]).astype(jnp.bfloat16)
+        r.gu_stage[n] = dot(r.xt[...], r.pg[:, pl.ds(j * w, w)]).astype(jnp.bfloat16)
 
 
 def expert_device(spot, e):
@@ -455,6 +455,8 @@
 
 
 class FrontScratch(NamedTuple):
+    dn_stage: object
+    gu_stage: object
     qkv: object
     rest: object
     q: object
@@ -570,11 +572,13 @@
         out += [t[3] for t in keyed[: last + 1]]
         del keyed[: last + 1]
         return out
-    saves = []
+    saves, number = [], []
     def save(src, dst):
-        copy = pltpu.make_async_copy(src, dst, r.local.at[len(keeps) + len(saves)])
+        number.append(0)
+        copy = pltpu.make_async_copy(src, dst, r.local.at[len(keeps) + len(number)])
         copy.start()
         saves.append(copy)
+        return copy
     def save_dense():
         for src, dst in ((r.qkv, r.qkv_hbm), (r.rest, r.rest_hbm), (r.q, r.q_hbm), (r.k, r.k_hbm), (r.v, r.v_hbm),
                          (r.normed, r.normed_hbm), (r.attended, r.attended_hbm), (r.lse, r.lse_hbm), (r.rows, r.rows_hbm),
@@ -593,6 +597,21 @@
     keeps[2].wait()
     keeps[3].wait()
     front.side_rows()
+    staged = {}
+    def stage(key, src, dst):
+        staged[key] = save(src, dst)
+    def grads(c):
+        for key in (c % 2, 2 + (c % 2) * 2, 3 + (c % 2) * 2):
+            if key in staged:
+                old = staged.pop(key)
+                saves[:] = [s for s in saves if s is not old]
+                old.wait()
+        front.down_grad(c)
+        stage(c % 2, r.dn_stage.at[c % 2], r.dn_grad.at[pl.ds(c * wide, wide)])
+        for j in (c, chunks + c):
+            n = (c % 2) * 2 + j // chunks
+            front.up_grad(j, n)
+            stage(2 + n, r.gu_stage.at[n], r.gu_grad.at[:, pl.ds(j * wide, wide)])
     for c in range(chunks):
         for event in upto(2 + 2 * c + 1):
             event()
@@ -600,6 +619,7 @@
         keeps[5 + 2 * c].wait()
         for p in range(2):
             front.hidden(c, p)
+        grads(c)
     for p in range(2):
         front.outward(p)
     save(r.yall, r.y_hbm)
@@ -609,12 +629,6 @@
     for f in floods:
         for drain in f.drains:
             drain()
-    for c in range(chunks):
-        front.down_grad(c)
-        save(r.dn.at[pl.ds(c * wide, wide)], r.dn_grad.at[pl.ds(c * wide, wide)])
-    for c in range(2 * chunks):
-        front.up_grad(c)
-        save(r.gu.at[:, pl.ds(c * wide, wide)], r.gu_grad.at[:, pl.ds(c * wide, wide)])
     for d in range(1, experts):
         for t in trades:
             t.drain(d)
@@ -627,7 +641,7 @@
     length, width = tokens.shape
     n_dp = sizes[0] * sizes[1]
     capacity = 2 * length // (experts + 4)
-    slots = experts * capacity
+    slots, ff = experts * capacity, gu.shape[1] // 2
     bf, f4 = jnp.bfloat16, jnp.float32
     S, V = jax.ShapeDtypeStruct, pltpu.VMEM
     token = S((length, width), bf)
@@ -645,7 +659,7 @@
         out_shape=tuple(outs),
         in_specs=[vmem] * 13,
         out_specs=(hbm,) * len(outs),
-        scratch_shapes=[V(o.shape, o.dtype) for o in outs[2:14]] + [
+        scratch_shapes=[V((2, ff // chunks, width), bf), V((4, width, ff // chunks), bf)] + [V(o.shape, o.dtype) for o in outs[2:14]] + [
             V(gu_all, bf), V(dn_all, bf), V((slots, width), bf), V((slots, width), bf), V((width, slots), bf),
             V((slots, dn_all[0]), bf), V((slots, gu_all[1]), bf), V((slots, width), bf), V((slots, width), bf),
             V((8, length), f4), V((length, BLOCK + LONGEST), f4), V((2, length, width), bf), send, send,
@@ -734,22 +748,25 @@
             self.take(cond, o, self.one.at[slot, q], self.recv_one.at[self.n, slot, q])
 
     def phase_two(self):
-        steps = []
-        for turn in range(2):
-            sign = jnp.where(self.q * 2 < self.nq, 1, -1) * (1 if turn == 0 else -1)
-            for k in range(self.nq - 1, 0, -1):
-                def step(sign=sign, k=k):
-                    q = self.q + sign * k
-                    here = between(q, self.nq)
-                    o = self.owner(self.p, q)
-                    self.settle(here, q)
-                    behind = jnp.logical_and(here, between(self.q - sign, self.nq))
-                    if self.nq > 2:
-                        self.take(behind, o, self.two.at[q], self.recv_two.at[self.n, q])
-                    slot = self.slot(self.nq, q, jnp.logical_and(k == 1, sign < 0))
-                    self.push(here, o, self.two.at[slot], self.recv_two.at[self.n, slot], self.along(False, self.q + sign))
-                steps.append(step)
-        return steps
+        def step(sign, k, now):
+            q = self.q + sign * k
+            here = jnp.logical_and(now, between(q, self.nq))
+            o = self.owner(self.p, q)
+            self.settle(here, q)
+            behind = jnp.logical_and(here, between(self.q - sign, self.nq))
+            if self.nq > 2:
+                self.take(behind, o, self.two.at[q], self.recv_two.at[self.n, q])
+            slot = self.slot(self.nq, q, jnp.logical_and(k == 1, sign < 0))
+            self.push(here, o, self.two.at[slot], self.recv_two.at[self.n, slot], self.along(False, self.q + sign))
+        levels = []
+        for level in range(self.nq - 1):
+            up, down = self.q == level, self.nq - 1 - self.q == level
+            if self.nq % 2 == 0:
+                ways = [(jnp.where(up, 1, -1), jnp.logical_or(up, down))]
+            else:
+                ways = [(jnp.int32(1), up), (jnp.int32(-1), down)]
+            levels.append([functools.partial(step, sign, k, now) for sign, now in ways for k in range(self.nq - 1, 0, -1)])
+        return levels
 
     def finish(self, out):
         o = self.owner(self.p, self.q)
@@ -833,7 +850,9 @@
             pl.when(self.spot.core != half)(lambda half=half: self.done(half, self.other[...]))
 
     def steps(self):
-        return [self.merge] + self.reduce.phase_two() + [self.settle, self.total, self.end]
+        out = [(HOP * (n + 1), f) for n, fs in enumerate(self.reduce.phase_two()) for f in fs]
+        end = HOP * self.reduce.nq
+        return out + [(end, self.settle), (end + 3, self.total), (end + 5, self.end)]
 
 
 class Tail:
@@ -863,9 +882,10 @@
 
     def combine(self, i):
         r, w, e = self.r, self.width, self.experts
-        rows = pl.ds(i * BLOCK, BLOCK)
+        tile = BLOCK // 2
+        rows = pl.ds(i * tile, tile)
         col = lambda j: r.scal[rows, j : j + 1]
-        slot = lax.broadcasted_iota(jnp.int32, (BLOCK, r.y.shape[0]), 1).astype(jnp.float32)
+        slot = lax.broadcasted_iota(jnp.int32, (tile, r.y.shape[0]), 1).astype(jnp.float32)
         at = [jnp.where(col(8 + k) == slot, 1.0, 0.0).astype(jnp.bfloat16) for k in range(2)]
         pair = [dot(at[k], r.y[...]) for k in range(2)]
         routed = dot(at[0] + at[1], r.dx[...])
@@ -889,9 +909,9 @@
                  + fixed[k][0] * mix[0][1] * with_const[0] + fixed[k][1] * mix[1][1] * with_const[1] for k in range(2)]
         mean = gates[0] * grads[0] + gates[1] * grads[1]
         picked = [gates[k] * (grads[k] - mean) for k in range(2)]
-        lane = lax.broadcasted_iota(jnp.int32, (BLOCK, r.prev_grad.shape[1]), 1).astype(jnp.float32)
+        lane = lax.broadcasted_iota(jnp.int32, (tile, r.prev_grad.shape[1]), 1).astype(jnp.float32)
         r.prev_grad[rows] = jnp.where(lane == route[0], picked[0], 0.0) + jnp.where(lane == route[1], picked[1], 0.0)
-        lane = lax.broadcasted_iota(jnp.int32, (BLOCK, 128), 1).astype(jnp.float32)
+        lane = lax.broadcasted_iota(jnp.int32, (tile, 128), 1).astype(jnp.float32)
         low = jnp.where(lane == route[0] + 8, picked[0], 0.0) + jnp.where(lane == route[1] + 8, picked[1], 0.0)
         for j in range(2):
             g = [chosen[j] * with_hn, chosen[j] * with_const[j]]
@@ -1061,16 +1081,19 @@
         items[n].finish(stage)
         stored[kind] = pltpu.make_async_copy(stage, out, r.local.at[kind])
         stored[kind].start()
-    lists = [item.phase_two() for item in items]
     events = []
-    for n in range(len(items) + 1):
-        if n < len(items):
-            events += lists[n][: len(lists[n]) // 2]
-        if n > 0:
-            events += lists[n - 1][len(lists[n - 1]) // 2 :]
-        if n > 1:
-            events.append(functools.partial(finish, n - 2))
-    events.append(functools.partial(finish, len(items) - 1))
+    place = 0
+    for n, item in enumerate(items):
+        if item.x_first:
+            place += 1
+        else:
+            events += [(8 + 0.8 * j, step) for j, step in enumerate(item.phase_one())]
+        at = FIRST + EACH * (place if item.x_first else len(items) - 1)
+        levels = item.phase_two()
+        for level, steps in enumerate(levels):
+            events += [(at + LEVEL_GAP * level, step) for step in steps]
+        events.append((at + LEVEL_GAP * len(levels), functools.partial(finish, n)))
+    events.sort(key=lambda t: t[0])
     return items, events, stored
 
 
@@ -1116,8 +1139,9 @@
     for n, item in enumerate(items):
         if n != 1:
             loads[max(n - 1, 0)].wait()
-        for step in item.phase_one():
-            step()
+        if item.x_first:
+            for step in item.phase_one():
+                step()
 
 
 def expert_kernel(sizes, chunks, *refs):
@@ -1127,7 +1151,7 @@
     enter(spot, line_neighbours(spot))
     items, events, stored = expert_items(spot, chunks, r)
     start_experts(items, loads)
-    for event in events:
+    for _, event in events:
         event()
     for copy in stored.values():
         copy.wait()
@@ -1172,14 +1196,14 @@
     first = pl.ds(0, r.cot.shape[0])
     r.ag, r.dh, r.normed = r.y.at[first], r.ag_, r.dx.at[first]
     r.attended = r.nt = r.layer_out
-    r.tokens, r.lse = r.hn, r.dq
+    r.tokens, r.lse, r.q = r.hn, r.dq, r.cot
     spot = Spot(sizes)
     tail = Tail(spot, experts, r)
-    loads = {}
+    loads = []
     def load(src, dst):
         copy = pltpu.make_async_copy(src, dst, r.local.at[4 + chunks + len(loads)])
         copy.start()
-        loads[id(dst)] = copy
+        loads.append(copy)
         return copy
     if together:
         loads_e = load_experts(chunks, r)
@@ -1189,7 +1213,7 @@
     firsts = [load(own[n](spot.ex), mine[n]) for n in range(2)]
     firsts += [load(*p) for p in ((r.lse_hbm, r.lse), (r.h_hbm, r.tg), (r.hn_hbm, r.hn), (r.cot_hbm, r.cot),
                                   (r.rest_hbm, r.rest), (r.scal_hbm, r.scal), (r.rows_hbm, r.rows))]
-    seconds = [load(*p) for p in ((r.q_hbm, r.q), (r.k_hbm, r.k), (r.v_hbm, r.v), (r.qkv_hbm, r.qkv))]
+    seconds = [load(*p) for p in ((r.k_hbm, r.k), (r.v_hbm, r.v), (r.qkv_hbm, r.qkv))]
     enter(spot, line_neighbours(spot)
           + [(None, expert_device(spot, lax.rem(spot.ex + d, experts))) for d in range(1, experts)])
     target = lambda at: lambda d: at(lax.rem(spot.ex + d, experts))
@@ -1227,51 +1251,60 @@
         for t in returns:
             for d in range(1, experts):
                 t.receive(d)
-    work = [arrived, tail.prepare, returned]
-    work += [part(tail.combine, i) for i in range(tail.blocks)]
-    thirds = []
+    thirds, lasts = [], []
+    def smalls():
+        tail.small_grad()
+        seconds.append(load(r.q_hbm, r.q))
+        lasts.append(load(r.tokens_hbm, r.tokens))
     def load_more():
         seconds.append(load(r.normed_hbm, r.normed))
         copy = pltpu.make_async_copy(r.layer_out, r.layer_hbm, r.local.at[2])
         copy.start()
         copy.wait()
         thirds.append(load(r.attended_hbm, r.attended))
-    work.append(load_more)
-    work += [part(tail.unproject, i) for i in range(tail.blocks)]
     def outs_of():
         thirds.pop().wait()
         tail.out_grad()
         dense[rounds].begin()
-    work.append(outs_of)
-    def smalls():
-        tail.small_grad()
-        thirds.append(load(r.tokens_hbm, r.tokens))
-    work.append(smalls)
+    def lasts_ready():
+        lasts.pop().wait()
     def ready():
         for copy in seconds:
             copy.wait()
         tail.normed_side()
-    work.append(ready)
-    later = {0: [dense[rounds].merge], }
+    plan = []
+    def at(time, *pieces):
+        plan.extend((time, p) for p in pieces)
+    at(4, arrived, tail.prepare)
+    at(27, returned)
+    at(28, *[part(tail.combine, i) for i in range(2 * tail.blocks)])
+    at(37, smalls, load_more)
+    at(38, *[part(tail.unproject, i) for i in range(tail.blocks)])
+    at(40, outs_of, ready)
+    now = 42.0
+    at(now + 5, dense[rounds].merge)
+    due = [(now + 50, dense[rounds])]
     for j in range(rounds):
         for pair in (j, rounds + j):
-            work.append(part(tail.pair_begin, pair))
-            work += [part(tail.attend, pair, i) for i in range(tail.blocks)]
-            work.append(part(tail.pair_end, pair))
-        work.append(dense[j].begin)
-        if j < rounds - 1:
-            work.append(dense[j].merge)
-        if j == 0:
-            work.append(dense[rounds].merge)
-    woven(work, events[: len(events) * EARLY // 8])
-    rest = events[len(events) * EARLY // 8 :]
-    thirds.pop().wait()
-    woven([dense[rounds - 1].merge] + [part(tail.last, i) for i in range(tail.blocks)] + [tail.small_end, dense[-1].begin, dense[-1].merge], rest)
-    stages = [d.steps()[1:] for d in dense]
-    for level in range(max(map(len, stages))):
-        for st in stages:
-            if level < len(st):
-                st[level]()
+            at(now, part(tail.pair_begin, pair))
+            for i in range(tail.blocks):
+                at(now + 1 + 2 * i, part(tail.attend, pair, i))
+            at(now + PAIR - 0.5, part(tail.pair_end, pair))
+            now += PAIR
+        at(now - 0.4, dense[j].begin)
+        at(now + 3, dense[j].merge)
+        due.append((now + 3, dense[j]))
+    at(now, lasts_ready, *[part(tail.last, i) for i in range(tail.blocks)])
+    at(now + 7, tail.small_end, dense[-1].begin)
+    at(now + 9, dense[-1].merge)
+    due.append((now + 9, dense[-1]))
+    busy = FIRST + EACH * (len(items) - 1) if together else 0
+    for time, d in due:
+        busy = max(busy, time) + DENSE_EACH
+        plan += [(busy + after, step) for after, step in d.steps()]
+    plan += events
+    for _, piece in sorted(plan, key=lambda t: t[0]):
+        piece()
     for copy in stored.values():
         copy.wait()
     for t in returns:
@@ -1307,7 +1340,7 @@
         sizes_ = ((n_dp,), (sx, nz), (sz,), (ny,), (), ())
         names = ("mine", "one", "two", "ybuf", "final", "other")
         return {n + end: V(lead + s + block, f4 if j > 3 else bf) for j, (n, s) in enumerate(zip(names, sizes_))}
-    scratch = dict(y=back, dx=back, ag_=token, hn=token, q=token, k=token, v=token, layer_out=token,
+    scratch = dict(y=back, dx=back, ag_=token, hn=token, k=token, v=token, layer_out=token,
                    low=V((length, 128), bf), coef=V((length, 128), bf), gain_rows=V((8, width), f4),
                    lse_rows=V((16, length), f4), bias=V((keys, BLOCK), bf), kt=V((128, length), bf), dq=pair, dk=pair,
                    dv=pair, own=V((kinds, 2, n_dp, rows, width // 2), bf), own_small=V((2, n_dp, rows, 128), bf),
@@ -1337,6 +1370,45 @@
     if not together:
         out.update(zip(ExpertOuts._fields, reduce_experts(sizes, by.gu_hbm, by.dn_hbm, chunks)))
     return [out[n] for n in TailOuts._fields]
+
+
+def release_kernel(whole, *refs):
+    n = len(whole)
+    ins, small_ref, outs = refs[:n], refs[n], refs[n + 1 : 2 * n + 1]
+    gain_one, gain_two, router, mix, const = refs[2 * n + 1 : 2 * n + 6]
+    bufs, sems = refs[2 * n + 6 : 3 * n + 6], refs[3 * n + 6]
+    loads = [pltpu.make_async_copy(ins[j], bufs[j], sems.at[0, j]) for j in range(n)]
+    stores = [pltpu.make_async_copy(bufs[j], outs[j], sems.at[1, j]) for j in range(n)]
+    for l in loads:
+        l.start()
+    small = small_ref[...]
+    rows = small.shape[0]
+    eye = lax.broadcasted_iota(jnp.int32, (rows, rows), 0) == lax.broadcasted_iota(jnp.int32, (rows, rows), 1)
+    for j, out in enumerate((gain_one, gain_two)):
+        out[...] = jnp.sum(jnp.where(eye, small[:, j : j + 1], 0.0), axis=0, keepdims=True)
+    mix[...] = small[:, 2:6]
+    const[...] = small[:, 6:8]
+    router[...] = small[:, 8 : 8 + router.shape[1]]
+    for l, s in zip(loads, stores):
+        l.wait()
+        s.start()
+    for s in stores:
+        s.wait()
+
+
+def release(whole, small, choices):
+    n, rows = len(whole), small.shape[0]
+    S = lambda *shape: jax.ShapeDtypeStruct(shape, jnp.float32)
+    hbm, vmem = pl.BlockSpec(memory_space=pl.ANY), pl.BlockSpec(memory_space=pltpu.VMEM)
+    return pl.pallas_call(
+        functools.partial(release_kernel, tuple(a.shape for a in whole)),
+        out_shape=tuple(jax.ShapeDtypeStruct(a.shape, a.dtype) for a in whole)
+        + (S(1, rows), S(1, rows), S(rows, choices), S(rows, 4), S(rows, 2)),
+        in_specs=[hbm] * n + [vmem],
+        out_specs=(hbm,) * n + (vmem,) * 5,
+        scratch_shapes=[pltpu.VMEM(a.shape, a.dtype) for a in whole] + [pltpu.SemaphoreType.DMA((2, n))],
+        name="release",
+    )(*whole, small)
 
 
 def pair_tables(length):
@@ -1386,17 +1458,20 @@
         (by_owner(f.gu_grad), by_owner(f.dn_grad), f.y_hbm, f.dx_hbm, f.h_hbm, f.attended_hbm, f.normed_hbm, f.q_hbm, f.k_hbm,
          f.v_hbm, f.hn_hbm, tokens, f.lse_hbm, cotangent, f.qkv_hbm, f.rest_hbm, f.scal_hbm, f.rows_hbm, segment_ids,
          pad_mask, cosine, sine), choices)
+    layer_out, tokens_grad, prev_grad, qkv_grad, out_grad, gu_shard, dn_shard, *smalls = release(
+        (layer_out, tokens_grad, prev_grad, qkv_grad, out_grad, gu_shard, dn_shard), small_grad, choices)
+    gain_one, gain_two, router, mix, const = smalls
     return (
         layer_out,
         tokens_grad,
         prev_grad,
-        small_grad[:, 0],
+        gain_one[0],
         qkv_grad,
         out_grad,
-        small_grad[:, 1],
-        small_grad[:, 8 : 8 + choices],
-        small_grad[:, 2:6],
-        small_grad[:, 6:8],
+        gain_two[0],
+        router,
+        mix,
+        const,
         gu_shard[None],
         dn_shard[None],
     )

time: 358 us -> 348 us (0.972)
  local copies, waits for them, and re-layouts: 22.3 us -> 11.8 us
    pallas_call x0 -> x1, Pallas kernels: none -> 7.53 us  [release(): pl.pallas_call(functools.partial(release_kernel, tuple((a.shape for a in...]
    unnamed x22 -> x6, local copies, waits for them, and re-layouts: 15.4 us -> 9.22 us
    slice x4 -> x0, local copies, waits for them, and re-layouts: 4.21 us -> none  [the longest x1 1.58 us: per_device(): small_grad[:, 1]]
where the time goes in v4:
time: 348 us; the launch traced here: 343 us
  Pallas kernels  328 us (94%)
  local copies, waits for them, and re-layouts  11.8 us (3%)
    pallas_call x1, Pallas kernels, run_tail(): pl.pallas_call(functools.partial(tail_kernel, sizes, experts, chunks, tog...  170 us
    pallas_call x1, Pallas kernels, run_front(): pl.pallas_call(functools.partial(front_kernel, sizes, experts, chunks), o...  151 us
    unnamed x6, local copies, waits for them, and re-layouts  9.22 us
    pallas_call x1, Pallas kernels, release(): pl.pallas_call(functools.partial(release_kernel, tuple((a.shape for a in...  7.53 us

profile of v4, /device:TPU:0, one launch (start us, length us, event | category | flops | bytes accessed | tf_op | source)
XLA Modules:
  0.0 343.4 jit_solution(6075312122736658813)
XLA Ops:
  0.6 1.4 concatenate.6
  2.1 0.7 reduce
  2.8 0.1 copy.53
  2.9 1.6 fusion.1.refs_10_
  4.5 1.5 copy.54.refs_1_
  6.0 1.1 reshape.33.refs_5_
  7.1 1.6 copy.52
  8.7 151.1 %front.1 = (bf16[768,4096]{1,0:T(8,128)(2,1)}, bf16[2048,768]{1,0:T(8,128)(2,1)}, bf16[768,2304]{1,0:T(8,128)(2,1)}, bf16[768,1024]{1,0:T(8,128)(2,1)}, bf16[768...) custom-call(bf16[768,768]{1,0:T(8,128)(2,1)} %refs_11_.1, ...), custom_call_target="tpu_custom_call" | custom-call | tf_op jit(solution)/shard_map/front/pallas_call | solution.py:657
  159.8 169.8 %tail.1 = (bf16[768,768]{1,0:T(8,128)(2,1)}, f32[96,4096]{1,0:T(8,128)}, f32[256,768]{1,0:T(8,128)}, f32[768,768]{1,0:T(8,128)}, f32[768,8]{1,0:T(8,128)}, /*ind...) custom-call(bf16[8,96,4096]{2,1,0:T(8,128)(2,1)} %bitcast.11, bf16[8,256,768]{2,1,0:T(8,128)(2,1)} %bitcast.12, ...), custom_call_target="tpu_custom_call" | custom-call | tf_op jit(solution)/shard_map/tail/pallas_call | solution.py:1360
  329.6 7.5 %release.1 = (bf16[768,768]{1,0:T(8,128)(2,1)}, f32[768,768]{1,0:T(8,128)}, f32[768,8]{1,0:T(8,128)}, f32[96,2304]{1,0:T(8,128)}, f32[96,768]{1,0:T(8,128)}, /*i...) custom-call(bf16[768,768]{1,0:T(8,128)(2,1)} %get-tuple-element.64.r, ...), custom_call_target="tpu_custom_call" | custom-call | tf_op jit(solution)/shard_map/release/pallas_call | solution.py:1403
  337.2 1.4 copy.58
  338.6 1.4 copy.57
  340.0 1.5 copy.56
  341.5 1.7 copy.55
